TPU v7x, 32 devices: a whole 2x2x4 slice. The times are simulated.
32 devices in a mesh: dp: 8 (over y, x, core), tensor: 4 (over z).
Axes of the slice: x: 2, y: 2, z: 4, core: 2. Of those that a mesh axis runs over, the one named last changes fastest.
Arguments:
- tokens_in: bfloat16 [16384, 1024], P(('dp', 'tensor'))
- out_grad: bfloat16 [16384, 1024], P(('dp', 'tensor')), may hold values from -6 to 6
- lengths: int32 [8, 4], P('dp'), may hold values from 1 to 1024, 2048 in all within a row
- owners: int32 [12], replicated, may hold values from 0 to 7, as said below
- matrix_master: float32 [4, 16, 256, 1024], P('tensor', 'dp')
- matrix_m1: float32 [4, 16, 256, 1024], P('tensor', 'dp')
- matrix_m2: float32 [4, 16, 256, 1024], P('tensor', 'dp'), as said below
- shared_params: float32 [3, 6, 1024], replicated, as said below
- bias_params: float32 [3, 4, 1792], P(None, 'tensor'), as said below
Outputs:
- layer_out: float32 [16384, 1024], P(('dp', 'tensor'))
- input_grad: float32 [16384, 1024], P(('dp', 'tensor'))
- head_max: float32 [16], P('tensor')
- matrix_grad: float32 [4, 16, 256, 1024], P('tensor', 'dp')
- matrix_moment1: float32 [4, 16, 256, 1024], P('tensor', 'dp')
- matrix_moment2: float32 [4, 16, 256, 1024], P('tensor', 'dp')
- matrix_new: float32 [4, 16, 256, 1024], P('tensor', 'dp')
- shared_out: float32 [2, 6, 1024], replicated
- shared_second: float32 [6, 1024], replicated
- shared_new: float32 [6, 1024], replicated
- bias_out: float32 [2, 4, 1792], P(None, 'tensor')
- bias_second: float32 [4, 1792], P('tensor')
- bias_new: float32 [4, 1792], P('tensor')
Inputs may be any that keep to these rules, and one draw needn't show every extreme that they name: `owners`: each index of dp owns at most 2 units, and some index owns exactly 2. `matrix_m2`: entries are positive. `shared_params`: second moments (first index 2) are positive. `bias_params`: second moments (first index 2) are positive.
All inputs are finite; a program needn't handle non-finite values.
Results may differ from a plain program's by a relative error of at most 0.017.
Values may be sent and summed in bfloat16 or wider, within the bound.
A program may use at most 192 MiB of HBM per device.

v0:
```python
import math

import jax
import jax.numpy as jnp
from jax import lax
from jax.sharding import PartitionSpec as P

HD = 64
BLK = 512
STEP = 10


EPS_NORM = 1e-05
BETA_ONE = 0.9
BETA_TWO = 0.95
LEARN_RATE = 0.08
WEIGHT_DECAY = 0.1
EPS_ADAM = 1e-08
CLIP_TAU = 10.0
MASKED = -1e30


def plain_dot(left, right):
    return jnp.dot(left, right, preferred_element_type=jnp.float32)


def rows_by_rows(left, right):
    return lax.dot_general(
        left, right, (((1,), (1,)), ((), ())), preferred_element_type=jnp.float32
    )


def cols_by_cols(left, right):
    return lax.dot_general(
        left, right, (((0,), (0,)), ((), ())), preferred_element_type=jnp.float32
    )


def gelu_tanh(values_in):
    return jax.nn.gelu(values_in, approximate=True)


def norm_rows(values_in, gain, shift):
    centre = jnp.mean(values_in, axis=-1, keepdims=True)
    shifted = values_in - centre
    inverse = lax.rsqrt(jnp.mean(shifted * shifted, axis=-1, keepdims=True) + EPS_NORM)
    normed = shifted * inverse
    return (normed * gain + shift, normed, inverse)


def norm_back(grad_in, normed, inverse, gain):
    scaled = grad_in * gain
    return inverse * (
        scaled
        - jnp.mean(scaled, axis=-1, keepdims=True)
        - normed * jnp.mean(scaled * normed, axis=-1, keepdims=True)
    )


def slot_tables(owners, n_slots, slot_cap):
    n_units = owners.shape[0]
    unit_order = jnp.arange(n_units, dtype=jnp.int32)
    same_owner = owners[:, None] == owners[None, :]
    earlier = unit_order[None, :] < unit_order[:, None]
    rank_counts = jnp.sum((same_owner & earlier).astype(jnp.int32), axis=1)
    slot_of_unit = owners * slot_cap + rank_counts
    matches = jnp.arange(n_slots, dtype=jnp.int32)[:, None] == slot_of_unit[None, :]
    occupied = jnp.any(matches, axis=1)
    unit_of_slot = jnp.sum(matches.astype(jnp.int32) * unit_order[None, :], axis=1)
    return (slot_of_unit, unit_of_slot, occupied)


def block_scores(queries, keys_in, segments, q_index, k_index, score_scale):
    q_blk = lax.dynamic_slice_in_dim(queries, q_index * BLK, BLK, 0)
    k_blk = lax.dynamic_slice_in_dim(keys_in, k_index * BLK, BLK, 0)
    raw_scores = (
        jnp.einsum("qhd,khd->hqk", q_blk, k_blk, preferred_element_type=jnp.float32) * score_scale
    )
    q_places = q_index * BLK + jnp.arange(BLK, dtype=jnp.int32)
    k_places = k_index * BLK + jnp.arange(BLK, dtype=jnp.int32)
    q_segments = lax.dynamic_slice_in_dim(segments, q_index * BLK, BLK, 0)
    k_segments = lax.dynamic_slice_in_dim(segments, k_index * BLK, BLK, 0)
    allowed = (q_places[:, None] >= k_places[None, :]) & (
        q_segments[:, None] == k_segments[None, :]
    )
    return (raw_scores, allowed[None])


def attend_forward(queries, keys_in, values_in, segments):
    seq_len, heads_here, head_dim = queries.shape
    n_blocks = seq_len // BLK
    score_scale = 1.0 / math.sqrt(head_dim)

    def one_block(q_index):

        def sweep_max(k_index, loop_carry):
            run_max, run_sum, peak_max = loop_carry
            raw_scores, allowed = block_scores(
                queries, keys_in, segments, q_index, k_index, score_scale
            )
            masked = jnp.where(allowed, raw_scores, MASKED)
            new_max = jnp.maximum(run_max, jnp.max(masked, axis=-1))
            exp_terms = jnp.where(allowed, jnp.exp(masked - new_max[..., None]), 0.0)
            run_sum = run_sum * jnp.exp(run_max - new_max) + jnp.sum(exp_terms, axis=-1)
            return (new_max, run_sum, jnp.maximum(peak_max, jnp.max(masked, axis=(1, 2))))

        start_carry = (
            jnp.full((heads_here, BLK), MASKED, jnp.float32),
            jnp.zeros((heads_here, BLK), jnp.float32),
            jnp.full((heads_here,), MASKED, jnp.float32),
        )
        run_max, run_sum, peak_max = lax.fori_loop(0, q_index + 1, sweep_max, start_carry)
        log_norm = run_max + jnp.log(run_sum)

        def sweep_out(k_index, accumulated):
            raw_scores, allowed = block_scores(
                queries, keys_in, segments, q_index, k_index, score_scale
            )
            prob_low = jnp.where(allowed, jnp.exp(raw_scores - log_norm[..., None]), 0.0).astype(
                jnp.bfloat16
            )
            v_blk = lax.dynamic_slice_in_dim(values_in, k_index * BLK, BLK, 0)
            return accumulated + jnp.einsum(
                "hqk,khd->qhd", prob_low, v_blk, preferred_element_type=jnp.float32
            )

        block_out = lax.fori_loop(
            0, q_index + 1, sweep_out, jnp.zeros((BLK, heads_here, head_dim), jnp.float32)
        )
        return (block_out, log_norm, peak_max)

    block_outs, log_norms, peaks = lax.map(one_block, jnp.arange(n_blocks, dtype=jnp.int32))
    return (block_outs.reshape(seq_len, heads_here * head_dim), log_norms, jnp.max(peaks, axis=0))


def attend_backward(queries, keys_in, values_in, grads_out, log_norms, segments):
    seq_len, heads_here, head_dim = queries.shape
    n_blocks = seq_len // BLK
    score_scale = 1.0 / math.sqrt(head_dim)

    def one_block(q_index, loop_carry):
        key_grads, value_grads, query_grads = loop_carry
        q_blk = lax.dynamic_slice_in_dim(queries, q_index * BLK, BLK, 0)
        g_blk = lax.dynamic_slice_in_dim(grads_out, q_index * BLK, BLK, 0)
        log_norm = log_norms[q_index]

        def sweep_delta(k_index, row_delta):
            raw_scores, allowed = block_scores(
                queries, keys_in, segments, q_index, k_index, score_scale
            )
            prob_f32 = jnp.where(allowed, jnp.exp(raw_scores - log_norm[..., None]), 0.0)
            v_blk = lax.dynamic_slice_in_dim(values_in, k_index * BLK, BLK, 0)
            grad_dots = jnp.einsum("qhd,khd->hqk", g_blk, v_blk, preferred_element_type=jnp.float32)
            return row_delta + jnp.sum(prob_f32 * grad_dots, axis=-1)

        row_delta = lax.fori_loop(
            0, q_index + 1, sweep_delta, jnp.zeros((heads_here, BLK), jnp.float32)
        )

        def sweep_grads(k_index, inner_carry):
            query_acc, key_all, value_all = inner_carry
            raw_scores, allowed = block_scores(
                queries, keys_in, segments, q_index, k_index, score_scale
            )
            prob_f32 = jnp.where(allowed, jnp.exp(raw_scores - log_norm[..., None]), 0.0)
            v_blk = lax.dynamic_slice_in_dim(values_in, k_index * BLK, BLK, 0)
            k_blk = lax.dynamic_slice_in_dim(keys_in, k_index * BLK, BLK, 0)
            grad_dots = jnp.einsum("qhd,khd->hqk", g_blk, v_blk, preferred_element_type=jnp.float32)
            score_grads = (prob_f32 * (grad_dots - row_delta[..., None])).astype(jnp.bfloat16)
            query_acc = query_acc + jnp.einsum(
                "hqk,khd->qhd", score_grads, k_blk, preferred_element_type=jnp.float32
            )
            key_piece = jnp.einsum(
                "hqk,qhd->khd", score_grads, q_blk, preferred_element_type=jnp.float32
            )
            value_piece = jnp.einsum(
                "hqk,qhd->khd",
                prob_f32.astype(jnp.bfloat16),
                g_blk,
                preferred_element_type=jnp.float32,
            )
            key_old = lax.dynamic_slice_in_dim(key_all, k_index * BLK, BLK, 0)
            value_old = lax.dynamic_slice_in_dim(value_all, k_index * BLK, BLK, 0)
            key_all = lax.dynamic_update_slice_in_dim(
                key_all, key_old + key_piece, k_index * BLK, 0
            )
            value_all = lax.dynamic_update_slice_in_dim(
                value_all, value_old + value_piece, k_index * BLK, 0
            )
            return (query_acc, key_all, value_all)

        start_acc = jnp.zeros((BLK, heads_here, head_dim), jnp.float32)
        query_acc, key_grads, value_grads = lax.fori_loop(
            0, q_index + 1, sweep_grads, (start_acc, key_grads, value_grads)
        )
        query_grads = lax.dynamic_update_slice_in_dim(query_grads, query_acc, q_index * BLK, 0)
        return (key_grads, value_grads, query_grads)

    zeros_full = jnp.zeros((seq_len, heads_here, head_dim), jnp.float32)
    key_grads, value_grads, query_grads = lax.fori_loop(
        0, n_blocks, one_block, (zeros_full, zeros_full, zeros_full)
    )
    return (query_grads * score_scale, key_grads * score_scale, value_grads)


def adam_step(param, grad, first, second, steps_done, decay):
    first_new = BETA_ONE * first + (1.0 - BETA_ONE) * grad
    second_new = BETA_TWO * second + (1.0 - BETA_TWO) * grad * grad
    fix_one = 1.0 - BETA_ONE**steps_done
    fix_two = 1.0 - BETA_TWO**steps_done
    direction = first_new / fix_one / (jnp.sqrt(second_new / fix_two) + EPS_ADAM)
    return (first_new, second_new, param - LEARN_RATE * (direction + decay * param))


def per_device(
    tokens_in,
    out_grad,
    lengths,
    owners,
    matrix_master,
    matrix_m1,
    matrix_m2,
    shared_params,
    bias_params,
):
    n_tensor = lax.axis_size("tensor")
    n_data = lax.axis_size("dp")
    tensor_index = lax.axis_index("tensor")
    data_index = lax.axis_index("dp")
    local_rows, model_width = tokens_in.shape
    seq_len = local_rows * n_tensor
    slot_cap = matrix_master.shape[1]
    unit_rows = matrix_master.shape[2]
    n_units = owners.shape[0]
    n_slots = n_data * slot_cap
    stack_rows = n_units * unit_rows
    head_rows = model_width // n_tensor
    heads_here = head_rows // HD
    ff_rows = (stack_rows - 4 * head_rows) // 2
    slot_of_unit, unit_of_slot, occupied = slot_tables(owners, n_slots, slot_cap)
    master_low = matrix_master[0].astype(jnp.bfloat16)
    every_slot = lax.all_gather(master_low, "dp", axis=0, tiled=True)
    stacked = jnp.take(every_slot, slot_of_unit, axis=0).reshape(stack_rows, model_width)
    w_qkv = stacked[: 3 * head_rows]
    w_out = stacked[3 * head_rows : 4 * head_rows]
    w_fc = stacked[4 * head_rows : 4 * head_rows + ff_rows]
    w_proj = stacked[4 * head_rows + ff_rows :]
    shared = shared_params[0]
    own_bias = bias_params[0, 0]
    b_qkv = own_bias[: 3 * head_rows]
    b_fc = own_bias[3 * head_rows :]
    bounds = jnp.cumsum(lengths[0])
    places = jnp.arange(seq_len, dtype=jnp.int32)
    segments = jnp.sum((places[:, None] >= bounds[None, :]).astype(jnp.int32), axis=1)
    inputs_f32 = tokens_in.astype(jnp.float32)
    normed_one, hat_one, inverse_one = norm_rows(inputs_f32, shared[0], shared[1])
    normed_all = lax.all_gather(normed_one.astype(jnp.bfloat16), "tensor", axis=0, tiled=True)
    qkv_low = (rows_by_rows(normed_all, w_qkv) + b_qkv).astype(jnp.bfloat16)
    queries = qkv_low[:, :head_rows].reshape(seq_len, heads_here, HD)
    keys_in = qkv_low[:, head_rows : 2 * head_rows].reshape(seq_len, heads_here, HD)
    values_in = qkv_low[:, 2 * head_rows :].reshape(seq_len, heads_here, HD)
    attended_f32, log_norms, local_peak = attend_forward(queries, keys_in, values_in, segments)
    attended = attended_f32.astype(jnp.bfloat16)
    attn_part = lax.psum_scatter(
        plain_dot(attended, w_out), "tensor", scatter_dimension=0, tiled=True
    )
    hidden = inputs_f32 + (attn_part + shared[2])
    normed_two, hat_two, inverse_two = norm_rows(hidden, shared[3], shared[4])
    second_all = lax.all_gather(normed_two.astype(jnp.bfloat16), "tensor", axis=0, tiled=True)
    pre_act = rows_by_rows(second_all, w_fc) + b_fc
    activ, gelu_back = jax.vjp(gelu_tanh, pre_act)
    activ_low = activ.astype(jnp.bfloat16)
    mlp_part = lax.psum_scatter(
        plain_dot(activ_low, w_proj).astype(jnp.bfloat16), "tensor", scatter_dimension=0, tiled=True
    ).astype(jnp.float32)
    layer_out = hidden + (mlp_part + shared[5])
    grad_y = out_grad.astype(jnp.float32)
    grad_y_all = lax.all_gather(out_grad, "tensor", axis=0, tiled=True)
    grad_proj_w = cols_by_cols(activ_low, grad_y_all)
    grad_activ = rows_by_rows(grad_y_all, w_proj)
    grad_pre_low = gelu_back(grad_activ)[0].astype(jnp.bfloat16)
    grad_fc_b = jnp.sum(grad_pre_low, axis=0, dtype=jnp.float32)
    grad_fc_w = cols_by_cols(grad_pre_low, second_all)
    grad_second = lax.psum_scatter(
        plain_dot(grad_pre_low, w_fc), "tensor", scatter_dimension=0, tiled=True
    )
    grad_hidden = grad_y + norm_back(grad_second, hat_two, inverse_two, shared[3])
    grad_hidden_low = grad_hidden.astype(jnp.bfloat16)
    grad_hidden_all = lax.all_gather(grad_hidden_low, "tensor", axis=0, tiled=True)
    grad_out_w = cols_by_cols(attended, grad_hidden_all)
    grad_attended = rows_by_rows(grad_hidden_all, w_out).astype(jnp.bfloat16)
    grad_heads = grad_attended.reshape(seq_len, heads_here, HD)
    grad_query, grad_key, grad_value = attend_backward(
        queries, keys_in, values_in, grad_heads, log_norms, segments
    )
    grad_qkv_low = jnp.concatenate(
        [
            grad_query.reshape(seq_len, head_rows),
            grad_key.reshape(seq_len, head_rows),
            grad_value.reshape(seq_len, head_rows),
        ],
        axis=1,
    ).astype(jnp.bfloat16)
    grad_qkv_b = jnp.sum(grad_qkv_low, axis=0, dtype=jnp.float32)
    grad_qkv_w = cols_by_cols(grad_qkv_low, normed_all)
    grad_first = lax.psum_scatter(
        plain_dot(grad_qkv_low, w_qkv).astype(jnp.bfloat16),
        "tensor",
        scatter_dimension=0,
        tiled=True,
    ).astype(jnp.float32)
    input_grad = grad_hidden + norm_back(grad_first, hat_one, inverse_one, shared[0])
    head_peak = lax.pmax(local_peak, "dp")
    shared_part = jnp.stack(
        [
            jnp.sum(grad_first * hat_one, axis=0),
            jnp.sum(grad_first, axis=0),
            jnp.sum(grad_hidden_low, axis=0, dtype=jnp.float32),
            jnp.sum(grad_second * hat_two, axis=0),
            jnp.sum(grad_second, axis=0),
            jnp.sum(grad_y, axis=0),
        ]
    )
    bias_part = jnp.concatenate([grad_qkv_b, grad_fc_b])
    own_row = (jnp.arange(n_tensor, dtype=jnp.int32) == tensor_index)[:, None]
    bias_rows = jnp.where(own_row, bias_part[None, :], 0.0)
    shared_grad, bias_total = lax.psum((shared_part, bias_rows), ("dp", "tensor"))
    bias_grad = lax.dynamic_index_in_dim(bias_total, tensor_index, 0, keepdims=False)
    grad_stack = jnp.concatenate([grad_qkv_w, grad_out_w, grad_fc_w, grad_proj_w], axis=0)
    my_units = lax.dynamic_slice_in_dim(unit_of_slot, data_index * slot_cap, slot_cap, 0)
    my_occupied = lax.dynamic_slice_in_dim(occupied, data_index * slot_cap, slot_cap, 0)[
        :, None, None
    ]
    summed = lax.psum(grad_stack.astype(jnp.bfloat16), "dp").astype(jnp.float32)
    picked_units = jnp.take(summed.reshape(n_units, unit_rows, model_width), my_units, axis=0)
    my_grads = jnp.where(my_occupied, picked_units, 0.0)
    steps_done = float(STEP)
    first_new, second_new, master_new = adam_step(
        matrix_master[0], my_grads, matrix_m1[0], matrix_m2[0], steps_done, WEIGHT_DECAY
    )
    root_gamma = jnp.sqrt(CLIP_TAU / jnp.maximum(head_peak, CLIP_TAU))
    row_index = my_units[:, None] * unit_rows + jnp.arange(unit_rows, dtype=jnp.int32)[None, :]
    local_head = jnp.where(row_index < head_rows, row_index // HD, (row_index - head_rows) // HD)
    head_match = local_head[..., None] == jnp.arange(heads_here, dtype=jnp.int32)[None, None, :]
    picked_root = jnp.sum(jnp.where(head_match, root_gamma, 0.0), axis=-1)
    factor = jnp.where(row_index < 2 * head_rows, picked_root, 1.0)
    master_new = jnp.where(my_occupied, master_new * factor[..., None], 0.0)
    first_new = jnp.where(my_occupied, first_new, 0.0)
    second_new = jnp.where(my_occupied, second_new, 0.0)
    shared_first, shared_second, shared_new = adam_step(
        shared, shared_grad, shared_params[1], shared_params[2], steps_done, 0.0
    )
    bias_first, bias_second, bias_new = adam_step(
        own_bias, bias_grad, bias_params[1, 0], bias_params[2, 0], steps_done, 0.0
    )
    shared_out = jnp.stack([shared_grad, shared_first])
    bias_out = jnp.stack([bias_grad, bias_first])[:, None, :]
    return (
        layer_out,
        input_grad,
        head_peak,
        my_grads[None],
        first_new[None],
        second_new[None],
        master_new[None],
        shared_out,
        shared_second,
        shared_new,
        bias_out,
        bias_second[None],
        bias_new[None],
    )


def solution(mesh):
    in_specs = (
        P(("dp", "tensor"), None),
        P(("dp", "tensor"), None),
        P("dp", None),
        P(),
        P("tensor", "dp", None, None),
        P("tensor", "dp", None, None),
        P("tensor", "dp", None, None),
        P(),
        P(None, "tensor", None),
    )
    out_specs = (
        P(("dp", "tensor"), None),
        P(("dp", "tensor"), None),
        P("tensor"),
        P("tensor", "dp", None, None),
        P("tensor", "dp", None, None),
        P("tensor", "dp", None, None),
        P("tensor", "dp", None, None),
        P(),
        P(),
        P(),
        P(None, "tensor", None),
        P("tensor", None),
        P("tensor", None),
    )
    return jax.shard_map(
        per_device, mesh=mesh, in_specs=in_specs, out_specs=out_specs, check_vma=False
    )
```

profile of v0, /device:TPU:9, one launch (start us, length us, event | category | flops | bytes accessed | tf_op | source)
XLA Modules:
  0.0 1282.6 jit_solution(12523372418249825493)
XLA Ops:
  15.7 50.8 %all-gather.15.cloned.1.call-done = bf16[1,16,256,1024]{3,2,0,1:T(8,128)(2,1)} async-done(((bf16[1,2,256,1024]{3,2,0,1:T(8,128)(2,1)}), bf16[1,16,256,1024]{3,2,0,1:T(8,128)(2,1)}) %all-gather.15.cloned.1.call-update) | async-done | bytes 8388624 | tf_op jit(solution)/shard_map/all_gather | solution.py:242
  66.5 7.6 gather_fusion
  80.9 65.6 %all-gather.7.cloned.1.call-done = bf16[2048,1024]{1,0:T(8,128)(2,1)} async-done(((bf16[512,1024]{1,0:T(8,128)(2,1)}), bf16[2048,1024]{1,0:T(8,128)(2,1)}) %all-gather.7.cloned.1.call-update) | async-done | bytes 4194320 | tf_op jit(solution)/shard_map/all_gather | solution.py:257
  153.6 72.7 %while.118 = (s32[]{:T(128)}, bf16[4,512,4,64]{1,3,2,0:T(8,128)(2,1)}, f32[4,4,512]{2,1,0:T(4,128)S(1)}, f32[4,4]{1,0:T(4,128)}, s32[4]{0:T(128)S(1)}, /*index=5...) while((s32[]{:T(128)}, ...), condition=%wide.region_13.14_spmd, body=%wide.region_5.13_spmd.sunk | while | flops 417996800 | bytes 14358569 | solution.py:132
  180.8 8.7 while.122
  190.8 8.2 while.123
  201.7 11.6 while.122
  214.7 10.9 while.123
  235.9 145.2 %reduce-scatter.5.cloned.1.call-done = f32[512,1024]{1,0:T(8,128)} async-done(((f32[2048,1024]{1,0:T(8,128)}), f32[512,1024]{1,0:T(8,128)}) %reduce-scatter.5.cloned.1.call-update) | async-done | bytes 2097168 | tf_op jit(solution)/shard_map/reduce_scatter | solution.py:264
  391.0 73.4 %all-gather.9.cloned.1.call-done = bf16[2048,1024]{1,0:T(8,128)(2,1)} async-done(((bf16[512,1024]{1,0:T(8,128)(2,1)}), bf16[2048,1024]{1,0:T(8,128)(2,1)}) %all-gather.9.cloned.1.call-update) | async-done | bytes 4194320 | tf_op jit(solution)/shard_map/all_gather | solution.py:269
  464.4 10.7 fusion.92
  475.1 70.0 %all-gather.11.cloned.1.call-done = bf16[2048,1024]{1,0:T(8,128)(2,1)} async-done(((bf16[512,1024]{1,0:T(8,128)(2,1)}), bf16[2048,1024]{1,0:T(8,128)(2,1)}) %all-gather.11.cloned.1.call-update) | async-done | bytes 4194320 | tf_op jit(solution)/shard_map/all_gather | solution.py:278
  545.1 13.8 %convert_reduce_fusion = (f32[1024]{0:T(1024)}, bf16[2048,1024]{1,0:T(8,128)(2,1)S(1)}) fusion(f32[2048,1024]{1,0:T(8,128)} %fusion.92, f32[1024]{0:T(1024)S(1)} %bitcast.295, bf16[1024,1024]{1,0:T(8,128)(2,1)} %bitcast.266, bf16[2048,1024]{1,0:T(8,128)(2,1)} %all-gather.11.cloned.1.call-done), kind=kOutput, calls=%fused_computation.85 | convolution fusion | flops 4343200768 | bytes 18882560 | tf_op jit(solution)/shard_map/dot_general | solution.py:28
  568.0 11.8 convolution_convert_fusion.1
  579.8 133.1 %reduce-scatter.9.cloned.1.call-done = f32[512,1024]{1,0:T(8,128)} async-done(((f32[2048,1024]{1,0:T(8,128)}), f32[512,1024]{1,0:T(8,128)}) %reduce-scatter.9.cloned.1.call-update) | async-done | bytes 2097168 | tf_op jit(solution)/shard_map/reduce_scatter | solution.py:284
  716.0 77.1 %reduce-scatter.7.cloned.1.call-done = bf16[512,1024]{1,0:T(8,128)(2,1)} async-done(((bf16[2048,1024]{1,0:T(8,128)(2,1)}), bf16[512,1024]{1,0:T(8,128)(2,1)}) %reduce-scatter.7.cloned.1.call-update) | async-done | bytes 1048592 | tf_op jit(solution)/shard_map/reduce_scatter | solution.py:273
  798.5 9.5 convolution_convert_fusion.4
  808.0 11.2 convolution_convert_fusion.3
  819.2 57.8 %all-gather.13.cloned.1.call-done = bf16[2048,1024]{1,0:T(8,128)(2,1)} async-done(((bf16[512,1024]{1,0:T(8,128)(2,1)}), bf16[2048,1024]{1,0:T(8,128)(2,1)}) %all-gather.13.cloned.1.call-update) | async-done | bytes 4194320 | tf_op jit(solution)/shard_map/all_gather | solution.py:289
  886.4 141.9 %while.121 = (s32[]{:T(128)}, f32[2048,4,64]{0,2,1:T(8,128)}, f32[2048,4,64]{0,2,1:T(8,128)}, f32[2048,4,64]{0,2,1:T(8,128)}, f32[4,4,512]{2,1,0:T(4,128)S(1)}, ...) while((s32[]{:T(128)}, f32[2048,4,64]{0,2,1:T(8,128)}, ...), condition=%wide.region_27.28_spmd, body=%wide.region_21.27_spmd.sunk | while | flops 957220864 | bytes 37352436 | solution.py:200
  891.5 9.7 while.125
  903.2 7.3 while.124
  910.6 19.4 %while.125 = (s32[]{:T(128)}, f32[512,4,64]{0,2,1:T(8,128)S(1)}, f32[2048,4,64]{0,2,1:T(8,128)}, f32[2048,4,64]{0,2,1:T(8,128)}, s32[]{:T(128)}, /*index=5*/bf16...) while((s32[]{:T(128)}, f32[512,4,64]{0,2,1:T(8,128)S(1)}, ...), condition=%wide.region_26.26_spmd, body=%wide.region_25.25_spmd.sunk | while | flops 682755072 | bytes 24682740 | solution.py:193
  931.9 11.0 while.124
  943.0 29.0 %while.125 = (s32[]{:T(128)}, f32[512,4,64]{0,2,1:T(8,128)S(1)}, f32[2048,4,64]{0,2,1:T(8,128)}, f32[2048,4,64]{0,2,1:T(8,128)}, s32[]{:T(128)}, /*index=5*/bf16...) while((s32[]{:T(128)}, f32[512,4,64]{0,2,1:T(8,128)S(1)}, ...), condition=%wide.region_26.26_spmd, body=%wide.region_25.25_spmd.sunk | while | flops 682755072 | bytes 24682740 | solution.py:193
  974.0 14.7 %while.124 = (s32[]{:T(128)}, f32[4,512]{1,0:T(4,128)S(1)}, s32[]{:T(128)}, s32[]{:T(128)}, s32[512]{0:T(512)S(1)}, /*index=5*/s32[2048]{0:T(1024)S(1)}, bf16[20...) while((s32[]{:T(128)}, f32[4,512]{1,0:T(4,128)S(1)}, ...), condition=%wide.region_24.24_spmd, body=%wide.region_22.23_spmd.sunk | while | flops 274465792 | bytes 10019023 | solution.py:156
  988.7 38.7 %while.125 = (s32[]{:T(128)}, f32[512,4,64]{0,2,1:T(8,128)S(1)}, f32[2048,4,64]{0,2,1:T(8,128)}, f32[2048,4,64]{0,2,1:T(8,128)}, s32[]{:T(128)}, /*index=5*/bf16...) while((s32[]{:T(128)}, f32[512,4,64]{0,2,1:T(8,128)S(1)}, ...), condition=%wide.region_26.26_spmd, body=%wide.region_25.25_spmd.sunk | while | flops 682755072 | bytes 24682740 | solution.py:193
  1051.9 12.2 pmax.7
  1064.9 83.2 %all-reduce.3.cloned.1.call-done = bf16[12,256,1024]{2,1,0:T(8,128)(2,1)} async-done(((bf16[12,256,1024]{2,1,0:T(8,128)(2,1)}), bf16[12,256,1024]{2,1,0:T(8,128)(2,1)}) %all-reduce.3.cloned.1.call-update) | async-done | bytes 6291472 | tf_op jit(solution)/shard_map/psum | solution.py:334
  1148.1 8.9 reshape.589
  1175.1 52.2 %reduce-scatter.11.cloned.1.call-done = bf16[512,1024]{1,0:T(8,128)(2,1)} async-done(((bf16[2048,1024]{1,0:T(8,128)(2,1)}), bf16[512,1024]{1,0:T(8,128)(2,1)}) %reduce-scatter.11.cloned.1.call-update) | async-done | bytes 1048592 | tf_op jit(solution)/shard_map/reduce_scatter | solution.py:306
  1229.7 39.7 %all-reduce = (f32[6,1024]{1,0:T(8,128)S(1)}, f32[4,1792]{1,0:T(4,128)S(1)}) all-reduce(f32[6,1024]{1,0:T(8,128)S(1)} %stack.41, f32[4,1792]{1,0:T(4,128)S(1)} %broadcast_select_fusion.3), channel_id=1, replica_groups=mesh['dp'=8,'tensor'=4] {'dp','tensor'}, use_global_device_ids=true, to_apply=%region_43.44 | all-reduce | flops 13312 | bytes 106496 | tf_op jit(solution)/shard_map/psum | solution.py:327
  (521 shorter events, 346.6 us)
Async XLA Ops:
  7.2 59.3 %all-gather.15.cloned.1.call-start = ((), (), s32[]{:S(2)}) async-start(), calls=%async_computation.13 | async-start | bytes 9437184 | tf_op jit(solution)/shard_map/all_gather | solution.py:242
  10.1 136.4 %all-gather.7.cloned.1.call-start = ((), (), s32[]{:S(2)}) async-start(), calls=%async_computation.4 | async-start | bytes 5242880 | tf_op jit(solution)/shard_map/all_gather | solution.py:257
  14.4 366.6 %reduce-scatter.5.cloned.1.call-start = ((), (), s32[]{:S(2)}) async-start(), calls=%async_computation.5 | async-start | bytes 10485760 | tf_op jit(solution)/shard_map/reduce_scatter | solution.py:264
  14.9 59.2 %copy-start.35 = (s32[12]{0:T(128)}, s32[12]{0:T(128)S(1)}, u32[]{:S(2)}) copy-start(s32[12]{0:T(128)S(1)} %get-tuple-element.1075) | copy-start | bytes 148
  80.9 65.6 %copy-start.18 = (bf16[3,256,1024]{2,1,0:T(8,128)(2,1)}, bf16[3,256,1024]{2,1,0:T(8,128)(2,1)S(1)}, u32[]{:S(2)}) copy-start(bf16[3,256,1024]{2,1,0:T(8,128)(2,1)S(1)} %slice.122) | copy-start | bytes 4718596
  226.3 9.2 copy-start.4
  235.6 228.8 %all-gather.9.cloned.1.call-start = ((), (), s32[]{:S(2)}) async-start(), calls=%async_computation.6 | async-start | bytes 5242880 | tf_op jit(solution)/shard_map/all_gather | solution.py:269
  385.0 160.1 %all-gather.11.cloned.1.call-start = ((), (), s32[]{:S(2)}) async-start(), calls=%async_computation.8 | async-start | bytes 5242880 | tf_op jit(solution)/shard_map/all_gather | solution.py:278
  385.6 327.3 %reduce-scatter.9.cloned.1.call-start = ((), (), s32[]{:S(2)}) async-start(), calls=%async_computation.9 | async-start | bytes 10485760 | tf_op jit(solution)/shard_map/reduce_scatter | solution.py:284
  545.1 15.7 %copy-start.17 = (bf16[4,256,1024]{2,1,0:T(8,128)(2,1)S(1)}, bf16[4,256,1024]{2,1,0:T(8,128)(2,1)}, u32[]{:S(2)}) copy-start(bf16[4,256,1024]{2,1,0:T(8,128)(2,1)} %get-tuple-element.1088) | copy-start | bytes 6291460
  567.5 225.5 %reduce-scatter.7.cloned.1.call-start = ((), (), s32[]{:S(2)}) async-start(), calls=%async_computation.7 | async-start | bytes 5242880 | tf_op jit(solution)/shard_map/reduce_scatter | solution.py:273
  579.8 213.3 %copy-start.29 = (f32[1,1,1024]{2,1,0:T(1,128)S(1)}, f32[1,1,1024]{2,1,0:T(1,128)}, u32[]{:S(2)}) copy-start(f32[1,1,1024]{2,1,0:T(1,128)} %get-tuple-element.1098) | copy-start | bytes 12292
  579.8 297.3 %all-gather.13.cloned.1.call-start = ((), (), s32[]{:S(2)}) async-start(), calls=%async_computation.10 | async-start | bytes 5242880 | tf_op jit(solution)/shard_map/all_gather | solution.py:289
  798.2 349.9 %all-reduce.3.cloned.1.call-start = ((), (), s32[]{:S(2)}) async-start(), calls=%async_computation.12 | async-start | bytes 12582912 | tf_op jit(solution)/shard_map/psum | solution.py:334
  798.5 9.6 copy-start.39
  1042.7 184.6 %reduce-scatter.11.cloned.1.call-start = ((), (), s32[]{:S(2)}) async-start(), calls=%async_computation.11 | async-start | bytes 5242880 | tf_op jit(solution)/shard_map/reduce_scatter | solution.py:306
  1050.6 14.1 %copy-start.32 = (f32[1024]{0:T(1024)S(1)}, f32[1024]{0:T(1024)}, u32[]{:S(2)}) copy-start(f32[1024]{0:T(1024)} %get-tuple-element.1104) | copy-start | bytes 12292
  1064.0 93.0 %copy-start.41 = (f32[4]{0:T(128)}, f32[4]{0:T(128)S(1)}, u32[]{:S(2)}) copy-start(f32[4]{0:T(128)S(1)} %pmax.7) | copy-start | bytes 52
  1157.0 7.0 copy-start.7
  1164.1 8.1 copy-start.8
  1164.1 8.1 copy-start.9
  1172.1 55.2 %copy-start.2 = (bf16[512,1024]{1,0:T(8,128)(2,1)S(1)}, bf16[512,1024]{1,0:T(8,128)(2,1)}, u32[]{:S(2)}) copy-start(bf16[512,1024]{1,0:T(8,128)(2,1)} %param.21) | copy-start | bytes 3145732
  1172.1 55.2 %copy-start.21 = (f32[1,1,1024]{2,1,0:T(1,128)S(1)}, f32[1,1,1024]{2,1,0:T(1,128)}, u32[]{:S(2)}) copy-start(f32[1,1,1024]{2,1,0:T(1,128)} %copy-done.20) | copy-start | bytes 12292
  1172.1 55.2 %copy-start.23 = (f32[512]{0:T(512)S(1)}, f32[512]{0:T(512)}, u32[]{:S(2)}) copy-start(f32[512]{0:T(512)} %copy-done.22) | copy-start | bytes 6148
  1172.1 55.2 %copy-start.26 = (f32[512]{0:T(512)S(1)}, f32[512]{0:T(512)}, u32[]{:S(2)}) copy-start(f32[512]{0:T(512)} %copy-done.25) | copy-start | bytes 6148
  1172.1 57.4 %copy-start.27 = (f32[1024]{0:T(1024)S(1)}, f32[1024]{0:T(1024)}, u32[]{:S(2)}) copy-start(f32[1024]{0:T(1024)} %get-tuple-element.1065) | copy-start | bytes 12292
  1172.2 57.4 %copy-start.28 = (f32[1024]{0:T(1024)S(1)}, f32[1024]{0:T(1024)}, u32[]{:S(2)}) copy-start(f32[1024]{0:T(1024)} %get-tuple-element.1096) | copy-start | bytes 12292
  1172.2 57.4 %copy-start.30 = (f32[1024]{0:T(1024)S(1)}, f32[1024]{0:T(1024)}, u32[]{:S(2)}) copy-start(f32[1024]{0:T(1024)} %get-tuple-element.919) | copy-start | bytes 12292
  1172.2 57.4 %copy-start.31 = (f32[1024]{0:T(1024)S(1)}, f32[1024]{0:T(1024)}, u32[]{:S(2)}) copy-start(f32[1024]{0:T(1024)} %get-tuple-element.924) | copy-start | bytes 12292
  1172.2 97.2 %copy-start.24 = (f32[3,1,1792]{2,1,0:T(1,128)S(1)}, f32[3,1,1792]{2,1,0:T(1,128)}, u32[]{:S(2)}) copy-start(f32[3,1,1792]{2,1,0:T(1,128)} %param.29) | copy-start | bytes 64516
  1172.2 98.5 %copy-start.19 = (f32[3,6,1024]{2,1,0:T(8,128)S(1)}, f32[3,6,1024]{2,1,0:T(8,128)}, u32[]{:S(2)}) copy-start(f32[3,6,1024]{2,1,0:T(8,128)} %param.28) | copy-start | bytes 221188
  1175.1 97.0 %copy-start.5 = (f32[512,1024]{1,0:T(8,128)S(1)}, f32[512,1024]{1,0:T(8,128)}, u32[]{:S(2)}) copy-start(f32[512,1024]{1,0:T(8,128)} %get-tuple-element.1067) | copy-start | bytes 6291460
  (21 other events, 46.2 us)
Sparse Core Ops, SparseCore 0:
  10.5 55.9 all-gather.14
  68.6 77.8 all-gather.6
  235.7 145.2 reduce-scatter.4
  385.1 79.2 all-gather.8
  465.8 79.2 all-gather.10
  567.7 145.2 reduce-scatter.8
  715.2 77.7 reduce-scatter.6
  798.4 78.6 all-gather.12
  1042.8 105.2 all-reduce.2
  1150.3 77.0 reduce-scatter.10
where the time goes:
time: 1300 us; the launch traced here: 1280 us
  waiting for transfers between devices  809 us (62%)
  matrix products  249 us (19%)
  other arithmetic  80.9 us (6%)
  local copies, waits for them, and re-layouts  68 us (5%)
  blocking collectives  51.9 us (4%)
  between operations  15.1 us (1%)
    reduce_scatter x1, waiting for transfers between devices, per_device(): lax.psum_scatter(plain_dot(attended, w_out), 'tensor', scatter_dimension=...  145 us
    reduce_scatter x1, waiting for transfers between devices, per_device(): lax.psum_scatter(plain_dot(grad_pre_low, w_fc), 'tensor', scatter_dimensi...  133 us
    psum x1, waiting for transfers between devices, per_device(): summed = lax.psum(grad_stack.astype(jnp.bfloat16), 'dp').astype(jnp.float32)  83.2 us
    reduce_scatter x1, waiting for transfers between devices, per_device(): lax.psum_scatter(plain_dot(activ_low, w_proj).astype(jnp.bfloat16), 'tens...  77.1 us
    all_gather x1, waiting for transfers between devices, per_device(): lax.all_gather(normed_two.astype(jnp.bfloat16), 'tensor', axis=0, tiled=T...  73.4 us
    all_gather x1, waiting for transfers between devices, per_device(): grad_y_all = lax.all_gather(out_grad, 'tensor', axis=0, tiled=True)  70 us
    all_gather x1, waiting for transfers between devices, per_device(): lax.all_gather(normed_one.astype(jnp.bfloat16), 'tensor', axis=0, tiled=T...  65.6 us
    all_gather x1, waiting for transfers between devices, per_device(): lax.all_gather(grad_hidden_low, 'tensor', axis=0, tiled=True)  57.8 us
  transfers between devices with their start and end apart: 10, of which 10 were waited for; matrix products, arithmetic and copies ran while one was open for 8% of the time, Pallas kernels for 0%

commit v1 on v0

v1 whole, which is shorter than its diff:
```python
import functools
import math

import jax
import jax.numpy as jnp
from jax import lax
from jax.experimental import pallas as pl
from jax.experimental.pallas import tpu as pltpu
from jax.sharding import PartitionSpec as P

HD = 64
DOC_MOST = 1024
STEP = 10
PAIR = 2 * HD

EPS_NORM = 1e-05
BETA_ONE = 0.9
BETA_TWO = 0.95
LEARN_RATE = 0.08
WEIGHT_DECAY = 0.1
EPS_ADAM = 1e-08
CLIP_TAU = 10.0
MASKED = -1e30
BF = jnp.bfloat16
F32 = jnp.float32


def plain_dot(left, right):
    return jnp.dot(left, right, preferred_element_type=F32)


def rows_by_rows(left, right):
    return lax.dot_general(left, right, (((1,), (1,)), ((), ())), preferred_element_type=F32)


def cols_by_cols(left, right):
    return lax.dot_general(left, right, (((0,), (0,)), ((), ())), preferred_element_type=F32)


def gelu_tanh(values_in):
    return jax.nn.gelu(values_in, approximate=True)


def norm_rows(values_in, gain, shift):
    centre = jnp.mean(values_in, axis=-1, keepdims=True)
    shifted = values_in - centre
    inverse = lax.rsqrt(jnp.mean(shifted * shifted, axis=-1, keepdims=True) + EPS_NORM)
    normed = shifted * inverse
    return (normed * gain + shift, normed, inverse)


def norm_back(grad_in, normed, inverse, gain):
    scaled = grad_in * gain
    return inverse * (
        scaled
        - jnp.mean(scaled, axis=-1, keepdims=True)
        - normed * jnp.mean(scaled * normed, axis=-1, keepdims=True)
    )


def slot_tables(owners, n_slots, slot_cap):
    n_units = owners.shape[0]
    unit_order = jnp.arange(n_units, dtype=jnp.int32)
    same_owner = owners[:, None] == owners[None, :]
    earlier = unit_order[None, :] < unit_order[:, None]
    rank_counts = jnp.sum((same_owner & earlier).astype(jnp.int32), axis=1)
    slot_of_unit = owners * slot_cap + rank_counts
    matches = jnp.arange(n_slots, dtype=jnp.int32)[:, None] == slot_of_unit[None, :]
    occupied = jnp.any(matches, axis=1)
    unit_of_slot = jnp.sum(matches.astype(jnp.int32) * unit_order[None, :], axis=1)
    return (slot_of_unit, unit_of_slot, occupied)


def head_lanes(head):
    lane = lax.broadcasted_iota(jnp.int32, (1, PAIR), 1)
    return (lane < HD) if head == 0 else (lane >= HD)


def q_tiles(n_query, n_keys):
    size = min(256, n_query)
    reach = n_keys - n_query
    return size, reach + size


def fill_bias(bias_ref, first_ref):
    n_keys, n_query = bias_ref.shape
    reach = n_keys - n_query
    key = lax.broadcasted_iota(jnp.int32, (n_keys, n_query), 0)
    query = lax.broadcasted_iota(jnp.int32, (n_keys, n_query), 1) + reach
    seen = (key <= query) & (key >= first_ref[...])
    bias_ref[...] = jnp.where(seen, 0.0, MASKED)


def attend_kernel(first_ref, q_ref, k_ref, v_ref, o_ref, lse_ref, peak_ref, bias_ref):
    @pl.when(pl.program_id(0) == 0)
    def _():
        fill_bias(bias_ref, first_ref)

    n_keys, n_query = bias_ref.shape
    size, span = q_tiles(n_query, n_keys)
    for j in range(n_query // size):
        rows, keys = pl.ds(j * size, size), pl.ds(j * size, span)
        v_t = v_ref[keys, :].T
        outs = []
        for h in range(2):
            k_h = jnp.where(head_lanes(h), k_ref[keys, :], 0)
            s = rows_by_rows(k_h, q_ref[rows, :]) + bias_ref[keys, rows]
            top = jnp.max(s, axis=0, keepdims=True)
            p = jnp.exp(s - top)
            total = jnp.sum(p, axis=0, keepdims=True)
            o_t = plain_dot(v_t[h * HD : (h + 1) * HD], p.astype(BF))
            outs.append(o_t / total)
            lse_ref[0, h : h + 1, rows] = top + jnp.log(total)
            peak_ref[0, h : h + 1, rows] = top
        o_ref[rows, :] = jnp.concatenate(outs, axis=0).T.astype(BF)


def attend_forward(q_scaled, keys_in, values_in, first_seen):
    n_query, width = q_scaled.shape
    n_keys = keys_in.shape[0]
    pairs = width // PAIR
    column = lambda i: (0, i)
    stats = jax.ShapeDtypeStruct((pairs, 2, n_query), F32)
    stat_spec = pl.BlockSpec((1, 2, n_query), lambda i: (i, 0, 0))
    return pl.pallas_call(
        attend_kernel,
        grid=(pairs,),
        in_specs=[
            pl.BlockSpec((1, n_query), lambda i: (0, 0)),
            pl.BlockSpec((n_query, PAIR), column),
            pl.BlockSpec((n_keys, PAIR), column),
            pl.BlockSpec((n_keys, PAIR), column),
        ],
        out_specs=[pl.BlockSpec((n_query, PAIR), column), stat_spec, stat_spec],
        out_shape=[jax.ShapeDtypeStruct((n_query, width), BF), stats, stats],
        scratch_shapes=[pltpu.VMEM((n_keys, n_query), F32)],
        compiler_params=pltpu.CompilerParams(vmem_limit_bytes=48 << 20),
        name="attend_forward",
    )(first_seen, q_scaled, keys_in, values_in)


def attend_back_kernel(
    first_ref, q_ref, k_ref, v_ref, o_ref, do_ref, lse_ref, dq_ref, dk_ref, dv_ref,
    bias_ref, dk_acc, dv_acc, *, scale
):
    @pl.when(pl.program_id(0) == 0)
    def _():
        fill_bias(bias_ref, first_ref)

    n_keys, n_query = bias_ref.shape
    size, span = q_tiles(n_query, n_keys)
    dk_acc[...] = jnp.zeros_like(dk_acc)
    dv_acc[...] = jnp.zeros_like(dv_acc)
    for j in range(n_query // size):
        rows, keys = pl.ds(j * size, size), pl.ds(j * size, span)
        q_here, do_here = q_ref[rows, :], do_ref[rows, :]
        k_here, v_here = k_ref[keys, :], v_ref[keys, :]
        k_t = k_here.T
        meet = (do_here.astype(F32) * o_ref[rows, :].astype(F32)).T
        outs = []
        for h in range(2):
            lanes = head_lanes(h)
            delta = jnp.sum(meet[h * HD : (h + 1) * HD], axis=0, keepdims=True)
            s = rows_by_rows(jnp.where(lanes, k_here, 0), q_here) + bias_ref[keys, rows]
            p = jnp.exp(s - lse_ref[0, h : h + 1, rows])
            dp = rows_by_rows(jnp.where(lanes, v_here, 0), do_here)
            ds = (p * (dp - delta)).astype(BF)
            dv_acc[keys, :] += plain_dot(p.astype(BF), jnp.where(lanes, do_here, 0))
            dk_acc[keys, :] += plain_dot(ds, jnp.where(lanes, q_here, 0))
            outs.append(plain_dot(k_t[h * HD : (h + 1) * HD], ds))
        dq_ref[rows, :] = (jnp.concatenate(outs, axis=0).T * scale).astype(BF)
    dk_ref[...] = dk_acc[...].astype(BF)
    dv_ref[...] = dv_acc[...].astype(BF)


def attend_backward(q_scaled, keys_in, values_in, attended, grads_out, log_norms, first_seen):
    n_query, width = q_scaled.shape
    n_keys = keys_in.shape[0]
    pairs = width // PAIR
    column = lambda i: (0, i)
    q_spec = pl.BlockSpec((n_query, PAIR), column)
    k_spec = pl.BlockSpec((n_keys, PAIR), column)
    q_out = jax.ShapeDtypeStruct((n_query, width), BF)
    k_out = jax.ShapeDtypeStruct((n_keys, width), BF)
    return pl.pallas_call(
        functools.partial(attend_back_kernel, scale=1.0 / math.sqrt(HD)),
        grid=(pairs,),
        in_specs=[
            pl.BlockSpec((1, n_query), lambda i: (0, 0)),
            q_spec, k_spec, k_spec, q_spec, q_spec,
            pl.BlockSpec((1, 2, n_query), lambda i: (i, 0, 0)),
        ],
        out_specs=[q_spec, k_spec, k_spec],
        out_shape=[q_out, k_out, k_out],
        scratch_shapes=[
            pltpu.VMEM((n_keys, n_query), F32),
            pltpu.VMEM((n_keys, PAIR), F32),
            pltpu.VMEM((n_keys, PAIR), F32),
        ],
        compiler_params=pltpu.CompilerParams(vmem_limit_bytes=48 << 20),
        name="attend_backward",
    )(first_seen, q_scaled, keys_in, values_in, attended, grads_out, log_norms)


def adam_step(param, grad, first, second, steps_done, decay):
    first_new = BETA_ONE * first + (1.0 - BETA_ONE) * grad
    second_new = BETA_TWO * second + (1.0 - BETA_TWO) * grad * grad
    fix_one = 1.0 - BETA_ONE**steps_done
    fix_two = 1.0 - BETA_TWO**steps_done
    direction = first_new / fix_one / (jnp.sqrt(second_new / fix_two) + EPS_ADAM)
    return (first_new, second_new, param - LEARN_RATE * (direction + decay * param))


def take_kernel(picks_ref, from_ref, to_ref):
    to_ref[...] = from_ref[...]


def take_blocks(blocks, picks):
    shape = (blocks.shape[0], 1, *blocks.shape[2:])
    return pl.pallas_call(
        take_kernel,
        grid_spec=pltpu.PrefetchScalarGridSpec(
            num_scalar_prefetch=1,
            grid=picks.shape,
            in_specs=[pl.BlockSpec(shape, lambda i, p: (0, p[i], 0, 0))],
            out_specs=pl.BlockSpec(shape, lambda i, p: (0, i, 0, 0)),
        ),
        out_shape=jax.ShapeDtypeStruct((shape[0], picks.shape[0], *shape[2:]), blocks.dtype),
        compiler_params=pltpu.CompilerParams(vmem_limit_bytes=32 << 20),
        name="take_blocks",
    )(picks, blocks)


def gather_units(master, slot_of_unit):
    slots = lax.all_gather(master.astype(BF), ("tensor", "dp"), axis=0, tiled=True)
    n_tensor = lax.axis_size("tensor")
    slots = slots.reshape(n_tensor, -1, *master.shape[1:])
    return take_blocks(slots, slot_of_unit)


def scatter_units(units, unit_of_slot):
    slots = take_blocks(units, unit_of_slot)
    slots = slots.reshape(-1, *units.shape[2:])
    return lax.psum_scatter(slots, ("tensor", "dp"), scatter_dimension=0, tiled=True)


def per_device(
    tokens_in,
    out_grad,
    lengths,
    owners,
    matrix_master,
    matrix_m1,
    matrix_m2,
    shared_params,
    bias_params,
):
    n_tensor = lax.axis_size("tensor")
    n_data = lax.axis_size("dp")
    tensor_index = lax.axis_index("tensor")
    data_index = lax.axis_index("dp")
    rows_here, width = tokens_in.shape
    slot_cap = matrix_master.shape[1]
    unit_rows = matrix_master.shape[2]
    n_units = owners.shape[0]
    n_slots = n_data * slot_cap
    head_rows = width // n_tensor
    heads_here = head_rows // HD
    ff_rows = (n_units * unit_rows - 4 * head_rows) // 2
    slot_of_unit, unit_of_slot, occupied = slot_tables(owners, n_slots, slot_cap)

    units = gather_units(matrix_master[0], slot_of_unit)
    stacks = units.reshape(n_tensor, n_units * unit_rows, width)
    part = lambda first, count: stacks[:, first : first + count].reshape(-1, width)
    w_q, w_k, w_v, w_out = (part(i * head_rows, head_rows) for i in range(4))
    w_fc = part(4 * head_rows, ff_rows)
    w_proj = part(4 * head_rows + ff_rows, ff_rows)
    all_bias = lax.all_gather(bias_params[0], "tensor", axis=0, tiled=True)
    bias = lambda first, count: all_bias[:, first : first + count].reshape(-1)
    b_q, b_k, b_v = (bias(i * head_rows, head_rows) for i in range(3))
    b_fc = bias(3 * head_rows, ff_rows)

    back = -(-(DOC_MOST - 1) // rows_here)
    reach = back * rows_here
    sizes = lengths[0]
    upto = jnp.arange(sizes.shape[0])[:, None] >= jnp.arange(sizes.shape[0])[None, :]
    bounds = jnp.sum(jnp.where(upto, sizes[None, :], 0), axis=1)
    places = tensor_index * rows_here + jnp.arange(rows_here, dtype=jnp.int32)
    starts = jnp.max(jnp.where(places[:, None] >= bounds[None, :], bounds[None, :], 0), axis=1)
    first_seen = (starts - tensor_index * rows_here + reach)[None, :]

    shared = shared_params[0]
    inputs_f32 = tokens_in.astype(F32)
    normed_one, hat_one, inverse_one = norm_rows(inputs_f32, shared[0], shared[1])
    normed_low = normed_one.astype(BF)
    before = [
        lax.ppermute(normed_low, "tensor", [(i, i + r) for i in range(n_tensor - r)])
        for r in range(min(back, n_tensor - 1), 0, -1)
    ]
    blank = [jnp.zeros_like(normed_low)] * (back - len(before))
    normed_all = jnp.concatenate([*blank, *before, normed_low], axis=0)
    scale = 1.0 / math.sqrt(HD)
    q_scaled = (rows_by_rows(normed_low, w_q) + b_q).astype(BF) * jnp.asarray(scale, BF)
    keys_in = (rows_by_rows(normed_all, w_k) + b_k).astype(BF)
    values_in = (rows_by_rows(normed_all, w_v) + b_v).astype(BF)
    attended, log_norms, peaks = attend_forward(q_scaled, keys_in, values_in, first_seen)
    hidden = inputs_f32 + (plain_dot(attended, w_out) + shared[2])
    normed_two, hat_two, inverse_two = norm_rows(hidden, shared[3], shared[4])
    second_low = normed_two.astype(BF)
    pre_act = rows_by_rows(second_low, w_fc) + b_fc
    activ, gelu_back = jax.vjp(gelu_tanh, pre_act)
    activ_low = activ.astype(BF)
    layer_out = hidden + (plain_dot(activ_low, w_proj) + shared[5])

    grad_y = out_grad.astype(F32)
    grad_proj_w = cols_by_cols(activ_low, out_grad)
    grad_activ = rows_by_rows(out_grad, w_proj)
    grad_pre_low = gelu_back(grad_activ)[0].astype(BF)
    grad_fc_b = jnp.sum(grad_pre_low, axis=0, dtype=F32)
    grad_fc_w = cols_by_cols(grad_pre_low, second_low)
    grad_second = plain_dot(grad_pre_low, w_fc)
    grad_hidden = grad_y + norm_back(grad_second, hat_two, inverse_two, shared[3])
    grad_hidden_low = grad_hidden.astype(BF)
    grad_out_w = cols_by_cols(attended, grad_hidden_low)
    grad_attended = rows_by_rows(grad_hidden_low, w_out).astype(BF)
    grad_q, grad_k, grad_v = attend_backward(
        q_scaled, keys_in, values_in, attended, grad_attended, log_norms, first_seen
    )
    grad_q_w = cols_by_cols(grad_q, normed_low)
    grad_k_w = cols_by_cols(grad_k, normed_all)
    grad_v_w = cols_by_cols(grad_v, normed_all)
    grad_wide = plain_dot(grad_k, w_k) + plain_dot(grad_v, w_v)
    grad_first = grad_wide[reach:] + plain_dot(grad_q, w_q)
    for r in range(1, min(back, n_tensor - 1) + 1):
        away = grad_wide[reach - r * rows_here : reach - (r - 1) * rows_here].astype(BF)
        grad_first += lax.ppermute(away, "tensor", [(i, i - r) for i in range(r, n_tensor)]).astype(F32)
    input_grad = grad_hidden + norm_back(grad_first, hat_one, inverse_one, shared[0])

    head_all = lax.pmax(jnp.max(peaks, axis=2).reshape(-1), ("dp", "tensor"))
    head_peak = lax.dynamic_slice_in_dim(head_all, tensor_index * heads_here, heads_here)
    grad_qkv_b = [jnp.sum(g, axis=0, dtype=F32) for g in (grad_q, grad_k, grad_v)]
    shared_part = jnp.stack(
        [
            jnp.sum(grad_first * hat_one, axis=0),
            jnp.sum(grad_first, axis=0),
            jnp.sum(grad_hidden_low, axis=0, dtype=F32),
            jnp.sum(grad_second * hat_two, axis=0),
            jnp.sum(grad_second, axis=0),
            jnp.sum(grad_y, axis=0),
        ]
    )
    by_tensor = lambda v: v.reshape(n_tensor, -1)
    bias_part = jnp.concatenate([by_tensor(v) for v in (*grad_qkv_b, grad_fc_b)], axis=1)
    shared_grad, bias_total = lax.psum((shared_part, bias_part), ("dp", "tensor"))
    bias_grad = lax.dynamic_index_in_dim(bias_total, tensor_index, 0, keepdims=False)

    by_stack = lambda g: g.astype(BF).reshape(n_tensor, -1, width)
    grad_units = jnp.concatenate(
        [by_stack(g) for g in (grad_q_w, grad_k_w, grad_v_w, grad_out_w, grad_fc_w, grad_proj_w)], axis=1
    ).reshape(units.shape)
    my_grads = scatter_units(grad_units, unit_of_slot).astype(F32)

    my_units = lax.dynamic_slice_in_dim(unit_of_slot, data_index * slot_cap, slot_cap, 0)
    my_occupied = lax.dynamic_slice_in_dim(occupied, data_index * slot_cap, slot_cap, 0)[:, None, None]
    steps_done = float(STEP)
    first_new, second_new, master_new = adam_step(
        matrix_master[0], my_grads, matrix_m1[0], matrix_m2[0], steps_done, WEIGHT_DECAY
    )
    root_gamma = jnp.sqrt(CLIP_TAU / jnp.maximum(head_peak, CLIP_TAU))
    row_index = my_units[:, None] * unit_rows + jnp.arange(unit_rows, dtype=jnp.int32)[None, :]
    local_head = jnp.where(row_index < head_rows, row_index // HD, (row_index - head_rows) // HD)
    head_match = local_head[..., None] == jnp.arange(heads_here, dtype=jnp.int32)[None, None, :]
    picked_root = jnp.sum(jnp.where(head_match, root_gamma, 0.0), axis=-1)
    factor = jnp.where(row_index < 2 * head_rows, picked_root, 1.0)
    my_grads = jnp.where(my_occupied, my_grads, 0.0)
    master_new = jnp.where(my_occupied, master_new * factor[..., None], 0.0)
    first_new = jnp.where(my_occupied, first_new, 0.0)
    second_new = jnp.where(my_occupied, second_new, 0.0)
    shared_first, shared_second, shared_new = adam_step(
        shared, shared_grad, shared_params[1], shared_params[2], steps_done, 0.0
    )
    bias_first, bias_second, bias_new = adam_step(
        bias_params[0, 0], bias_grad, bias_params[1, 0], bias_params[2, 0], steps_done, 0.0
    )
    shared_out = jnp.stack([shared_grad, shared_first])
    bias_out = jnp.stack([bias_grad, bias_first])[:, None, :]
    return (
        layer_out,
        input_grad,
        head_peak,
        my_grads[None],
        first_new[None],
        second_new[None],
        master_new[None],
        shared_out,
        shared_second,
        shared_new,
        bias_out,
        bias_second[None],
        bias_new[None],
    )


def solution(mesh):
    in_specs = (
        P(("dp", "tensor"), None),
        P(("dp", "tensor"), None),
        P("dp", None),
        P(),
        P("tensor", "dp", None, None),
        P("tensor", "dp", None, None),
        P("tensor", "dp", None, None),
        P(),
        P(None, "tensor", None),
    )
    out_specs = (
        P(("dp", "tensor"), None),
        P(("dp", "tensor"), None),
        P("tensor"),
        P("tensor", "dp", None, None),
        P("tensor", "dp", None, None),
        P("tensor", "dp", None, None),
        P("tensor", "dp", None, None),
        P(),
        P(),
        P(),
        P(None, "tensor", None),
        P("tensor", None),
        P("tensor", None),
    )
    return jax.shard_map(
        per_device, mesh=mesh, in_specs=in_specs, out_specs=out_specs, check_vma=False
    )
```

time: 1300 us -> 905 us (0.70)
  waiting for transfers between devices: 809 us -> 274 us
  blocking collectives: 51.9 us -> 300 us
  matrix products: 249 us -> 112 us
  Pallas kernels: 0 us -> 112 us
  other arithmetic: 80.9 us -> 24.4 us
  local copies, waits for them, and re-layouts: 68 us -> 48.1 us
    reduce_scatter x4 -> x1, waiting for transfers between devices: 408 us -> 115 us  [scatter_units(): lax.psum_scatter(slots, ('tensor', 'dp'), scatter_dimension=0, tiled=True)]
    all_gather x5 -> x1, waiting for transfers between devices: 318 us -> 103 us  [gather_units(): lax.all_gather(master.astype(BF), ('tensor', 'dp'), axis=0, tiled=True)]
    dot_general x94 -> x6, matrix products: 188 us -> 37.9 us  [plain_dot(): return jnp.dot(left, right, preferred_element_type=F32)]
    all_gather x0 -> x1, blocking collectives: none -> 134 us  [per_device(): all_bias = lax.all_gather(bias_params[0], 'tensor', axis=0, tiled=True)]
    pallas_call x0 -> x4, Pallas kernels: none -> 112 us  [the longest x2 48.6 us: take_blocks(): pl.pallas_call(take_kernel, grid_spec=pltpu.PrefetchScalarGridSpec(num_sc...]
    psum x1 -> x0, waiting for transfers between devices: 83.2 us -> none  [per_device(): summed = lax.psum(grad_stack.astype(jnp.bfloat16), 'dp').astype(jnp.float32)]
    psum x1, blocking collectives: 39.7 us -> 107 us  [per_device(): lax.psum((shared_part, bias_part), ('dp', 'tensor'))]
    ppermute x0 -> x4, waiting for transfers between devices: none -> 56 us  [the longest x2 56 us: per_device(): lax.ppermute(away, 'tensor', [(i, i - r) for i in range(r, n_tensor)])]
  transfers between devices with their start and end apart: 10 -> 6, of which waited for: 10 -> 4; matrix products, arithmetic and copies ran while one was open for 8% -> 6% of each run, Pallas kernels for 0% -> 2%
where the time goes in v1:
time: 905 us; the launch traced here: 896 us
  blocking collectives  300 us (33%)
  waiting for transfers between devices  274 us (30%)
  Pallas kernels  112 us (12%)
  matrix products  112 us (12%)
  local copies, waits for them, and re-layouts  48.1 us (5%)
  other arithmetic  24.4 us (3%)
  between operations  15.1 us (2%)
  starting transfers between devices  10 us (1%)
    all_gather x1, blocking collectives, per_device(): all_bias = lax.all_gather(bias_params[0], 'tensor', axis=0, tiled=True)  134 us
    reduce_scatter x1, waiting for transfers between devices, scatter_units(): lax.psum_scatter(slots, ('tensor', 'dp'), scatter_dimension=0, tiled=True)  115 us
    psum x1, blocking collectives, per_device(): lax.psum((shared_part, bias_part), ('dp', 'tensor'))  107 us
    all_gather x1, waiting for transfers between devices, gather_units(): lax.all_gather(master.astype(BF), ('tensor', 'dp'), axis=0, tiled=True)  103 us
    pmax x1, blocking collectives, per_device(): head_all = lax.pmax(jnp.max(peaks, axis=2).reshape(-1), ('dp', 'tensor'))  59.8 us
    ppermute x2, waiting for transfers between devices, per_device(): lax.ppermute(away, 'tensor', [(i, i - r) for i in range(r, n_tensor)])  56 us
    pallas_call x2, Pallas kernels, take_blocks(): pl.pallas_call(take_kernel, grid_spec=pltpu.PrefetchScalarGridSpec(num_sc...  48.6 us
    dot_general x6, matrix products, rows_by_rows(): lax.dot_general(left, right, (((1,), (1,)), ((), ())), preferred_element_...  40.9 us
  transfers between devices with their start and end apart: 6, of which 4 were waited for; matrix products, arithmetic and copies ran while one was open for 6% of the time, Pallas kernels for 2%

profile of v1, /device:TPU:9, one launch (start us, length us, event | category | flops | bytes accessed | tf_op | source)
XLA Modules:
  0.0 895.8 jit_solution(16086563431394006515)
XLA Ops:
  16.1 3.3 collective-permute-start
  19.4 133.8 %all-gather = f32[4,1,1792]{2,1,0:T(1,128)S(1)} all-gather(f32[1,1,1792]{2,1,0:T(1,128)S(1)} %slice-done.2), channel_id=2, replica_groups=mesh['dp'=8,'tensor'=4] {'tensor'}, dimensions={0}, use_global_device_ids=true | all-gather | bytes 35840 | tf_op jit(solution)/shard_map/all_gather | solution.py:278
  153.8 103.1 %all-gather.3.cloned.1.call-done = bf16[64,256,1024]{2,1,0:T(8,128)(2,1)} async-done(((bf16[2,256,1024]{2,1,0:T(8,128)(2,1)}), bf16[64,256,1024]{2,1,0:T(8,128)(2,1)}) %all-gather.3.cloned.1.call-update) | async-done | bytes 33554448 | tf_op jit(solution)/shard_map/all_gather | solution.py:235
  256.9 21.0 %take_blocks.2 = bf16[4,12,256,1024]{3,2,1,0:T(8,128)(2,1)} custom-call(s32[12]{0:T(128)S(1)} %multiply_add_fusion.picks_ref, bf16[4,16,256,1024]{3,2,1,0:T(8,128)(2,1)} %bitcast.164), custom_call_target="tpu_custom_call" | custom-call | tf_op jit(solution)/shard_map/take_blocks/pallas_call | solution.py:220
  277.9 5.0 fusion.51
  285.6 6.0 copy-done.3
  291.5 6.2 fusion.50
  297.8 6.6 add_convert_fusion.v_ref
  304.3 5.0 add_convert_fusion.1.k_ref
  309.4 32.5 %attend_forward.1 = (bf16[512,1024]{1,0:T(8,128)(2,1)S(1)}, f32[8,2,512]{2,1,0:T(2,128)S(1)}, f32[8,2,512]{2,1,0:T(2,128)S(1)}) custom-call(s32[1,512]{1,0:T(1,128)S(1)} %bitcast.159, bf16[512,1024]{1,0:T(8,128)(2,1)S(1)} %fusion.34.q_ref, bf16[1536,1024]{1,0:T(8,128)(2,1)S(1)} %add_convert_fusion.1.k_ref, bf16[1536,1024]{1,0:T(8,128)(2,1)} %add_convert_fusion.v_ref), custom_call_target="tpu_custom_call" | custom-call | tf_op jit(solution)/shard_map/attend_forward/pallas_call | solution.py:125
  343.8 10.4 %fusion.56 = f32[4096,512]{0,1:T(8,128)} fusion(bf16[4096,1024]{1,0:T(8,128)(2,1)} %bitcast.167, bf16[512,1024]{1,0:T(8,128)(2,1)S(1)} %copy-done.18), kind=kOutput, calls=%fused_computation.156 | convolution fusion | flops 4294967296 | bytes 17825792 | tf_op jit(solution)/shard_map/dot_general | solution.py:33
  354.2 16.3 %convert_reduce_fusion = (f32[4096]{0:T(1024)S(1)}, bf16[512,4096]{1,0:T(8,128)(2,1)}, f32[512,4096]{1,0:T(8,128)}) fusion(f32[4096]{0:T(1024)S(1)} %bitcast.198, f32[4096,512]{0,1:T(8,128)} %fusion.56, bf16[4096,1024]{1,0:T(8,128)(2,1)} %bitcast.171, f32[512,1024]{1,0:T(8,128)S(1)} %get-tuple-element.123, f32[1024]{0:T(1024)S(1)} %bitcast.206, ...), kind=kOutput, calls=%fused_computation.14 | convolution fusion | flops 4345819136 | bytes 31502336 | tf_op jit(solution)/shard_map/dot_general | solution.py:33
  370.5 9.1 %multiply_reduce_fusion = (f32[1024]{0:T(1024)S(1)}, f32[512]{0:T(512)S(1)}, f32[512]{0:T(512)S(1)}, f32[1024]{0:T(1024)S(1)}, f32[512,1024]{1,0:T(8,128)S(1)}) fusion(f32[512,1024]{1,0:T(8,128)S(1)} %get-tuple-element.123, f32[512]{0:T(512)S(1)} %add_rsqrt_fusion, f32[512]{0:T(512)S(1)} %broadcast_multiply_fusion.4, f32[1024]{0:T(1024)S(1)} %bitcast.194, ...), kind=kOutput, calls=%fused_computation.62 | convolution fusion | flops 4299682816 | bytes 16797696 | tf_op jit(solution)/shard_map/dot_general | solution.py:29
  384.1 7.2 convolution_convert_fusion.1
  391.3 13.1 %convolution_convert_fusion = bf16[4096,1024]{1,0:T(8,128)(2,1)} fusion(bf16[512,1024]{1,0:T(8,128)(2,1)S(1)} %copy-done.18, f32[512,4096]{1,0:T(8,128)} %get-tuple-element.124, f32[4096]{0:T(1024)S(1)} %bitcast.199), kind=kOutput, calls=%fused_computation.16 | convolution fusion | flops 4320133120 | bytes 17842176 | tf_op jit(solution)/shard_map/dot_general | solution.py:37
  404.4 30.8 %attend_backward.1 = (bf16[512,1024]{1,0:T(8,128)(2,1)S(1)}, bf16[1536,1024]{1,0:T(8,128)(2,1)}, bf16[1536,1024]{1,0:T(8,128)(2,1)}) custom-call(s32[1,512]{1,0:T(1,128)S(1)} %bitcast.160, bf16[512,1024]{1,0:T(8,128)(2,1)S(1)} %fusion.34.q_ref, bf16[1536,1024]{1,0:T(8,128)(2,1)} %copy-done, bf16[1536,1024]{1,0:T(8,128)(2,1)} %add_convert_fusion.v_ref, ...), custom_call_target="tpu_custom_call" | custom-call | tf_op jit(solution)/shard_map/attend_backward/pallas_call | solution.py:185
  439.1 5.1 convolution_convert_fusion.4
  446.9 5.1 convolution_convert_fusion.3
  455.0 7.8 constant_dynamic-update-slice_fusion.1
  462.8 7.6 constant_dynamic-update-slice_fusion
  470.4 27.6 %take_blocks.3 = bf16[4,16,256,1024]{3,2,1,0:T(8,128)(2,1)} custom-call(s32[16]{0:T(128)S(1)} %select_reduce_fusion.1.picks_ref, bf16[4,12,256,1024]{3,2,1,0:T(8,128)(2,1)} %bitcast.24.from_ref), custom_call_target="tpu_custom_call" | custom-call | tf_op jit(solution)/shard_map/take_blocks/pallas_call | solution.py:220
  499.1 59.8 %pmax.7 = f32[16]{0:T(128)S(1)} all-reduce(f32[16]{0:T(128)S(1)} %reshape.296), channel_id=1, replica_groups=mesh['dp'=8,'tensor'=4] {'dp','tensor'}, use_global_device_ids=true, to_apply=%region_12.13 | all-reduce | flops 16 | bytes 128 | tf_op jit(solution)/shard_map/pmax | solution.py:339
  561.6 5.6 fusion.57
  567.2 5.3 fusion.55
  577.2 10.4 %add_add_fusion = f32[512,1024]{1,0:T(8,128)} fusion(f32[512,1024]{1,0:T(8,128)S(1)} %copy-done.7, bf16[4096,1024]{1,0:T(8,128)(2,1)S(1)} %bitcast.170, f32[1024]{0:T(1024)S(1)} %bitcast.205, f32[512,4096]{1,0:T(8,128)} %get-tuple-element.124, f32[4096]{0:T(1024)S(1)} %bitcast.200), kind=kOutput, calls=%fused_computation.67 | convolution fusion | flops 4316987392 | bytes 20992000 | tf_op jit(solution)/shard_map/dot_general | solution.py:29
  589.2 24.7 %collective-permute-done.2 = bf16[512,1024]{1,0:T(8,128)(2,1)} collective-permute-done((bf16[512,1024]{1,0:T(8,128)(2,1)}, bf16[512,1024]{1,0:T(8,128)(2,1)}, u32[]{:S(2)}, u32[]{:S(2)}) %collective-permute-start.2) | collective-permute-done | bytes 1048608 | tf_op jit(solution)/shard_map/ppermute | solution.py:336
  613.9 31.3 %collective-permute-done.3 = bf16[512,1024]{1,0:T(8,128)(2,1)} collective-permute-done((bf16[512,1024]{1,0:T(8,128)(2,1)S(1)}, bf16[512,1024]{1,0:T(8,128)(2,1)}, u32[]{:S(2)}, u32[]{:S(2)}) %collective-permute-start.3) | collective-permute-done | bytes 1048608 | tf_op jit(solution)/shard_map/ppermute | solution.py:336
  645.2 6.1 fusion.22
  651.4 106.6 %all-reduce = (f32[6,1024]{1,0:T(8,128)S(1)}, f32[4,1792]{1,0:T(4,128)S(1)}) all-reduce(f32[6,1024]{1,0:T(8,128)S(1)} %stack.41, f32[4,1792]{1,0:T(4,128)S(1)} %pad_maximum_fusion.2), channel_id=1, replica_groups=mesh['dp'=8,'tensor'=4] {'dp','tensor'}, use_global_device_ids=true, to_apply=%region_23.24 | all-reduce | flops 13312 | bytes 106496 | tf_op jit(solution)/shard_map/psum | solution.py:354
  760.6 4.3 fusion.21
  765.0 115.0 %reduce-scatter.2.cloned.1.call-done = bf16[2,256,1024]{2,1,0:T(8,128)(2,1)} async-done(((bf16[64,256,1024]{2,1,0:T(8,128)(2,1)}), bf16[2,256,1024]{2,1,0:T(8,128)(2,1)}) %reduce-scatter.2.cloned.1.call-update) | async-done | bytes 1048592 | tf_op jit(solution)/shard_map/reduce_scatter | solution.py:244
  879.9 8.5 fusion.33
  (143 shorter events, 40.3 us)
Async XLA Ops:
  7.2 249.7 %all-gather.3.cloned.1.call-start = ((), (), s32[]{:S(2)}) async-start(), calls=%async_computation.1 | async-start | bytes 34603008 | tf_op jit(solution)/shard_map/all_gather | solution.py:235
  10.0 9.3 %slice-start.2 = ((f32[3,1,1792]{2,1,0:T(1,128)}), f32[1,1,1792]{2,1,0:T(1,128)S(1)}, s32[]{:S(2)}) async-start(f32[3,1,1792]{2,1,0:T(1,128)} %param.17), calls=%async_computation.5 | async-start | bytes 14336 | tf_op jit(solution)/shard_map/slice | solution.py:278
  10.0 143.2 %copy-start.30 = (s32[1,4]{1,0:T(1,128)S(1)}, s32[1,4]{1,0:T(1,128)}, u32[]{:S(2)}) copy-start(s32[1,4]{1,0:T(1,128)} %param.11) | copy-start | bytes 52
  10.0 143.4 %copy-start.31 = (s32[12]{0:T(128)S(1)}, s32[12]{0:T(128)}, u32[]{:S(2)}) copy-start(s32[12]{0:T(128)} %param.12) | copy-start | bytes 148
  10.1 869.9 %reduce-scatter.2.cloned.1.call-start = ((), (), s32[]{:S(2)}) async-start(), calls=%async_computation.2 | async-start | bytes 34603008 | tf_op jit(solution)/shard_map/reduce_scatter | solution.py:244
  10.3 267.6 %copy-start.25 = (f32[512]{0:T(512)}, f32[512]{0:T(512)S(1)}, u32[]{:S(2)}) copy-start(f32[512]{0:T(512)S(1)} %broadcast_multiply_fusion.5) | copy-start | bytes 6148
  10.8 267.1 %copy-start.27 = (f32[512]{0:T(512)}, f32[512]{0:T(512)S(1)}, u32[]{:S(2)}) copy-start(f32[512]{0:T(512)S(1)} %add_rsqrt_fusion.1) | copy-start | bytes 6148
  12.4 265.5 %copy-start.23 = (f32[1,1,1024]{2,1,0:T(1,128)}, f32[1,1,1024]{2,1,0:T(1,128)S(1)}, u32[]{:S(2)}) copy-start(f32[1,1,1024]{2,1,0:T(1,128)S(1)} %get-tuple-element.118) | copy-start | bytes 12292
  12.8 291.5 %copy-start.19 = (bf16[512,1024]{1,0:T(8,128)(2,1)}, bf16[512,1024]{1,0:T(8,128)(2,1)S(1)}, u32[]{:S(2)}) copy-start(bf16[512,1024]{1,0:T(8,128)(2,1)S(1)} %fusion.17) | copy-start | bytes 3145732
  12.9 284.9 %collective-permute-start.1 = (bf16[512,1024]{1,0:T(8,128)(2,1)S(1)}, bf16[512,1024]{1,0:T(8,128)(2,1)}, u32[]{:S(2)}, u32[]{:S(2)}) collective-permute-start(bf16[512,1024]{1,0:T(8,128)(2,1)S(1)} %fusion.17), channel_id=1, source_target_pairs={{0,1},{1,2},{2,3},{4,5},{5,6},{6,7},{8,9},{9,10},{10,11},{12,13},{... | collective-permute-start | bytes 3145736 | tf_op jit(solution)/shard_map/ppermute | solution.py:297
  16.1 281.7 %collective-permute-start = (bf16[512,1024]{1,0:T(8,128)(2,1)S(1)}, bf16[512,1024]{1,0:T(8,128)(2,1)}, u32[]{:S(2)}, u32[]{:S(2)}) collective-permute-start(bf16[512,1024]{1,0:T(8,128)(2,1)S(1)} %fusion.17), channel_id=1, source_target_pairs={{0,2},{1,3},{4,6},{5,7},{8,10},{9,11},{12,14},{13,15},{16,18},{17,... | collective-permute-start | bytes 3145736 | tf_op jit(solution)/shard_map/ppermute | solution.py:297
  153.6 124.3 %copy-start.1 = (s32[12]{0:T(128)}, s32[12]{0:T(128)S(1)}, u32[]{:S(2)}) copy-start(s32[12]{0:T(128)S(1)} %multiply_add_fusion.picks_ref) | copy-start | bytes 148
  277.9 13.6 %copy-start.3 = (bf16[4,12,256,1024]{3,2,1,0:T(8,128)(2,1)S(1)}, bf16[4,12,256,1024]{3,2,1,0:T(8,128)(2,1)}, u32[]{:S(2)}) copy-start(bf16[4,12,256,1024]{3,2,1,0:T(8,128)(2,1)} %take_blocks.2) | copy-start | bytes 75497472
  283.0 14.8 %copy-start.13 = (bf16[4,256,1024]{2,1,0:T(8,128)(2,1)}, bf16[4,256,1024]{2,1,0:T(8,128)(2,1)S(1)}, u32[]{:S(2)}) copy-start(bf16[4,256,1024]{2,1,0:T(8,128)(2,1)S(1)} %get-tuple-element.102) | copy-start | bytes 6291460
  283.0 21.4 %copy-start.15 = (bf16[4,256,1024]{2,1,0:T(8,128)(2,1)}, bf16[4,256,1024]{2,1,0:T(8,128)(2,1)S(1)}, u32[]{:S(2)}) copy-start(bf16[4,256,1024]{2,1,0:T(8,128)(2,1)S(1)} %get-tuple-element.103) | copy-start | bytes 6291460
  309.4 32.6 %copy-start = (bf16[1536,1024]{1,0:T(8,128)(2,1)}, bf16[1536,1024]{1,0:T(8,128)(2,1)S(1)}, u32[]{:S(2)}) copy-start(bf16[1536,1024]{1,0:T(8,128)(2,1)S(1)} %add_convert_fusion.1.k_ref) | copy-start | bytes 9437188
  309.4 32.6 %copy-start.17 = (bf16[4,256,1024]{2,1,0:T(8,128)(2,1)S(1)}, bf16[4,256,1024]{2,1,0:T(8,128)(2,1)}, u32[]{:S(2)}) copy-start(bf16[4,256,1024]{2,1,0:T(8,128)(2,1)} %get-tuple-element.101) | copy-start | bytes 6291460
  343.4 39.9 %copy-start.6 = (f32[512,1024]{1,0:T(8,128)}, f32[512,1024]{1,0:T(8,128)S(1)}, u32[]{:S(2)}) copy-start(f32[512,1024]{1,0:T(8,128)S(1)} %get-tuple-element.123) | copy-start | bytes 6291460
  380.6 10.7 %copy-start.8 = (f32[512,1024]{1,0:T(8,128)}, f32[512,1024]{1,0:T(8,128)S(1)}, u32[]{:S(2)}) copy-start(f32[512,1024]{1,0:T(8,128)S(1)} %get-tuple-element.96) | copy-start | bytes 6291460
  404.3 30.8 %copy-start.20 = (bf16[512,1024]{1,0:T(8,128)(2,1)S(1)}, bf16[512,1024]{1,0:T(8,128)(2,1)}, u32[]{:S(2)}) copy-start(bf16[512,1024]{1,0:T(8,128)(2,1)} %copy-done.19) | copy-start | bytes 3145732
  498.0 63.5 %copy-start.16 = (bf16[4,256,1024]{2,1,0:T(8,128)(2,1)S(1)}, bf16[4,256,1024]{2,1,0:T(8,128)(2,1)}, u32[]{:S(2)}) copy-start(bf16[4,256,1024]{2,1,0:T(8,128)(2,1)} %copy-done.15) | copy-start | bytes 6291460
  561.5 5.7 copy-start.10
  561.5 15.6 %slice-start = ((s8[8388608]{0:T(1024)(128)(4,1)}), s8[4194304]{0:T(1024)(128)(4,1)S(1)}, s32[]{:S(2)}) async-start(s8[8388608]{0:T(1024)(128)(4,1)} %bitcast.168), calls=%async_computation.3 | async-start | bytes 8388608
  567.2 10.0 %slice-start.1 = ((s8[8388608]{0:T(1024)(128)(4,1)}), s8[4194304]{0:T(1024)(128)(4,1)S(1)}, s32[]{:S(2)}) async-start(s8[8388608]{0:T(1024)(128)(4,1)} %bitcast.168), calls=%async_computation.4 | async-start | bytes 8388608
  573.7 40.2 %collective-permute-start.2 = (bf16[512,1024]{1,0:T(8,128)(2,1)}, bf16[512,1024]{1,0:T(8,128)(2,1)}, u32[]{:S(2)}, u32[]{:S(2)}) collective-permute-start(bf16[512,1024]{1,0:T(8,128)(2,1)} %get-tuple-element.108), channel_id=1, source_target_pairs={{1,0},{2,1},{3,2},{5,4},{6,5},{7,6},{9,8},{10,9},{11,10},{13,12},{... | collective-permute-start | bytes 3145736 | tf_op jit(solution)/shard_map/ppermute | solution.py:336
  575.6 69.6 %collective-permute-start.3 = (bf16[512,1024]{1,0:T(8,128)(2,1)S(1)}, bf16[512,1024]{1,0:T(8,128)(2,1)}, u32[]{:S(2)}, u32[]{:S(2)}) collective-permute-start(bf16[512,1024]{1,0:T(8,128)(2,1)S(1)} %get-tuple-element.109), channel_id=1, source_target_pairs={{2,0},{3,1},{6,4},{7,5},{10,8},{11,9},{14,12},{15,13},{18,16},{19,... | collective-permute-start | bytes 3145736 | tf_op jit(solution)/shard_map/ppermute | solution.py:336
  587.6 57.6 %copy-start.5 = (bf16[512,1024]{1,0:T(8,128)(2,1)S(1)}, bf16[512,1024]{1,0:T(8,128)(2,1)}, u32[]{:S(2)}) copy-start(bf16[512,1024]{1,0:T(8,128)(2,1)} %param.9) | copy-start | bytes 3145732
  587.6 57.6 %copy-start.24 = (f32[1,1,1024]{2,1,0:T(1,128)S(1)}, f32[1,1,1024]{2,1,0:T(1,128)}, u32[]{:S(2)}) copy-start(f32[1,1,1024]{2,1,0:T(1,128)} %copy-done.23) | copy-start | bytes 12292
  587.6 57.6 %copy-start.26 = (f32[512]{0:T(512)S(1)}, f32[512]{0:T(512)}, u32[]{:S(2)}) copy-start(f32[512]{0:T(512)} %copy-done.25) | copy-start | bytes 6148
  587.6 57.6 %copy-start.28 = (f32[512]{0:T(512)S(1)}, f32[512]{0:T(512)}, u32[]{:S(2)}) copy-start(f32[512]{0:T(512)} %copy-done.27) | copy-start | bytes 6148
  645.2 112.8 %copy-start.22 = (f32[3,1,1792]{2,1,0:T(1,128)S(1)}, f32[3,1,1792]{2,1,0:T(1,128)}, u32[]{:S(2)}) copy-start(f32[3,1,1792]{2,1,0:T(1,128)} %param.17) | copy-start | bytes 64516
  645.2 114.1 %copy-start.21 = (f32[3,6,1024]{2,1,0:T(8,128)S(1)}, f32[3,6,1024]{2,1,0:T(8,128)}, u32[]{:S(2)}) copy-start(f32[3,6,1024]{2,1,0:T(8,128)} %param.16) | copy-start | bytes 221188
  (10 other events, 29.1 us)
Sparse Core Ops, SparseCore 0:
  11.5 245.3 all-gather.2
  498.1 381.8 reduce-scatter.1

commit v2 on v1

--- a/solution.py
+++ b/solution.py
@@ -23,6 +23,8 @@
 MASKED = -1e30
 BF = jnp.bfloat16
 F32 = jnp.float32
+MESH = pl.DeviceIdType.MESH
+MAX_ROW = 13
 
 
 def plain_dot(left, right):
@@ -244,6 +246,436 @@
     return lax.psum_scatter(slots, ("tensor", "dp"), scatter_dimension=0, tiled=True)
 
 
+def send(src, dst, send_sem, recv_sem, to):
+    copy = pltpu.make_async_remote_copy(
+        src_ref=src, dst_ref=dst, send_sem=send_sem, recv_sem=recv_sem,
+        device_id=to, device_id_type=MESH,
+    )
+    copy.start()
+    return copy
+
+
+def arrived(ref, sem):
+    pltpu.make_async_copy(ref, ref, sem).wait()
+
+
+def place():
+    d, t = lax.axis_index("dp"), lax.axis_index("tensor")
+    core, x, y = d % 2, (d // 2) % 2, d // 4
+    return d, t, core, x, y
+
+
+def greet(d, t, n_tensor):
+    barrier = pltpu.get_barrier_semaphore()
+    for k in range(1, 8):
+        pl.semaphore_signal(barrier, inc=1, device_id=((d + k) % 8, t), device_id_type=MESH)
+    for k in range(1, n_tensor):
+        pl.semaphore_signal(barrier, inc=1, device_id=(d, (t + k) % n_tensor), device_id_type=MESH)
+    pl.semaphore_wait(barrier, 6 + n_tensor)
+
+
+def spread_kernel(
+    groups, n_tensor, back,
+    slot_ref, master_ref, a_ref, bias_ref, w_ref, wide_ref, biases_ref,
+    pieces, own, blank, swap_send, swap_recv, local_sem, a_send, a_recv, bias_send, bias_recv,
+    z_send, z_recv, xy_send, xy_recv, core_send, core_recv,
+):
+    d, t, core, x, y = place()
+    column = y * 2 + x
+    by_x, by_y = d + 2 - 4 * x, d + 4 - 8 * y
+    sibling = d + 1 - 2 * core
+    greet(d, t, n_tensor)
+    first, last = t > 0, t < n_tensor - 1
+    for k in range(1, n_tensor):
+        send(bias_ref, biases_ref.at[t], bias_send.at[k - 1], bias_recv.at[k - 1], (d, (t + k) % n_tensor))
+    biases_ref[t] = bias_ref[...]
+
+    @pl.when(last)
+    def _():
+        send(a_ref, wide_ref.at[back - 1], a_send.at[0], a_recv.at[0], (d, t + 1))
+
+    cap = master_ref.shape[0]
+    for k in range(1, 8):
+        to = (d + k) % 8
+        send(master_ref.at[:, to], pieces.at[d], swap_send.at[k - 1], swap_recv.at[k - 1], (to, t))
+    mine = pltpu.make_async_copy(master_ref.at[:, d], pieces.at[d], local_sem.at[0])
+    mine.start()
+    keep = pltpu.make_async_copy(a_ref, wide_ref.at[back], local_sem.at[1])
+    keep.start()
+    blank[...] = jnp.zeros_like(blank)
+    for r in range(back):
+        @pl.when(t < back - r)
+        def _(r=r):
+            fill = pltpu.make_async_copy(blank, wide_ref.at[r], local_sem.at[2])
+            fill.start()
+            fill.wait()
+    mine.wait()
+    for k in range(1, 8):
+        arrived(pieces.at[(d + 8 - k) % 8], swap_recv.at[k - 1])
+    for u in range(own.shape[0]):
+        slot = slot_ref[u]
+        own[u] = pieces[slot // cap, slot % cap]
+
+    def block(g, at, col, c):
+        u0, u1 = groups[g]
+        return w_ref.at[u0:u1, at, col, c]
+
+    def onward(g, k, at, source):
+        side = at * 2 // n_tensor
+        one, two = by_x + (by_y - by_x) * side, by_y + (by_x - by_y) * side
+        here = block(g, at, column, core)
+        send(source, here, xy_send.at[g, k, 0], xy_recv.at[g, k, 0], (one, t))
+        send(source, here, xy_send.at[g, k, 1], xy_recv.at[g, k, 1], (two, t))
+        send(source, here, core_send.at[g, k, 0], core_recv.at[g, k, 0], (sibling, t))
+
+    def columns(at):
+        side = at * 2 // n_tensor
+        col_x, col_y, col_xy = y * 2 + 1 - x, (1 - y) * 2 + x, (1 - y) * 2 + 1 - x
+        return col_x + (col_y - col_x) * side, col_y + (col_x - col_y) * side, col_xy, by_y + (by_x - by_y) * side
+
+    def forward(g, k, at):
+        one, two, both, to = columns(at)
+        got = block(g, at, one, core)
+        arrived(got, xy_recv.at[g, k, 0])
+        send(got, got, xy_send.at[g, k, 2], xy_recv.at[g, k, 2], (to, t))
+        send(got, got, core_send.at[g, k, 1], core_recv.at[g, k, 1], (sibling, t))
+
+    def finish(g, k, at):
+        one, two, both, to = columns(at)
+        for i, col in ((1, two), (2, both)):
+            got = block(g, at, col, core)
+            arrived(got, xy_recv.at[g, k, i])
+            send(got, got, core_send.at[g, k, i + 1], core_recv.at[g, k, i + 1], (sibling, t))
+
+    def done(g, k, at):
+        one, two, both, to = columns(at)
+        cols = (column, one, two, both)
+        for i, col in enumerate(cols):
+            arrived(block(g, at, col, 1 - core), core_recv.at[g, k, i])
+        for i in range(3):
+            arrived(block(g, at, cols[min(i, 1)], core), xy_send.at[g, k, i])
+        for i, col in enumerate(cols):
+            arrived(block(g, at, col, core), core_send.at[g, k, i])
+
+    def z_step(g, s, up):
+        k = 1 + 2 * s + (0 if up else 1)
+        at = t - 1 - s if up else t + 1 + s
+        return k, at, (at >= 0) if up else (at < n_tensor)
+
+    def z_go(g, s, up, at, source):
+        i = 0 if up else 1
+
+        @pl.when(last if up else first)
+        def _():
+            send(source, block(g, at, column, core), z_send.at[g, i, s], z_recv.at[g, i, s], (d, t + 1 if up else t - 1))
+
+    def z_sent(g, s, up, at, have):
+        i = 0 if up else 1
+
+        @pl.when(have & (last if up else first))
+        def _():
+            arrived(block(g, at, column, core), z_send.at[g, i, s])
+
+    n_groups = len(groups)
+    local = []
+    for g, (u0, u1) in enumerate(groups):
+        source = own.at[u0:u1]
+        for up in (True, False):
+            z_go(g, 0, up, t, source)
+        onward(g, 0, t, source)
+        copy = pltpu.make_async_copy(source, block(g, t, column, core), local_sem.at[3 + g])
+        copy.start()
+        local.append(copy)
+
+    @pl.when(first)
+    def _():
+        arrived(wide_ref.at[back - 1], a_recv.at[0])
+    for r in range(1, back):
+        @pl.when(last & (t >= r))
+        def _(r=r):
+            send(wide_ref.at[back - r], wide_ref.at[back - r - 1], a_send.at[r], a_recv.at[r], (d, t + 1))
+
+        if r + 1 <= back:
+            @pl.when(t > r)
+            def _(r=r):
+                arrived(wide_ref.at[back - r - 1], a_recv.at[r])
+
+    for g in range(n_groups):
+        queue = [(0, t, None)]
+        for s in range(n_tensor - 1):
+            for up in (True, False):
+                k, at, have = z_step(g, s, up)
+
+                @pl.when(have)
+                def _(k=k, at=at, s=s, up=up):
+                    got = block(g, at, column, core)
+                    arrived(got, z_recv.at[g, 0 if up else 1, s])
+                    if s + 1 < n_tensor - 1:
+                        z_go(g, s + 1, up, at, got)
+                    onward(g, k, at, got)
+                queue.append((k, at, have))
+            while queue:
+                k, at, have = queue.pop(0)
+                guard = pl.when(have) if have is not None else (lambda f: f())
+                guard(functools.partial(forward, g, k, at))
+                guard(functools.partial(finish, g, k, at))
+
+    for g in range(n_groups):
+        local[g].wait()
+        for k, at, have in [(0, t, None)] + [z_step(g, s, up) for s in range(n_tensor - 1) for up in (True, False)]:
+            guard = pl.when(have) if have is not None else (lambda f: f())
+            guard(functools.partial(done, g, k, at))
+        for up in (True, False):
+            z_sent(g, 0, up, t, t >= 0)
+            for s in range(n_tensor - 2):
+                k, at, have = z_step(g, s, up)
+                z_sent(g, s + 1, up, at, have)
+    keep.wait()
+    for k in range(1, n_tensor):
+        arrived(biases_ref.at[(t + n_tensor - k) % n_tensor], bias_recv.at[k - 1])
+        arrived(bias_ref, bias_send.at[k - 1])
+    for k in range(1, 8):
+        arrived(pieces.at[0], swap_send.at[k - 1])
+    for r in range(back):
+        @pl.when(last & (t >= r))
+        def _(r=r):
+            arrived(a_ref, a_send.at[r])
+
+
+def unit_groups(n_units):
+    half = (n_units - 4) // 2
+    return ((0, 4), (4, 4 + half), (4 + half, n_units))
+
+
+def spread(master_low, normed_low, bias_row, slot_of_unit, n_tensor, back, groups):
+    cap, unit_rows, width = master_low.shape
+    n_units = slot_of_unit.shape[0]
+    piece = unit_rows // 8
+    n_groups, slots = len(groups), 2 * n_tensor - 1
+    rows = normed_low.shape[0]
+    bias_row = bias_row.reshape(-1, 128)
+    any_spec = pl.BlockSpec(memory_space=pl.ANY)
+    vmem = pl.BlockSpec(memory_space=pltpu.VMEM)
+    dma = pltpu.SemaphoreType.DMA
+    w, wide, biases = pl.pallas_call(
+        functools.partial(spread_kernel, groups, n_tensor, back),
+        out_shape=[
+            jax.ShapeDtypeStruct((n_units, n_tensor, 4, 2, piece, width), BF),
+            jax.ShapeDtypeStruct((back + 1, rows, width), BF),
+            jax.ShapeDtypeStruct((n_tensor, *bias_row.shape), F32),
+        ],
+        in_specs=[pl.BlockSpec(memory_space=pltpu.SMEM), any_spec, any_spec, vmem],
+        out_specs=[any_spec, any_spec, vmem],
+        scratch_shapes=[
+            pltpu.VMEM((8, cap, piece, width), BF),
+            pltpu.VMEM((n_units, piece, width), BF),
+            pltpu.VMEM((rows, width), BF),
+            dma((7,)), dma((7,)), dma((3 + n_groups,)), dma((back,)), dma((back,)),
+            dma((n_tensor - 1,)), dma((n_tensor - 1,)),
+            dma((n_groups, 2, n_tensor - 1)), dma((n_groups, 2, n_tensor - 1)),
+            dma((n_groups, slots, 3)), dma((n_groups, slots, 3)),
+            dma((n_groups, slots, 4)), dma((n_groups, slots, 4)),
+        ],
+        compiler_params=pltpu.CompilerParams(collective_id=0, has_side_effects=True, vmem_limit_bytes=24 << 20),
+        name="spread",
+    )(slot_of_unit, master_low.reshape(cap, 8, piece, width), normed_low, bias_row)
+    return w.reshape(n_units, -1, width), wide.reshape(-1, width), biases.reshape(n_tensor, -1)
+
+
+def add_block(into, part, count):
+    def body(i, _):
+        a, b = into(i), part(i)
+        a[...] = a[...] + b[...]
+        return 0
+    lax.fori_loop(0, count, body, 0)
+
+
+def join(row, a, b):
+    return jnp.where(row == MAX_ROW, jnp.maximum(a, b), a + b)
+
+
+def reduce_kernel(
+    groups, n_tensor,
+    unit_ref, g_ref, v_ref, out_ref, vsum_ref,
+    half, other, plane_one, plane_two, up_in, down_in, final, outgo, v_in, v_z,
+    load_sem, core_send, core_recv, one_send, one_recv, two_send, two_recv, z_send, z_recv,
+    swap_send, swap_recv, v_send, v_recv, local_sem,
+):
+    d, t, core, x, y = place()
+    by_x, by_y = d + 2 - 4 * x, d + 4 - 8 * y
+    sibling = d + 1 - 2 * core
+    greet(d, t, n_tensor)
+    n_groups = len(groups)
+    ends = lambda g: (groups[g][0], groups[g][1] - groups[g][0])
+    order = sorted(range(n_tensor), key=lambda a: -abs(2 * a - n_tensor + 1))
+
+    loads = {}
+    for g in range(n_groups):
+        u0, n = ends(g)
+        us = pl.ds(u0, n)
+        send(g_ref.at[us, :, :, :, 1 - core], other.at[us], core_send.at[g], core_recv.at[g], (sibling, t))
+        loads[g] = pltpu.make_async_copy(g_ref.at[us, :, :, :, core], half.at[us], load_sem.at[g])
+        loads[g].start()
+
+    row = lax.broadcasted_iota(jnp.int32, v_ref.shape, 0)
+    vsum_ref[...] = v_ref[...]
+    for i, to in enumerate((sibling, by_x, by_y)):
+        send(vsum_ref, v_in.at[i], v_send.at[i], v_recv.at[i], (to, t))
+        arrived(v_in.at[i], v_recv.at[i])
+        arrived(v_in.at[i], v_send.at[i])
+        vsum_ref[...] = join(row, vsum_ref[...], v_in[i])
+    for k in range(1, n_tensor):
+        to = (t + k) % n_tensor
+        send(vsum_ref, v_z.at[k - 1], v_send.at[2 + k], v_recv.at[2 + k], (d, to))
+
+    def merge(g, at):
+        u0, n = ends(g)
+        lead = half.shape[2] * half.shape[3]
+        def pick(ref):
+            return lambda i: ref.at[u0 + i // lead, at, (i % lead) // 2, i % 2]
+        add_block(pick(half), pick(other), n * lead)
+
+    def first_hop(g, at):
+        u0, n = ends(g)
+        us = pl.ds(u0, n)
+        by_rows = at * 2 < n_tensor
+        source = half.at[us, at, 1 - y] if by_rows else half.at[us, at, :, 1 - x]
+        send(source, plane_one.at[us, at], one_send.at[g, at], one_recv.at[g, at], (by_y if by_rows else by_x, t))
+
+    def second_hop(g, at):
+        u0, n = ends(g)
+        us = pl.ds(u0, n)
+        by_rows = at * 2 < n_tensor
+        arrived(plane_one.at[us, at], one_recv.at[g, at])
+        if by_rows:
+            into = lambda i: half.at[u0 + i // 2, at, y, i % 2]
+        else:
+            into = lambda i: half.at[u0 + i // 2, at, i % 2, x]
+        add_block(into, lambda i: plane_one.at[u0 + i // 2, at, i % 2], 2 * n)
+        source = half.at[us, at, y, 1 - x] if by_rows else half.at[us, at, 1 - y, x]
+        send(source, plane_two.at[us, at], two_send.at[g, at], two_recv.at[g, at], (by_x if by_rows else by_y, t))
+
+    def line(g, at):
+        u0, n = ends(g)
+        us = pl.ds(u0, n)
+        arrived(plane_two.at[us, at], two_recv.at[g, at])
+        mine = lambda i: half.at[u0 + i, at, y, x]
+        add_block(mine, lambda i: plane_two.at[u0 + i, at], n)
+
+        def take(buffer, way):
+            arrived(buffer.at[us, at], z_recv.at[g, at, way])
+            add_block(mine, lambda i: buffer.at[u0 + i, at], n)
+
+        @pl.when((t <= at) & (t > 0))
+        def _():
+            take(up_in, 0)
+
+        @pl.when((t >= at) & (t < n_tensor - 1))
+        def _():
+            take(down_in, 1)
+
+        source = half.at[us, at, y, x]
+
+        @pl.when(t < at)
+        def _():
+            send(source, up_in.at[us, at], z_send.at[g, at], z_recv.at[g, at, 0], (d, t + 1))
+
+        @pl.when(t > at)
+        def _():
+            send(source, down_in.at[us, at], z_send.at[g, at], z_recv.at[g, at, 1], (d, t - 1))
+
+        @pl.when(t == at)
+        def _():
+            add_block(lambda i: final.at[u0 + i], lambda i: half.at[u0 + i, at, y, x], n)
+
+    final[...] = jnp.zeros_like(final)
+    for g in range(n_groups):
+        u0, n = ends(g)
+        loads[g].wait()
+        arrived(other.at[pl.ds(u0, n)], core_recv.at[g])
+        for at in order:
+            merge(g, at)
+            first_hop(g, at)
+        if g == 0:
+            for k in range(1, n_tensor):
+                arrived(v_z.at[k - 1], v_recv.at[2 + k])
+                arrived(v_z.at[k - 1], v_send.at[2 + k])
+            for k in range(1, n_tensor):
+                vsum_ref[...] = join(row, vsum_ref[...], v_z[k - 1])
+        if g > 0:
+            for at in order:
+                line(g - 1, at)
+        for at in order:
+            second_hop(g, at)
+    for at in order:
+        line(n_groups - 1, at)
+
+    cap = out_ref.shape[0]
+    for k in range(1, 9):
+        to = (d + k) % 8
+        for j in range(cap):
+            outgo[to, j] = final[unit_ref[to * cap + j]]
+        if k < 8:
+            send(outgo.at[to], out_ref.at[:, d], swap_send.at[k - 1], swap_recv.at[k - 1], (to, t))
+    keep = pltpu.make_async_copy(outgo.at[d], out_ref.at[:, d], local_sem.at[0])
+    keep.start()
+    for k in range(1, 8):
+        arrived(out_ref.at[:, (d + 8 - k) % 8], swap_recv.at[k - 1])
+    for g in range(n_groups):
+        us = pl.ds(*ends(g))
+        arrived(other.at[us], core_send.at[g])
+        for at in range(n_tensor):
+            arrived(plane_one.at[us, at], one_send.at[g, at])
+            arrived(plane_two.at[us, at], two_send.at[g, at])
+
+            @pl.when(t != at)
+            def _():
+                arrived(up_in.at[us, at], z_send.at[g, at])
+    for k in range(1, 8):
+        arrived(outgo.at[0], swap_send.at[k - 1])
+    keep.wait()
+
+
+def reduce_units(grads, vectors, unit_of_slot, n_tensor, cap, groups):
+    n_units, _, width = grads.shape
+    piece = grads.shape[1] // (8 * n_tensor)
+    grads = grads.reshape(n_units, n_tensor, 2, 2, 2, piece, width)
+    n_groups = len(groups)
+    any_spec = pl.BlockSpec(memory_space=pl.ANY)
+    vmem = pl.BlockSpec(memory_space=pltpu.VMEM)
+    dma = pltpu.SemaphoreType.DMA
+    block = (piece, width)
+    out, vsum = pl.pallas_call(
+        functools.partial(reduce_kernel, groups, n_tensor),
+        out_shape=[
+            jax.ShapeDtypeStruct((cap, 8, *block), BF),
+            jax.ShapeDtypeStruct(vectors.shape, F32),
+        ],
+        in_specs=[pl.BlockSpec(memory_space=pltpu.SMEM), any_spec, vmem],
+        out_specs=[vmem, vmem],
+        scratch_shapes=[
+            pltpu.VMEM((n_units, n_tensor, 2, 2, *block), BF),
+            pltpu.VMEM((n_units, n_tensor, 2, 2, *block), BF),
+            pltpu.VMEM((n_units, n_tensor, 2, *block), BF),
+            pltpu.VMEM((n_units, n_tensor, *block), BF),
+            pltpu.VMEM((n_units, n_tensor, *block), BF),
+            pltpu.VMEM((n_units, n_tensor, *block), BF),
+            pltpu.VMEM((n_units, *block), BF),
+            pltpu.VMEM((8, cap, *block), BF),
+            pltpu.VMEM((3, *vectors.shape), F32),
+            pltpu.VMEM((n_tensor - 1, *vectors.shape), F32),
+            dma((n_groups,)), dma((n_groups,)), dma((n_groups,)),
+            dma((n_groups, n_tensor)), dma((n_groups, n_tensor)),
+            dma((n_groups, n_tensor)), dma((n_groups, n_tensor)),
+            dma((n_groups, n_tensor)), dma((n_groups, n_tensor, 2)),
+            dma((7,)), dma((7,)), dma((2 + n_tensor,)), dma((2 + n_tensor,)), dma((1,)),
+        ],
+        compiler_params=pltpu.CompilerParams(collective_id=1, has_side_effects=True, vmem_limit_bytes=56 << 20),
+        name="reduce_units",
+    )(unit_of_slot, grads, vectors)
+    return out.reshape(cap, -1, width), vsum
+
+
 def per_device(
     tokens_in,
     out_grad,
@@ -269,16 +701,7 @@
     ff_rows = (n_units * unit_rows - 4 * head_rows) // 2
     slot_of_unit, unit_of_slot, occupied = slot_tables(owners, n_slots, slot_cap)
 
-    units = gather_units(matrix_master[0], slot_of_unit)
-    stacks = units.reshape(n_tensor, n_units * unit_rows, width)
-    part = lambda first, count: stacks[:, first : first + count].reshape(-1, width)
-    w_q, w_k, w_v, w_out = (part(i * head_rows, head_rows) for i in range(4))
-    w_fc = part(4 * head_rows, ff_rows)
-    w_proj = part(4 * head_rows + ff_rows, ff_rows)
-    all_bias = lax.all_gather(bias_params[0], "tensor", axis=0, tiled=True)
-    bias = lambda first, count: all_bias[:, first : first + count].reshape(-1)
-    b_q, b_k, b_v = (bias(i * head_rows, head_rows) for i in range(3))
-    b_fc = bias(3 * head_rows, ff_rows)
+    own_kernels = n_data == 8 and head_rows == unit_rows and unit_rows % 128 == 0 and n_tensor > 1
 
     back = -(-(DOC_MOST - 1) // rows_here)
     reach = back * rows_here
@@ -293,12 +716,30 @@
     inputs_f32 = tokens_in.astype(F32)
     normed_one, hat_one, inverse_one = norm_rows(inputs_f32, shared[0], shared[1])
     normed_low = normed_one.astype(BF)
-    before = [
-        lax.ppermute(normed_low, "tensor", [(i, i + r) for i in range(n_tensor - r)])
-        for r in range(min(back, n_tensor - 1), 0, -1)
-    ]
-    blank = [jnp.zeros_like(normed_low)] * (back - len(before))
-    normed_all = jnp.concatenate([*blank, *before, normed_low], axis=0)
+    if own_kernels:
+        units, normed_all, all_bias = spread(
+            matrix_master[0].astype(BF), normed_low, bias_params[0, 0], slot_of_unit, n_tensor, back, unit_groups(n_units)
+        )
+        w_q, w_k, w_v, w_out = (units[i] for i in range(4))
+        w_fc, w_proj = (units[4 + i * (n_units - 4) // 2 :][: (n_units - 4) // 2].reshape(-1, width) for i in range(2))
+    else:
+        units = gather_units(matrix_master[0], slot_of_unit)
+        stacks = units.reshape(n_tensor, n_units * unit_rows, width)
+        part = lambda first, count: stacks[:, first : first + count].reshape(-1, width)
+        w_q, w_k, w_v, w_out = (part(i * head_rows, head_rows) for i in range(4))
+        w_fc = part(4 * head_rows, ff_rows)
+        w_proj = part(4 * head_rows + ff_rows, ff_rows)
+        all_bias = lax.all_gather(bias_params[0], "tensor", axis=0, tiled=True).reshape(n_tensor, -1)
+        before = [
+            lax.ppermute(normed_low, "tensor", [(i, i + r) for i in range(n_tensor - r)])
+            for r in range(min(back, n_tensor - 1), 0, -1)
+        ]
+        blank = [jnp.zeros_like(normed_low)] * (back - len(before))
+        normed_all = jnp.concatenate([*blank, *before, normed_low], axis=0)
+    bias = lambda first, count: all_bias[:, first : first + count].reshape(-1)
+    b_q, b_k, b_v = (bias(i * head_rows, head_rows) for i in range(3))
+    swap = (lambda v: v.swapaxes(0, 1)) if own_kernels else (lambda v: v)
+    b_fc = swap(all_bias[:, 3 * head_rows :].reshape(n_tensor, -1, unit_rows)).reshape(-1)
     scale = 1.0 / math.sqrt(HD)
     q_scaled = (rows_by_rows(normed_low, w_q) + b_q).astype(BF) * jnp.asarray(scale, BF)
     keys_in = (rows_by_rows(normed_all, w_k) + b_k).astype(BF)
@@ -336,8 +777,7 @@
         grad_first += lax.ppermute(away, "tensor", [(i, i - r) for i in range(r, n_tensor)]).astype(F32)
     input_grad = grad_hidden + norm_back(grad_first, hat_one, inverse_one, shared[0])
 
-    head_all = lax.pmax(jnp.max(peaks, axis=2).reshape(-1), ("dp", "tensor"))
-    head_peak = lax.dynamic_slice_in_dim(head_all, tensor_index * heads_here, heads_here)
+    head_here = jnp.max(peaks, axis=2).reshape(-1)
     grad_qkv_b = [jnp.sum(g, axis=0, dtype=F32) for g in (grad_q, grad_k, grad_v)]
     shared_part = jnp.stack(
         [
@@ -350,15 +790,32 @@
         ]
     )
     by_tensor = lambda v: v.reshape(n_tensor, -1)
+    fc_shape = (-1, n_tensor, unit_rows) if own_kernels else (n_tensor, -1, unit_rows)
+    grad_fc_b = swap(grad_fc_b.reshape(fc_shape))
     bias_part = jnp.concatenate([by_tensor(v) for v in (*grad_qkv_b, grad_fc_b)], axis=1)
-    shared_grad, bias_total = lax.psum((shared_part, bias_part), ("dp", "tensor"))
+    if own_kernels:
+        head_row = jnp.pad(head_here, (0, width - head_here.shape[0]))[None]
+        vectors = jnp.concatenate([shared_part, bias_part.reshape(-1, width), head_row], axis=0)
+        vectors = jnp.pad(vectors, ((0, 16 - vectors.shape[0]), (0, 0)))
+        grad_units = jnp.concatenate(
+            [g.astype(BF) for g in (grad_q_w, grad_k_w, grad_v_w, grad_out_w, grad_fc_w, grad_proj_w)], axis=0
+        ).reshape(units.shape)
+        my_grads, totals = reduce_units(
+            grad_units, vectors, unit_of_slot, n_tensor, slot_cap, unit_groups(n_units)[::-1]
+        )
+        my_grads = my_grads.astype(F32)
+        shared_grad, bias_total = totals[:6], totals[6:MAX_ROW].reshape(n_tensor, -1)
+        head_all = totals[MAX_ROW, : head_here.shape[0]]
+    else:
+        head_all = lax.pmax(head_here, ("dp", "tensor"))
+        shared_grad, bias_total = lax.psum((shared_part, bias_part), ("dp", "tensor"))
+        by_stack = lambda g: g.astype(BF).reshape(n_tensor, -1, width)
+        grad_units = jnp.concatenate(
+            [by_stack(g) for g in (grad_q_w, grad_k_w, grad_v_w, grad_out_w, grad_fc_w, grad_proj_w)], axis=1
+        ).reshape(units.shape)
+        my_grads = scatter_units(grad_units, unit_of_slot).astype(F32)
+    head_peak = lax.dynamic_slice_in_dim(head_all, tensor_index * heads_here, heads_here)
     bias_grad = lax.dynamic_index_in_dim(bias_total, tensor_index, 0, keepdims=False)
-
-    by_stack = lambda g: g.astype(BF).reshape(n_tensor, -1, width)
-    grad_units = jnp.concatenate(
-        [by_stack(g) for g in (grad_q_w, grad_k_w, grad_v_w, grad_out_w, grad_fc_w, grad_proj_w)], axis=1
-    ).reshape(units.shape)
-    my_grads = scatter_units(grad_units, unit_of_slot).astype(F32)
 
     my_units = lax.dynamic_slice_in_dim(unit_of_slot, data_index * slot_cap, slot_cap, 0)
     my_occupied = lax.dynamic_slice_in_dim(occupied, data_index * slot_cap, slot_cap, 0)[:, None, None]

time: 905 us -> 673 us (0.74)
  Pallas kernels: 112 us -> 456 us
  blocking collectives: 300 us -> 0 us
  waiting for transfers between devices: 274 us -> 19.2 us
  between operations: 15.1 us -> 1.64 us
  local copies, waits for them, and re-layouts: 48.1 us -> 37.3 us
    pallas_call x2, Pallas kernels: 48.6 us -> 393 us  [the longest x1 220 us: reduce_units(): pl.pallas_call(functools.partial(reduce_kernel, groups, n_tensor), out_sh...]
    all_gather x1 -> x0, blocking collectives: 134 us -> none  [per_device(): all_bias = lax.all_gather(bias_params[0], 'tensor', axis=0, tiled=True)]
    reduce_scatter x1 -> x0, waiting for transfers between devices: 115 us -> none  [scatter_units(): lax.psum_scatter(slots, ('tensor', 'dp'), scatter_dimension=0, tiled=True)]
    psum x1 -> x0, blocking collectives: 107 us -> none  [per_device(): lax.psum((shared_part, bias_part), ('dp', 'tensor'))]
    all_gather x1 -> x0, waiting for transfers between devices: 103 us -> none  [gather_units(): lax.all_gather(master.astype(BF), ('tensor', 'dp'), axis=0, tiled=True)]
    pmax x1 -> x0, blocking collectives: 59.8 us -> none  [per_device(): head_all = lax.pmax(jnp.max(peaks, axis=2).reshape(-1), ('dp', 'tensor'))]
    ppermute x2, waiting for transfers between devices: 56 us -> 19.2 us  [per_device(): lax.ppermute(away, 'tensor', [(i, i - r) for i in range(r, n_tensor)])]
    unnamed x83 -> x77, local copies, waits for them, and re-layouts: 25.6 us -> 11.4 us
  transfers between devices with their start and end apart: 6 -> 2, of which waited for: 4 -> 1; matrix products, arithmetic and copies ran while one was open for 6% -> 8% of each run, Pallas kernels for 2% -> 0%
where the time goes in v2:
time: 673 us; the launch traced here: 665 us
  Pallas kernels  456 us (68%)
  matrix products  117 us (17%)
  local copies, waits for them, and re-layouts  37.3 us (6%)
  other arithmetic  20.8 us (3%)
  waiting for transfers between devices  19.2 us (3%)
  starting transfers between devices  12.8 us (2%)
    pallas_call x1, Pallas kernels, reduce_units(): pl.pallas_call(functools.partial(reduce_kernel, groups, n_tensor), out_sh...  220 us
    pallas_call x1, Pallas kernels, spread(): pl.pallas_call(functools.partial(spread_kernel, groups, n_tensor, back),...  173 us
    dot_general x6, matrix products, rows_by_rows(): lax.dot_general(left, right, (((1,), (1,)), ((), ())), preferred_element_...  39.9 us
    dot_general x6, matrix products, plain_dot(): return jnp.dot(left, right, preferred_element_type=F32)  39.9 us
    dot_general x6, matrix products, cols_by_cols(): lax.dot_general(left, right, (((0,), (0,)), ((), ())), preferred_element_...  37.6 us
    pallas_call x1, Pallas kernels, attend_forward(): pl.pallas_call(attend_kernel, grid=(pairs,), in_specs=[pl.BlockSpec((1, n...  31.6 us
    pallas_call x1, Pallas kernels, attend_backward(): pl.pallas_call(functools.partial(attend_back_kernel, scale=1.0 / math.sqr...  30.8 us
    ppermute x2, waiting for transfers between devices, per_device(): lax.ppermute(away, 'tensor', [(i, i - r) for i in range(r, n_tensor)])  19.2 us
  transfers between devices with their start and end apart: 2, of which 1 were waited for; matrix products, arithmetic and copies ran while one was open for 8% of the time, Pallas kernels for 0%

profile of v2, /device:TPU:9, one launch (start us, length us, event | category | flops | bytes accessed | tf_op | source)
XLA Modules:
  0.0 664.9 jit_solution(4346815374641905376)
XLA Ops:
  2.3 1.4 convert_reduce_fusion.3
  3.8 1.7 fusion.23
  8.0 173.1 %spread.1 = (bf16[12,4,4,2,32,1024]{5,4,3,2,1,0:T(8,128)(2,1)S(1)}, bf16[3,512,1024]{2,1,0:T(8,128)(2,1)S(1)}, f32[4,14,128]{2,1,0:T(8,128)S(1)}) custom-call(s32[12]{0:T(128)S(1)} %multiply_add_fusion.slot_ref, bf16[2,8,32,1024]{3,2,1,0:T(8,128)(2,1)S(1)} %bitcast.132, bf16[512,1024]{1,0:T(8,128)(2,1)S(1)} %fusion.17.a_ref, f32[14,128]{1,0:T(8,128)S(1)} %bitcast.133), custom_call_target="tpu_custom_call" | custom-call | tf_op jit(solution)/shard_map/spread/pallas_call | solution.py:460
  181.1 8.3 %copy-done = bf16[12,4,4,2,32,1024]{5,4,3,2,1,0:T(8,128)(2,1)} copy-done((bf16[12,4,4,2,32,1024]{5,4,3,2,1,0:T(8,128)(2,1)}, bf16[12,4,4,2,32,1024]{5,4,3,2,1,0:T(8,128)(2,1)S(1)}, u32[]{:S(2)}) %copy-start) | copy-done | bytes 25165848
  189.4 7.2 %fusion.47 = (bf16[1,4,4,2,32,1024]{5,4,3,2,1,0:T(8,128)(2,1)}, bf16[1,4,4,2,32,1024]{5,4,3,2,1,0:T(8,128)(2,1)}, bf16[1,4,4,2,32,1024]{5,4,3,2,1,0:T(8,128)(2,1)}, bf16[1,4,4,2,32,1024]{5,4,3,2,1,0:T(8,128)(2,1)}) fusion(bf16[12,4,4,2,32,1024]{5,4,3,2,1,0:T(8,128)(2,1)} %copy-done), kind=kLoop, calls=%fused_computation.137 | loop fusion | bytes 16777216 | tf_op jit(solution)/shard_map/slice | solution.py:723
  196.6 12.3 %fusion.46 = (bf16[4,4,4,2,32,1024]{5,4,3,2,1,0:T(8,128)(2,1)}, bf16[4,4,4,2,32,1024]{5,4,3,2,1,0:T(8,128)(2,1)}) fusion(bf16[12,4,4,2,32,1024]{5,4,3,2,1,0:T(8,128)(2,1)} %copy-done), kind=kLoop, calls=%fused_computation.136 | loop fusion | bytes 33554432 | tf_op jit(solution)/shard_map/slice | solution.py:724
  209.2 3.0 fusion.28.q_ref
  212.4 5.0 add_convert_fusion.v_ref
  217.4 3.8 add_convert_fusion.1.k_ref
  221.1 31.6 %attend_forward.1 = (bf16[512,1024]{1,0:T(8,128)(2,1)S(1)}, f32[8,2,512]{2,1,0:T(2,128)S(1)}, f32[8,2,512]{2,1,0:T(2,128)S(1)}) custom-call(s32[1,512]{1,0:T(1,128)S(1)} %bitcast.135, bf16[512,1024]{1,0:T(8,128)(2,1)S(1)} %fusion.28.q_ref, bf16[1536,1024]{1,0:T(8,128)(2,1)S(1)} %add_convert_fusion.1.k_ref, bf16[1536,1024]{1,0:T(8,128)(2,1)} %add_convert_fusion.v_ref), custom_call_target="tpu_custom_call" | custom-call | tf_op jit(solution)/shard_map/attend_forward/pallas_call | solution.py:127
  252.8 3.0 fusion.50
  257.0 10.6 %fusion.52 = f32[4096,512]{0,1:T(8,128)} fusion(bf16[4096,1024]{1,0:T(8,128)(2,1)} %bitcast.141, bf16[512,1024]{1,0:T(8,128)(2,1)S(1)} %copy-done.20), kind=kOutput, calls=%fused_computation.142 | convolution fusion | flops 4294967296 | bytes 17825792 | tf_op jit(solution)/shard_map/dot_general | solution.py:35
  267.7 16.3 %convert_reduce_fusion = (f32[4096]{0:T(1024)S(1)}, bf16[512,4096]{1,0:T(8,128)(2,1)}, f32[512,4096]{1,0:T(8,128)}) fusion(f32[4096]{0:T(1024)S(1)} %bitcast.171, f32[4096,512]{0,1:T(8,128)} %fusion.52, bf16[4096,1024]{1,0:T(8,128)(2,1)} %bitcast.145, f32[512,1024]{1,0:T(8,128)S(1)} %get-tuple-element.119, f32[1024]{0:T(1024)S(1)} %bitcast.177, ...), kind=kOutput, calls=%fused_computation.14 | convolution fusion | flops 4345819136 | bytes 31502336 | tf_op jit(solution)/shard_map/dot_general | solution.py:35
  283.9 8.7 %multiply_reduce_fusion = (f32[1024]{0:T(1024)S(1)}, f32[512]{0:T(512)S(1)}, f32[512]{0:T(512)S(1)}, f32[1024]{0:T(1024)S(1)}, f32[512,1024]{1,0:T(8,128)S(1)}) fusion(f32[512,1024]{1,0:T(8,128)S(1)} %get-tuple-element.119, f32[512]{0:T(512)S(1)} %add_rsqrt_fusion, f32[512]{0:T(512)S(1)} %broadcast_multiply_fusion.4, f32[1024]{0:T(1024)S(1)} %bitcast.166, ...), kind=kOutput, calls=%fused_computation.53 | convolution fusion | flops 4299682816 | bytes 16797696 | tf_op jit(solution)/shard_map/dot_general | solution.py:31
  295.6 30.8 %attend_backward.1 = (bf16[512,1024]{1,0:T(8,128)(2,1)S(1)}, bf16[1536,1024]{1,0:T(8,128)(2,1)}, bf16[1536,1024]{1,0:T(8,128)(2,1)}) custom-call(s32[1,512]{1,0:T(1,128)S(1)} %bitcast.136, bf16[512,1024]{1,0:T(8,128)(2,1)S(1)} %fusion.28.q_ref, bf16[1536,1024]{1,0:T(8,128)(2,1)} %copy-done.1, bf16[1536,1024]{1,0:T(8,128)(2,1)} %add_convert_fusion.v_ref, ...), custom_call_target="tpu_custom_call" | custom-call | tf_op jit(solution)/shard_map/attend_backward/pallas_call | solution.py:187
  326.4 6.2 fusion.53
  332.6 5.3 fusion.51
  337.9 1.5 fusion.48
  339.4 11.5 %collective-permute-start = (bf16[512,1024]{1,0:T(8,128)(2,1)}, bf16[512,1024]{1,0:T(8,128)(2,1)}, u32[]{:S(2)}, u32[]{:S(2)}) collective-permute-start(bf16[512,1024]{1,0:T(8,128)(2,1)} %get-tuple-element.103), channel_id=1, source_target_pairs={{1,0},{2,1},{3,2},{5,4},{6,5},{7,6},{9,8},{10,9},{11,10},{13,12},{... | collective-permute-start | bytes 3145736 | tf_op jit(solution)/shard_map/ppermute | solution.py:777
  352.8 2.6 convert_dynamic-update-slice_fusion.5
  355.5 4.7 convert_dynamic-update-slice_fusion.4
  360.2 4.8 convert_dynamic-update-slice_fusion.3
  365.0 2.6 convert_dynamic-update-slice_fusion.2
  367.6 9.6 %convert_dynamic-update-slice_fusion.1 = bf16[12288,1024]{1,0:T(8,128)(2,1)} fusion(bf16[12288,1024]{1,0:T(8,128)(2,1)} %convert_dynamic-update-slice_fusion.2, bf16[512,4096]{1,0:T(8,128)(2,1)} %get-tuple-element.91, f32[512,1024]{1,0:T(8,128)S(1)} %get-tuple-element.119, f32[1024]{0:T(1024)S(1)} %bitcast.178, f32[1024]{0:T(1024)S(1)} %bitcast.168, ...), kind=kOutput, calls=%fused_computation.16 | convolution fusion | flops 4301783040 | bytes 14692352 | tf_op jit(solution)/shard_map/dot_general | solution.py:39
  377.2 10.4 %add_add_fusion = f32[512,1024]{1,0:T(8,128)} fusion(f32[512,1024]{1,0:T(8,128)S(1)} %get-tuple-element.119, bf16[4096,1024]{1,0:T(8,128)(2,1)S(1)} %bitcast.144, f32[1024]{0:T(1024)S(1)} %bitcast.176, f32[512,4096]{1,0:T(8,128)} %get-tuple-element.120, f32[4096]{0:T(1024)S(1)} %bitcast.172), kind=kOutput, calls=%fused_computation.60 | convolution fusion | flops 4316987392 | bytes 20992000 | tf_op jit(solution)/shard_map/dot_general | solution.py:31
  387.7 13.2 %convert_dynamic-update-slice_fusion = bf16[12288,1024]{1,0:T(8,128)(2,1)} fusion(bf16[12288,1024]{1,0:T(8,128)(2,1)} %convert_dynamic-update-slice_fusion.1, bf16[512,1024]{1,0:T(8,128)(2,1)S(1)} %copy-done.21, f32[512,4096]{1,0:T(8,128)} %get-tuple-element.120, f32[4096]{0:T(1024)S(1)} %bitcast.173), kind=kOutput, calls=%fused_computation.15 | convolution fusion | flops 4320133120 | bytes 17842176 | tf_op jit(solution)/shard_map/dot_general | solution.py:39
  402.5 19.2 %collective-permute-done.1 = bf16[512,1024]{1,0:T(8,128)(2,1)} collective-permute-done((bf16[512,1024]{1,0:T(8,128)(2,1)}, bf16[512,1024]{1,0:T(8,128)(2,1)}, u32[]{:S(2)}, u32[]{:S(2)}) %collective-permute-start.1) | collective-permute-done | bytes 1048608 | tf_op jit(solution)/shard_map/ppermute | solution.py:777
  421.7 6.3 fusion.22
  428.8 220.1 %reduce_units.1 = (bf16[2,8,32,1024]{3,2,1,0:T(8,128)(2,1)}, f32[16,1024]{1,0:T(8,128)}) custom-call(s32[16]{0:T(128)} %copy-done.31, bf16[12,4,2,2,2,32,1024]{6,5,4,3,2,1,0:T(8,128)(2,1)} %bitcast.19.g_ref, f32[16,1024]{1,0:T(8,128)} %pad.9.v_ref), custom_call_target="tpu_custom_call" | custom-call | tf_op jit(solution)/shard_map/reduce_units/pallas_call | solution.py:648
  650.5 1.4 bitcast_subtract_fusion
  654.6 3.8 fusion.21
  659.1 5.3 multiply_select_fusion
  (129 shorter events, 17.7 us)
Async XLA Ops:
  0.6 6.6 copy-start.7
  2.3 5.6 copy-start.2
  3.8 3.7 copy-start.27
  3.8 3.7 copy-start.6
  181.1 8.3 %copy-start = (bf16[12,4,4,2,32,1024]{5,4,3,2,1,0:T(8,128)(2,1)}, bf16[12,4,4,2,32,1024]{5,4,3,2,1,0:T(8,128)(2,1)S(1)}, u32[]{:S(2)}) copy-start(bf16[12,4,4,2,32,1024]{5,4,3,2,1,0:T(8,128)(2,1)S(1)} %get-tuple-element.24) | copy-start | bytes 75497472
  189.4 7.2 %copy-start.4 = (bf16[3,512,1024]{2,1,0:T(8,128)(2,1)}, bf16[3,512,1024]{2,1,0:T(8,128)(2,1)S(1)}, u32[]{:S(2)}) copy-start(bf16[3,512,1024]{2,1,0:T(8,128)(2,1)S(1)} %get-tuple-element.26) | copy-start | bytes 9437188
  196.6 12.3 %copy-start.32 = (s32[1,4]{1,0:T(1,128)S(1)}, s32[1,4]{1,0:T(1,128)}, u32[]{:S(2)}) copy-start(s32[1,4]{1,0:T(1,128)} %param.11) | copy-start | bytes 52
  209.2 3.1 copy-start.5
  209.2 3.2 copy-start.16
  212.4 5.0 copy-start.18
  221.1 31.7 %copy-start.1 = (bf16[1536,1024]{1,0:T(8,128)(2,1)}, bf16[1536,1024]{1,0:T(8,128)(2,1)S(1)}, u32[]{:S(2)}) copy-start(bf16[1536,1024]{1,0:T(8,128)(2,1)S(1)} %add_convert_fusion.1.k_ref) | copy-start | bytes 9437188
  293.7 71.3 %copy-start.9 = (f32[512,1024]{1,0:T(8,128)}, f32[512,1024]{1,0:T(8,128)S(1)}, u32[]{:S(2)}) copy-start(f32[512,1024]{1,0:T(8,128)S(1)} %get-tuple-element.93) | copy-start | bytes 6291460
  326.4 6.2 copy-start.11
  326.4 6.2 copy-start.17
  337.9 14.3 %copy-start.13 = (bf16[1536,1024]{1,0:T(8,128)(2,1)S(1)}, bf16[1536,1024]{1,0:T(8,128)(2,1)}, u32[]{:S(2)}) copy-start(bf16[1536,1024]{1,0:T(8,128)(2,1)} %get-tuple-element.29) | copy-start | bytes 9437188
  339.4 63.1 %collective-permute-start = (bf16[512,1024]{1,0:T(8,128)(2,1)}, bf16[512,1024]{1,0:T(8,128)(2,1)}, u32[]{:S(2)}, u32[]{:S(2)}) collective-permute-start(bf16[512,1024]{1,0:T(8,128)(2,1)} %get-tuple-element.103), channel_id=1, source_target_pairs={{1,0},{2,1},{3,2},{5,4},{6,5},{7,6},{9,8},{10,9},{11,10},{13,12},{... | collective-permute-start | bytes 3145736 | tf_op jit(solution)/shard_map/ppermute | solution.py:777
  350.9 70.8 %collective-permute-start.1 = (bf16[512,1024]{1,0:T(8,128)(2,1)}, bf16[512,1024]{1,0:T(8,128)(2,1)}, u32[]{:S(2)}, u32[]{:S(2)}) collective-permute-start(bf16[512,1024]{1,0:T(8,128)(2,1)} %get-tuple-element.104), channel_id=1, source_target_pairs={{2,0},{3,1},{6,4},{7,5},{10,8},{11,9},{14,12},{15,13},{18,16},{19,... | collective-permute-start | bytes 3145736 | tf_op jit(solution)/shard_map/ppermute | solution.py:777
  365.0 12.2 %slice-start = ((s8[8388608]{0:T(1024)(128)(4,1)}), s8[4194304]{0:T(1024)(128)(4,1)S(1)}, s32[]{:S(2)}) async-start(s8[8388608]{0:T(1024)(128)(4,1)} %bitcast.142), calls=%async_computation | async-start | bytes 8388608
  367.6 9.6 %slice-start.1 = ((s8[8388608]{0:T(1024)(128)(4,1)}), s8[4194304]{0:T(1024)(128)(4,1)S(1)}, s32[]{:S(2)}) async-start(s8[8388608]{0:T(1024)(128)(4,1)} %bitcast.142), calls=%async_computation.1 | async-start | bytes 8388608
  377.2 10.4 %copy-start.21 = (bf16[512,1024]{1,0:T(8,128)(2,1)S(1)}, bf16[512,1024]{1,0:T(8,128)(2,1)}, u32[]{:S(2)}) copy-start(bf16[512,1024]{1,0:T(8,128)(2,1)} %param.10) | copy-start | bytes 3145732
  387.7 13.2 %copy-start.12 = (bf16[1536,1024]{1,0:T(8,128)(2,1)S(1)}, bf16[1536,1024]{1,0:T(8,128)(2,1)}, u32[]{:S(2)}) copy-start(bf16[1536,1024]{1,0:T(8,128)(2,1)} %get-tuple-element.30) | copy-start | bytes 9437188
  400.9 20.8 %copy-start.26 = (f32[1,1,1024]{2,1,0:T(1,128)S(1)}, f32[1,1,1024]{2,1,0:T(1,128)}, u32[]{:S(2)}) copy-start(f32[1,1,1024]{2,1,0:T(1,128)} %copy-done.25) | copy-start | bytes 12292
  400.9 20.8 %copy-start.28 = (f32[512]{0:T(512)S(1)}, f32[512]{0:T(512)}, u32[]{:S(2)}) copy-start(f32[512]{0:T(512)} %copy-done.27) | copy-start | bytes 6148
  400.9 20.8 %copy-start.30 = (f32[512]{0:T(512)S(1)}, f32[512]{0:T(512)}, u32[]{:S(2)}) copy-start(f32[512]{0:T(512)} %copy-done.29) | copy-start | bytes 6148
  402.3 25.7 %copy-start.31 = (s32[16]{0:T(128)}, s32[16]{0:T(128)S(1)}, u32[]{:S(2)}) copy-start(s32[16]{0:T(128)S(1)} %select_reduce_fusion.1.unit_ref) | copy-start | bytes 196
  428.8 221.7 %copy-start.23 = (f32[3,6,1024]{2,1,0:T(8,128)S(1)}, f32[3,6,1024]{2,1,0:T(8,128)}, u32[]{:S(2)}) copy-start(f32[3,6,1024]{2,1,0:T(8,128)} %param.16) | copy-start | bytes 221188
  428.8 223.9 %copy-start.24 = (f32[3,1,1792]{2,1,0:T(1,128)S(1)}, f32[3,1,1792]{2,1,0:T(1,128)}, u32[]{:S(2)}) copy-start(f32[3,1,1792]{2,1,0:T(1,128)} %param.17) | copy-start | bytes 64516
  428.8 225.8 %copy-start.10 = (f32[512,1024]{1,0:T(8,128)S(1)}, f32[512,1024]{1,0:T(8,128)}, u32[]{:S(2)}) copy-start(f32[512,1024]{1,0:T(8,128)} %copy-done.9) | copy-start | bytes 6291460
  654.6 3.8 copy-start.8
  654.6 3.8 copy-start.14
  654.6 3.8 copy-start.15
  654.6 4.5 copy-start.22
  (5 other events, 7.0 us)

commit v3 on v2

--- a/solution.py
+++ b/solution.py
@@ -252,7 +252,6 @@
         device_id=to, device_id_type=MESH,
     )
     copy.start()
-    return copy
 
 
 def arrived(ref, sem):
@@ -261,8 +260,7 @@
 
 def place():
     d, t = lax.axis_index("dp"), lax.axis_index("tensor")
-    core, x, y = d % 2, (d // 2) % 2, d // 4
-    return d, t, core, x, y
+    return d, t, d % 2, (d // 2) % 2, d // 4
 
 
 def greet(d, t, n_tensor):
@@ -274,212 +272,307 @@
     pl.semaphore_wait(barrier, 6 + n_tensor)
 
 
-def spread_kernel(
-    groups, n_tensor, back,
-    slot_ref, master_ref, a_ref, bias_ref, w_ref, wide_ref, biases_ref,
-    pieces, own, blank, swap_send, swap_recv, local_sem, a_send, a_recv, bias_send, bias_recv,
+def loop_with(count, body, events):
+    per = -(-len(events) // count)
+
+    def step(i, carry):
+        body(i)
+        for n in range(count):
+            mine = events[n * per : (n + 1) * per]
+            if mine:
+                @pl.when(i == n)
+                def _(mine=mine):
+                    for event in mine:
+                        event()
+        return carry
+
+    lax.fori_loop(0, count, step, 0)
+
+
+def attend_pair(i, q_ref, k_ref, v_ref, o_ref, lse_ref, peak_ref, bias_ref):
+    n_keys, n_query = bias_ref.shape
+    size, span = q_tiles(n_query, n_keys)
+    lanes = pl.ds(pl.multiple_of(i * PAIR, PAIR), PAIR)
+    for j in range(n_query // size):
+        rows, keys = pl.ds(j * size, size), pl.ds(j * size, span)
+        v_t = v_ref[keys, lanes].T
+        outs = []
+        for h in range(2):
+            k_h = jnp.where(head_lanes(h), k_ref[keys, lanes], 0)
+            s = rows_by_rows(k_h, q_ref[rows, lanes]) + bias_ref[keys, rows]
+            top = jnp.max(s, axis=0, keepdims=True)
+            p = jnp.exp(s - top)
+            total = jnp.sum(p, axis=0, keepdims=True)
+            o_t = plain_dot(v_t[h * HD : (h + 1) * HD], p.astype(BF))
+            outs.append(o_t / total)
+            lse_ref[i, h : h + 1, rows] = top + jnp.log(total)
+            peak_ref[i, h : h + 1, rows] = top
+        o_ref[rows, lanes] = jnp.concatenate(outs, axis=0).T.astype(BF)
+
+
+def forward_kernel(
+    n_tensor, back, scale,
+    slot_ref, master_ref, a_ref, x_ref, bias_in_ref, first_ref, shared_ref,
+    att_ref, fc_ref, proj_ref, wide_ref, biases_ref, q_ref, k_ref, v_ref, o_ref, lse_ref, peak_ref, hidden_ref,
+    pieces, own, seen_ref, bias_rows, swap_send, swap_recv, local_sem, a_send, a_recv, bias_send, bias_recv,
     z_send, z_recv, xy_send, xy_recv, core_send, core_recv,
 ):
     d, t, core, x, y = place()
     column = y * 2 + x
     by_x, by_y = d + 2 - 4 * x, d + 4 - 8 * y
     sibling = d + 1 - 2 * core
+    first, last = t > 0, t < n_tensor - 1
+    rows_here, width = a_ref.shape
+    weights = (att_ref, fc_ref, proj_ref)
+    starts = [0]
+    for w in weights:
+        starts.append(starts[-1] + w.shape[0])
     greet(d, t, n_tensor)
-    first, last = t > 0, t < n_tensor - 1
-    for k in range(1, n_tensor):
-        send(bias_ref, biases_ref.at[t], bias_send.at[k - 1], bias_recv.at[k - 1], (d, (t + k) % n_tensor))
-    biases_ref[t] = bias_ref[...]
-
-    @pl.when(last)
-    def _():
-        send(a_ref, wide_ref.at[back - 1], a_send.at[0], a_recv.at[0], (d, t + 1))
-
-    cap = master_ref.shape[0]
+
+    def tokens_up(r):
+        @pl.when(last & (t >= r))
+        def _():
+            source = a_ref if r == 0 else wide_ref.at[back - r]
+            send(source, wide_ref.at[back - r - 1], a_send.at[r], a_recv.at[r], (d, t + 1))
+
+    def tokens_in(r):
+        @pl.when(t > r)
+        def _():
+            arrived(wide_ref.at[back - r - 1], a_recv.at[r])
+        if r + 1 < back:
+            tokens_up(r + 1)
+
+    tokens_up(0)
     for k in range(1, 8):
         to = (d + k) % 8
         send(master_ref.at[:, to], pieces.at[d], swap_send.at[k - 1], swap_recv.at[k - 1], (to, t))
     mine = pltpu.make_async_copy(master_ref.at[:, d], pieces.at[d], local_sem.at[0])
     mine.start()
-    keep = pltpu.make_async_copy(a_ref, wide_ref.at[back], local_sem.at[1])
-    keep.start()
-    blank[...] = jnp.zeros_like(blank)
+    for k in range(1, n_tensor):
+        send(bias_in_ref, biases_ref.at[t], bias_send.at[k - 1], bias_recv.at[k - 1], (d, (t + k) % n_tensor))
+    biases_ref[t] = bias_in_ref[...]
+    wide_ref[back] = a_ref[...]
     for r in range(back):
         @pl.when(t < back - r)
         def _(r=r):
-            fill = pltpu.make_async_copy(blank, wide_ref.at[r], local_sem.at[2])
-            fill.start()
-            fill.wait()
+            wide_ref[r] = jnp.zeros((rows_here, width), BF)
+    fill_bias(seen_ref, first_ref)
     mine.wait()
     for k in range(1, 8):
         arrived(pieces.at[(d + 8 - k) % 8], swap_recv.at[k - 1])
+    cap = master_ref.shape[0]
     for u in range(own.shape[0]):
         slot = slot_ref[u]
         own[u] = pieces[slot // cap, slot % cap]
 
     def block(g, at, col, c):
-        u0, u1 = groups[g]
-        return w_ref.at[u0:u1, at, col, c]
-
-    def onward(g, k, at, source):
+        return weights[g].at[:, at, col, c]
+
+    def route(at):
         side = at * 2 // n_tensor
         one, two = by_x + (by_y - by_x) * side, by_y + (by_x - by_y) * side
+        col_x, col_y, col_xy = y * 2 + 1 - x, (1 - y) * 2 + x, (1 - y) * 2 + 1 - x
+        return one, two, col_x + (col_y - col_x) * side, col_y + (col_x - col_y) * side, col_xy
+
+    def onward(g, k, at, source):
+        one, two, _, _, _ = route(at)
         here = block(g, at, column, core)
-        send(source, here, xy_send.at[g, k, 0], xy_recv.at[g, k, 0], (one, t))
-        send(source, here, xy_send.at[g, k, 1], xy_recv.at[g, k, 1], (two, t))
-        send(source, here, core_send.at[g, k, 0], core_recv.at[g, k, 0], (sibling, t))
-
-    def columns(at):
-        side = at * 2 // n_tensor
-        col_x, col_y, col_xy = y * 2 + 1 - x, (1 - y) * 2 + x, (1 - y) * 2 + 1 - x
-        return col_x + (col_y - col_x) * side, col_y + (col_x - col_y) * side, col_xy, by_y + (by_x - by_y) * side
+        send(source, here, xy_send.at[g], xy_recv.at[g, k, 0], (one, t))
+        send(source, here, xy_send.at[g], xy_recv.at[g, k, 1], (two, t))
 
     def forward(g, k, at):
-        one, two, both, to = columns(at)
-        got = block(g, at, one, core)
+        one, two, from_one, _, _ = route(at)
+        got = block(g, at, from_one, core)
         arrived(got, xy_recv.at[g, k, 0])
-        send(got, got, xy_send.at[g, k, 2], xy_recv.at[g, k, 2], (to, t))
-        send(got, got, core_send.at[g, k, 1], core_recv.at[g, k, 1], (sibling, t))
-
-    def finish(g, k, at):
-        one, two, both, to = columns(at)
-        for i, col in ((1, two), (2, both)):
-            got = block(g, at, col, core)
-            arrived(got, xy_recv.at[g, k, i])
-            send(got, got, core_send.at[g, k, i + 1], core_recv.at[g, k, i + 1], (sibling, t))
+        send(got, got, xy_send.at[g], xy_recv.at[g, k, 2], (two, t))
+
+    def settle(g, k, at):
+        _, _, _, from_two, beyond = route(at)
+        arrived(block(g, at, from_two, core), xy_recv.at[g, k, 1])
+        arrived(block(g, at, beyond, core), xy_recv.at[g, k, 2])
+        got = weights[g].at[:, at, :, core]
+        send(got, got, core_send.at[g, k], core_recv.at[g, k], (sibling, t))
 
     def done(g, k, at):
-        one, two, both, to = columns(at)
-        cols = (column, one, two, both)
-        for i, col in enumerate(cols):
-            arrived(block(g, at, col, 1 - core), core_recv.at[g, k, i])
-        for i in range(3):
-            arrived(block(g, at, cols[min(i, 1)], core), xy_send.at[g, k, i])
-        for i, col in enumerate(cols):
-            arrived(block(g, at, col, core), core_send.at[g, k, i])
-
-    def z_step(g, s, up):
-        k = 1 + 2 * s + (0 if up else 1)
-        at = t - 1 - s if up else t + 1 + s
-        return k, at, (at >= 0) if up else (at < n_tensor)
-
-    def z_go(g, s, up, at, source):
+        arrived(weights[g].at[:, at, :, 1 - core], core_recv.at[g, k])
+        arrived(weights[g].at[:, at, :, core], core_send.at[g, k])
+
+    def z_go(g, s, up, source, at):
         i = 0 if up else 1
 
         @pl.when(last if up else first)
         def _():
             send(source, block(g, at, column, core), z_send.at[g, i, s], z_recv.at[g, i, s], (d, t + 1 if up else t - 1))
 
-    def z_sent(g, s, up, at, have):
-        i = 0 if up else 1
-
-        @pl.when(have & (last if up else first))
-        def _():
-            arrived(block(g, at, column, core), z_send.at[g, i, s])
-
-    n_groups = len(groups)
+    def z_step(s, up):
+        at = t - 1 - s if up else t + 1 + s
+        return 1 + 2 * s + (0 if up else 1), at, (at >= 0) if up else (at < n_tensor)
+
+    def z_event(g, s):
+        for up in (True, False):
+            k, at, have = z_step(s, up)
+
+            @pl.when(have)
+            def _(k=k, at=at, up=up):
+                got = block(g, at, column, core)
+                arrived(got, z_recv.at[g, 0 if up else 1, s])
+                if s + 1 < n_tensor - 1:
+                    z_go(g, s + 1, up, got, at)
+                onward(g, k, at, got)
+
+    def each(fn, g, s):
+        if s < 0:
+            fn(g, 0, t)
+        else:
+            for up in (True, False):
+                k, at, have = z_step(s, up)
+                pl.when(have)(functools.partial(fn, g, k, at))
+
+    n_groups, steps = len(weights), n_tensor - 1
     local = []
-    for g, (u0, u1) in enumerate(groups):
-        source = own.at[u0:u1]
+    for g in range(n_groups):
+        source = own.at[starts[g] : starts[g + 1]]
         for up in (True, False):
-            z_go(g, 0, up, t, source)
-        onward(g, 0, t, source)
-        copy = pltpu.make_async_copy(source, block(g, t, column, core), local_sem.at[3 + g])
+            z_go(g, 0, up, source, t)
+        copy = pltpu.make_async_copy(source, block(g, t, column, core), local_sem.at[1 + g])
         copy.start()
         local.append(copy)
-
-    @pl.when(first)
-    def _():
-        arrived(wide_ref.at[back - 1], a_recv.at[0])
-    for r in range(1, back):
-        @pl.when(last & (t >= r))
-        def _(r=r):
-            send(wide_ref.at[back - r], wide_ref.at[back - r - 1], a_send.at[r], a_recv.at[r], (d, t + 1))
-
-        if r + 1 <= back:
-            @pl.when(t > r)
-            def _(r=r):
-                arrived(wide_ref.at[back - r - 1], a_recv.at[r])
-
-    for g in range(n_groups):
-        queue = [(0, t, None)]
-        for s in range(n_tensor - 1):
-            for up in (True, False):
-                k, at, have = z_step(g, s, up)
-
-                @pl.when(have)
-                def _(k=k, at=at, s=s, up=up):
-                    got = block(g, at, column, core)
-                    arrived(got, z_recv.at[g, 0 if up else 1, s])
-                    if s + 1 < n_tensor - 1:
-                        z_go(g, s + 1, up, at, got)
-                    onward(g, k, at, got)
-                queue.append((k, at, have))
-            while queue:
-                k, at, have = queue.pop(0)
-                guard = pl.when(have) if have is not None else (lambda f: f())
-                guard(functools.partial(forward, g, k, at))
-                guard(functools.partial(finish, g, k, at))
-
-    for g in range(n_groups):
-        local[g].wait()
-        for k, at, have in [(0, t, None)] + [z_step(g, s, up) for s in range(n_tensor - 1) for up in (True, False)]:
-            guard = pl.when(have) if have is not None else (lambda f: f())
-            guard(functools.partial(done, g, k, at))
-        for up in (True, False):
-            z_sent(g, 0, up, t, t >= 0)
-            for s in range(n_tensor - 2):
-                k, at, have = z_step(g, s, up)
-                z_sent(g, s + 1, up, at, have)
-    keep.wait()
+        onward(g, 0, t, source)
+
+    def chain(g):
+        events = []
+        for s in range(steps + 2):
+            if s < steps:
+                events.append(functools.partial(z_event, g, s))
+            if s <= steps:
+                events.append(functools.partial(each, forward, g, s - 1))
+            if s >= 1:
+                if s == 1:
+                    events.append(local[g].wait)
+                events.append(functools.partial(each, settle, g, s - 2))
+        return events
+
+    events = chain(0)
+    for r in range(back):
+        events.insert(1 + 4 * r, functools.partial(tokens_in, r))
+    early = [functools.partial(z_event, g, 0) for g in range(1, n_groups)]
+    events[3:3] = early
+    for event in events:
+        event()
+    late = []
+    for g in range(1, n_groups):
+        late += chain(g)[1:]
     for k in range(1, n_tensor):
         arrived(biases_ref.at[(t + n_tensor - k) % n_tensor], bias_recv.at[k - 1])
-        arrived(bias_ref, bias_send.at[k - 1])
-    for k in range(1, 8):
-        arrived(pieces.at[0], swap_send.at[k - 1])
+        arrived(bias_in_ref, bias_send.at[k - 1])
+    per = width // n_tensor // 128
+    for n in range(3):
+        for at in range(n_tensor):
+            for i in range(per):
+                lanes = pl.ds((at * per + i) * 128, 128)
+                bias_rows[n : n + 1, lanes] = biases_ref[at, n * per + i : n * per + i + 1]
+    for s in range(-1, steps):
+        each(done, 0, s)
+
+    tile = 256
+
+    def project(n, source_ref, into_ref, factor):
+        def body(i):
+            cols = pl.ds(pl.multiple_of(i * tile, tile), tile)
+            w = att_ref[n, pl.ds(i * tile // (width // n_tensor), 1)].reshape(tile, width)
+            for r in range(into_ref.shape[0] // rows_here):
+                a = wide_ref[r] if source_ref is None else source_ref[...]
+                full = rows_by_rows(a, w) + bias_rows[n : n + 1, cols]
+                into_ref[r * rows_here : (r + 1) * rows_here, cols] = (full.astype(BF) * jnp.asarray(factor, BF)) if factor else full.astype(BF)
+        return body
+
+    tiles = width // tile
+    n_late = len(late)
+    cut = n_late // 5
+    loop_with(tiles, project(0, a_ref, q_ref, scale), late[:0])
+    loop_with(tiles, project(1, None, k_ref, None), late[:cut])
+    loop_with(tiles, project(2, None, v_ref, None), late[cut : 2 * cut])
+    loop_with(
+        width // PAIR,
+        lambda i: attend_pair(i, q_ref, k_ref, v_ref, o_ref, lse_ref, peak_ref, seen_ref),
+        late[2 * cut :],
+    )
+    w_out = att_ref[3].reshape(width, width)
+    half = rows_here // 2
+    for r in range(2):
+        rows = pl.ds(r * half, half)
+        hidden_ref[rows, :] = x_ref[rows, :].astype(F32) + (plain_dot(o_ref[rows, :], w_out) + shared_ref[2:3, :])
+
+    for g in range(n_groups):
+        if g > 0:
+            for s in range(-1, steps):
+                each(done, g, s)
+        arrived(weights[g].at[:, :, pl.ds(0, 3), 0], xy_send.at[g])
+        for up in (True, False):
+            for s in range(steps):
+                have = last if up else first
+                if s > 0:
+                    have = have & z_step(s - 1, up)[2]
+
+                @pl.when(have)
+                def _(g=g, s=s, up=up):
+                    arrived(block(g, t, column, core), z_send.at[g, 0 if up else 1, s])
     for r in range(back):
         @pl.when(last & (t >= r))
         def _(r=r):
             arrived(a_ref, a_send.at[r])
-
-
-def unit_groups(n_units):
-    half = (n_units - 4) // 2
-    return ((0, 4), (4, 4 + half), (4 + half, n_units))
-
-
-def spread(master_low, normed_low, bias_row, slot_of_unit, n_tensor, back, groups):
+    for k in range(1, 8):
+        arrived(pieces.at[0], swap_send.at[k - 1])
+
+
+def forward_spread(master_low, normed_low, tokens, bias_row, first_seen, shared, slot_of_unit, n_tensor, back):
     cap, unit_rows, width = master_low.shape
     n_units = slot_of_unit.shape[0]
+    n_ff = (n_units - 4) // 2
     piece = unit_rows // 8
-    n_groups, slots = len(groups), 2 * n_tensor - 1
     rows = normed_low.shape[0]
+    n_keys = (back + 1) * rows
     bias_row = bias_row.reshape(-1, 128)
     any_spec = pl.BlockSpec(memory_space=pl.ANY)
     vmem = pl.BlockSpec(memory_space=pltpu.VMEM)
     dma = pltpu.SemaphoreType.DMA
-    w, wide, biases = pl.pallas_call(
-        functools.partial(spread_kernel, groups, n_tensor, back),
+    shape = jax.ShapeDtypeStruct
+    units = lambda n: shape((n, n_tensor, 4, 2, piece, width), BF)
+    stats = shape((width // PAIR, 2, rows), F32)
+    outs = pl.pallas_call(
+        functools.partial(forward_kernel, n_tensor, back, 1.0 / math.sqrt(HD)),
         out_shape=[
-            jax.ShapeDtypeStruct((n_units, n_tensor, 4, 2, piece, width), BF),
-            jax.ShapeDtypeStruct((back + 1, rows, width), BF),
-            jax.ShapeDtypeStruct((n_tensor, *bias_row.shape), F32),
+            units(4), units(n_ff), units(n_ff),
+            shape((back + 1, rows, width), BF), shape((n_tensor, *bias_row.shape), F32),
+            shape((rows, width), BF), shape((n_keys, width), BF), shape((n_keys, width), BF), shape((rows, width), BF),
+            stats, stats, shape((rows, width), F32),
         ],
-        in_specs=[pl.BlockSpec(memory_space=pltpu.SMEM), any_spec, any_spec, vmem],
-        out_specs=[any_spec, any_spec, vmem],
+        in_specs=[pl.BlockSpec(memory_space=pltpu.SMEM), any_spec, vmem, vmem, vmem, vmem, vmem],
+        out_specs=[vmem, any_spec, any_spec, vmem, vmem, vmem, vmem, vmem, vmem, vmem, vmem, vmem],
         scratch_shapes=[
             pltpu.VMEM((8, cap, piece, width), BF),
             pltpu.VMEM((n_units, piece, width), BF),
-            pltpu.VMEM((rows, width), BF),
-            dma((7,)), dma((7,)), dma((3 + n_groups,)), dma((back,)), dma((back,)),
+            pltpu.VMEM((n_keys, rows), F32),
+            pltpu.VMEM((3, width), F32),
+            dma((7,)), dma((7,)), dma((4,)), dma((back,)), dma((back,)),
             dma((n_tensor - 1,)), dma((n_tensor - 1,)),
-            dma((n_groups, 2, n_tensor - 1)), dma((n_groups, 2, n_tensor - 1)),
-            dma((n_groups, slots, 3)), dma((n_groups, slots, 3)),
-            dma((n_groups, slots, 4)), dma((n_groups, slots, 4)),
+            dma((3, 2, n_tensor - 1)), dma((3, 2, n_tensor - 1)),
+            dma((3,)), dma((3, 2 * n_tensor - 1, 3)),
+            dma((3, 2 * n_tensor - 1)), dma((3, 2 * n_tensor - 1)),
         ],
-        compiler_params=pltpu.CompilerParams(collective_id=0, has_side_effects=True, vmem_limit_bytes=24 << 20),
-        name="spread",
-    )(slot_of_unit, master_low.reshape(cap, 8, piece, width), normed_low, bias_row)
-    return w.reshape(n_units, -1, width), wide.reshape(-1, width), biases.reshape(n_tensor, -1)
+        compiler_params=pltpu.CompilerParams(collective_id=0, has_side_effects=True, vmem_limit_bytes=56 << 20),
+        name="forward_spread",
+    )(slot_of_unit, master_low.reshape(cap, 8, piece, width), normed_low, tokens, bias_row, first_seen, shared)
+    att, fc, proj, wide, biases, q, k, v, o, lse, peaks, hidden = outs
+    return (
+        att.reshape(4, -1, width), fc.reshape(-1, width), proj.reshape(-1, width), wide.reshape(-1, width),
+        biases.reshape(n_tensor, -1), q, k, v, o, lse, peaks, hidden,
+    )
+
+
+def unit_groups(n_units):
+    half = (n_units - 4) // 2
+    return ((0, 4), (4, 4 + half), (4 + half, n_units))
 
 
 def add_block(into, part, count):
@@ -717,11 +810,14 @@
     normed_one, hat_one, inverse_one = norm_rows(inputs_f32, shared[0], shared[1])
     normed_low = normed_one.astype(BF)
     if own_kernels:
-        units, normed_all, all_bias = spread(
-            matrix_master[0].astype(BF), normed_low, bias_params[0, 0], slot_of_unit, n_tensor, back, unit_groups(n_units)
+        (
+            w_att, w_fc, w_proj, normed_all, all_bias,
+            q_scaled, keys_in, values_in, attended, log_norms, peaks, hidden,
+        ) = forward_spread(
+            matrix_master[0].astype(BF), normed_low, tokens_in, bias_params[0, 0], first_seen, shared,
+            slot_of_unit, n_tensor, back,
         )
-        w_q, w_k, w_v, w_out = (units[i] for i in range(4))
-        w_fc, w_proj = (units[4 + i * (n_units - 4) // 2 :][: (n_units - 4) // 2].reshape(-1, width) for i in range(2))
+        w_q, w_k, w_v, w_out = (w_att[i] for i in range(4))
     else:
         units = gather_units(matrix_master[0], slot_of_unit)
         stacks = units.reshape(n_tensor, n_units * unit_rows, width)
@@ -736,16 +832,16 @@
         ]
         blank = [jnp.zeros_like(normed_low)] * (back - len(before))
         normed_all = jnp.concatenate([*blank, *before, normed_low], axis=0)
-    bias = lambda first, count: all_bias[:, first : first + count].reshape(-1)
-    b_q, b_k, b_v = (bias(i * head_rows, head_rows) for i in range(3))
+    if not own_kernels:
+        bias = lambda first, count: all_bias[:, first : first + count].reshape(-1)
+        b_q, b_k, b_v = (bias(i * head_rows, head_rows) for i in range(3))
+        q_scaled = (rows_by_rows(normed_low, w_q) + b_q).astype(BF) * jnp.asarray(1.0 / math.sqrt(HD), BF)
+        keys_in = (rows_by_rows(normed_all, w_k) + b_k).astype(BF)
+        values_in = (rows_by_rows(normed_all, w_v) + b_v).astype(BF)
+        attended, log_norms, peaks = attend_forward(q_scaled, keys_in, values_in, first_seen)
+        hidden = inputs_f32 + (plain_dot(attended, w_out) + shared[2])
     swap = (lambda v: v.swapaxes(0, 1)) if own_kernels else (lambda v: v)
     b_fc = swap(all_bias[:, 3 * head_rows :].reshape(n_tensor, -1, unit_rows)).reshape(-1)
-    scale = 1.0 / math.sqrt(HD)
-    q_scaled = (rows_by_rows(normed_low, w_q) + b_q).astype(BF) * jnp.asarray(scale, BF)
-    keys_in = (rows_by_rows(normed_all, w_k) + b_k).astype(BF)
-    values_in = (rows_by_rows(normed_all, w_v) + b_v).astype(BF)
-    attended, log_norms, peaks = attend_forward(q_scaled, keys_in, values_in, first_seen)
-    hidden = inputs_f32 + (plain_dot(attended, w_out) + shared[2])
     normed_two, hat_two, inverse_two = norm_rows(hidden, shared[3], shared[4])
     second_low = normed_two.astype(BF)
     pre_act = rows_by_rows(second_low, w_fc) + b_fc
@@ -799,7 +895,7 @@
         vectors = jnp.pad(vectors, ((0, 16 - vectors.shape[0]), (0, 0)))
         grad_units = jnp.concatenate(
             [g.astype(BF) for g in (grad_q_w, grad_k_w, grad_v_w, grad_out_w, grad_fc_w, grad_proj_w)], axis=0
-        ).reshape(units.shape)
+        ).reshape(n_units, -1, width)
         my_grads, totals = reduce_units(
             grad_units, vectors, unit_of_slot, n_tensor, slot_cap, unit_groups(n_units)[::-1]
         )

time: 673 us -> 582 us (0.86)
  Pallas kernels: 456 us -> 404 us
  local copies, waits for them, and re-layouts: 37.3 us -> 13.9 us
  matrix products: 117 us -> 102 us
    pallas_call x2 -> x1, Pallas kernels: 205 us -> 158 us  [forward_spread(): pl.pallas_call(functools.partial(forward_kernel, n_tensor, back, 1.0 / ma...]
    slice x2 -> x1, local copies, waits for them, and re-layouts: 19.5 us -> 2.77 us  [per_device(): w_q, w_k, w_v, w_out = (w_att[i] for i in range(4))]
    dot_general x6 -> x3, matrix products: 39.9 us -> 28.1 us  [rows_by_rows(): lax.dot_general(left, right, (((1,), (1,)), ((), ())), preferred_element_...]
    unnamed x77 -> x63, local copies, waits for them, and re-layouts: 11.4 us -> 3.46 us
    dot_general x6 -> x5, matrix products: 39.9 us -> 38.5 us  [plain_dot(): return jnp.dot(left, right, preferred_element_type=F32)]
  transfers between devices with their start and end apart: 2 -> 2, of which waited for: 1 -> 1; matrix products, arithmetic and copies ran while one was open for 8% -> 9% of each run, Pallas kernels for 0% -> 0%
where the time goes in v3:
time: 582 us; the launch traced here: 574 us
  Pallas kernels  404 us (69%)
  matrix products  102 us (18%)
  other arithmetic  26.2 us (5%)
  waiting for transfers between devices  16.1 us (3%)
  local copies, waits for them, and re-layouts  13.9 us (2%)
  starting transfers between devices  11.1 us (2%)
    pallas_call x1, Pallas kernels, reduce_units(): pl.pallas_call(functools.partial(reduce_kernel, groups, n_tensor), out_sh...  215 us
    pallas_call x1, Pallas kernels, forward_spread(): pl.pallas_call(functools.partial(forward_kernel, n_tensor, back, 1.0 / ma...  158 us
    dot_general x5, matrix products, plain_dot(): return jnp.dot(left, right, preferred_element_type=F32)  38.5 us
    dot_general x6, matrix products, cols_by_cols(): lax.dot_general(left, right, (((0,), (0,)), ((), ())), preferred_element_...  35.6 us
    pallas_call x1, Pallas kernels, attend_backward(): pl.pallas_call(functools.partial(attend_back_kernel, scale=1.0 / math.sqr...  30.9 us
    dot_general x3, matrix products, rows_by_rows(): lax.dot_general(left, right, (((1,), (1,)), ((), ())), preferred_element_...  28.1 us
    ppermute x2, waiting for transfers between devices, per_device(): lax.ppermute(away, 'tensor', [(i, i - r) for i in range(r, n_tensor)])  16.1 us
  transfers between devices with their start and end apart: 2, of which 1 were waited for; matrix products, arithmetic and copies ran while one was open for 9% of the time, Pallas kernels for 0%

profile of v3, /device:TPU:9, one launch (start us, length us, event | category | flops | bytes accessed | tf_op | source)
XLA Modules:
  0.0 574.2 jit_solution(8000158015376190062)
XLA Ops:
  1.7 1.4 slice_bitcast_fusion.shared_ref
  4.7 1.2 multiply_add_fusion.slot_ref
  5.9 1.4 convert_reduce_fusion.4
  7.4 1.7 fusion.23
  10.4 1.1 convert_element_type.103
  11.5 1.4 fusion.17.a_ref
  12.9 158.0 %forward_spread.1 = (bf16[4,4,4,2,32,1024]{5,4,3,2,1,0:T(8,128)(2,1)}, bf16[4,4,4,2,32,1024]{5,4,3,2,1,0:T(8,128)(2,1)}, bf16[4,4,4,2,32,1024]{5,4,3,2,1,0:T(8,1...) custom-call(s32[12]{0:T(128)} %multiply_add_fusion.slot_ref, ...), custom_call_target="tpu_custom_call" | custom-call | tf_op jit(solution)/shard_map/forward_spread/pallas_call | solution.py:542
  171.9 1.9 reduce_sum.202
  174.2 10.2 %fusion.47 = f32[4096,512]{0,1:T(8,128)} fusion(bf16[4096,1024]{1,0:T(8,128)(2,1)} %bitcast.145, bf16[512,1024]{1,0:T(8,128)(2,1)S(1)} %copy-done.18), kind=kOutput, calls=%fused_computation.130 | convolution fusion | flops 4294967296 | bytes 17825792 | tf_op jit(solution)/shard_map/dot_general | solution.py:35
  184.4 16.5 %convert_reduce_fusion = (f32[4096]{0:T(1024)S(1)}, bf16[512,4096]{1,0:T(8,128)(2,1)}, f32[512,4096]{1,0:T(8,128)}) fusion(f32[4096]{0:T(1024)S(1)} %bitcast.135, f32[4096,512]{0,1:T(8,128)} %fusion.47, bf16[4096,1024]{1,0:T(8,128)(2,1)} %bitcast.147, f32[512,1024]{1,0:T(8,128)S(1)} %copy-done.6, f32[1024]{0:T(1024)S(1)} %bitcast.141, ...), kind=kOutput, calls=%fused_computation.14 | convolution fusion | flops 4345819136 | bytes 31502336 | tf_op jit(solution)/shard_map/dot_general | solution.py:35
  200.9 8.7 %multiply_reduce_fusion = (f32[1024]{0:T(1024)S(1)}, f32[512]{0:T(512)S(1)}, f32[512]{0:T(512)S(1)}, f32[1024]{0:T(1024)S(1)}, f32[512,1024]{1,0:T(8,128)S(1)}) fusion(f32[512,1024]{1,0:T(8,128)S(1)} %copy-done.6, f32[512]{0:T(512)S(1)} %add_rsqrt_fusion, f32[512]{0:T(512)S(1)} %broadcast_multiply_fusion.4, f32[1024]{0:T(1024)S(1)} %bitcast.130, ...), kind=kOutput, calls=%fused_computation.50 | convolution fusion | flops 4299682816 | bytes 16797696 | tf_op jit(solution)/shard_map/dot_general | solution.py:31
  209.7 2.8 fusion.43
  213.4 1.3 convolution_convert_fusion.do_ref
  215.7 30.9 %attend_backward.1 = (bf16[512,1024]{1,0:T(8,128)(2,1)S(1)}, bf16[1536,1024]{1,0:T(8,128)(2,1)}, bf16[1536,1024]{1,0:T(8,128)(2,1)}) custom-call(s32[1,512]{1,0:T(1,128)S(1)} %bitcast.110, bf16[512,1024]{1,0:T(8,128)(2,1)S(1)} %copy-done.1, bf16[1536,1024]{1,0:T(8,128)(2,1)} %get-tuple-element.35.k_ref, bf16[1536,1024]{1,0:T(8,128)(2,1)} %get-tuple-element.36.v_ref, ...), custom_call_target="tpu_custom_call" | custom-call | tf_op jit(solution)/shard_map/attend_backward/pallas_call | solution.py:187
  246.6 5.5 fusion.48
  252.1 5.4 fusion.46
  257.5 1.5 fusion.44
  259.0 9.8 %collective-permute-start = (bf16[512,1024]{1,0:T(8,128)(2,1)}, bf16[512,1024]{1,0:T(8,128)(2,1)}, u32[]{:S(2)}, u32[]{:S(2)}) collective-permute-start(bf16[512,1024]{1,0:T(8,128)(2,1)} %get-tuple-element.113), channel_id=1, source_target_pairs={{1,0},{2,1},{3,2},{5,4},{6,5},{7,6},{9,8},{10,9},{11,10},{13,12},{... | collective-permute-start | bytes 3145736 | tf_op jit(solution)/shard_map/ppermute | solution.py:873
  268.8 1.3 collective-permute-start.1
  270.7 2.7 convert_dynamic-update-slice_fusion.5
  273.4 5.1 convert_dynamic-update-slice_fusion.4
  278.5 4.8 convert_dynamic-update-slice_fusion.3
  283.3 2.7 convert_dynamic-update-slice_fusion.2
  286.0 7.3 %convert_dynamic-update-slice_fusion.1 = bf16[12288,1024]{1,0:T(8,128)(2,1)} fusion(bf16[12288,1024]{1,0:T(8,128)(2,1)} %convert_dynamic-update-slice_fusion.2, bf16[512,4096]{1,0:T(8,128)(2,1)S(1)} %copy-done.27, f32[512,1024]{1,0:T(8,128)S(1)} %copy-done.6, f32[1024]{0:T(1024)S(1)} %bitcast.142, f32[1024]{0:T(1024)S(1)} %bitcast.132, ...), kind=kOutput, calls=%fused_computation.16 | convolution fusion | flops 4301783040 | bytes 14692352 | tf_op jit(solution)/shard_map/dot_general | solution.py:39
  293.3 12.6 %add_add_fusion = f32[512,1024]{1,0:T(8,128)} fusion(f32[512,1024]{1,0:T(8,128)S(1)} %copy-done.6, bf16[4096,1024]{1,0:T(8,128)(2,1)} %bitcast.146, f32[1024]{0:T(1024)S(1)} %bitcast.140, f32[512,4096]{1,0:T(8,128)} %get-tuple-element.124, f32[4096]{0:T(1024)S(1)} %bitcast.136), kind=kOutput, calls=%fused_computation.57 | convolution fusion | flops 4316987392 | bytes 20992000 | tf_op jit(solution)/shard_map/dot_general | solution.py:31
  305.9 13.1 %convert_dynamic-update-slice_fusion = bf16[12288,1024]{1,0:T(8,128)(2,1)} fusion(bf16[12288,1024]{1,0:T(8,128)(2,1)} %convert_dynamic-update-slice_fusion.1, bf16[512,1024]{1,0:T(8,128)(2,1)S(1)} %copy-done.19, f32[512,4096]{1,0:T(8,128)} %get-tuple-element.124, f32[4096]{0:T(1024)S(1)} %bitcast.137), kind=kOutput, calls=%fused_computation.15 | convolution fusion | flops 4320133120 | bytes 17842176 | tf_op jit(solution)/shard_map/dot_general | solution.py:39
  320.7 16.1 %collective-permute-done.1 = bf16[512,1024]{1,0:T(8,128)(2,1)} collective-permute-done((bf16[512,1024]{1,0:T(8,128)(2,1)}, bf16[512,1024]{1,0:T(8,128)(2,1)}, u32[]{:S(2)}, u32[]{:S(2)}) %collective-permute-start.1) | collective-permute-done | bytes 1048608 | tf_op jit(solution)/shard_map/ppermute | solution.py:873
  336.8 6.2 %fusion.22 = (f32[1024]{0:T(1024)S(1)}, f32[512]{0:T(512)S(1)}, f32[512]{0:T(512)S(1)}, f32[1024]{0:T(1024)S(1)}, f32[512,1024]{1,0:T(8,128)}) fusion(bf16[512,1024]{1,0:T(8,128)(2,1)S(1)} %copy-done.5, f32[512]{0:T(512)S(1)} %add_rsqrt_fusion.1, f32[512]{0:T(512)S(1)} %broadcast_multiply_fusion.5, f32[1024]{0:T(1024)S(1)} %bitcast.123, ...), kind=kOutput, calls=%fused_computation.41 | convolution fusion | flops 1081603072 | bytes 10506240 | tf_op jit(solution)/shard_map/dot_general | solution.py:31
  343.8 214.7 %reduce_units.1 = (bf16[2,8,32,1024]{3,2,1,0:T(8,128)(2,1)}, f32[16,1024]{1,0:T(8,128)}) custom-call(s32[16]{0:T(128)} %copy-done.25, bf16[12,4,2,2,2,32,1024]{6,5,4,3,2,1,0:T(8,128)(2,1)} %bitcast.19.g_ref, f32[16,1024]{1,0:T(8,128)} %pad.9.v_ref), custom_call_target="tpu_custom_call" | custom-call | tf_op jit(solution)/shard_map/reduce_units/pallas_call | solution.py:741
  560.1 1.4 multiply_subtract_fusion
  564.2 3.8 fusion.21
  568.7 5.3 multiply_select_fusion
  (111 shorter events, 15.2 us)
Async XLA Ops:
  0.6 9.1 %copy-start.22 = (f32[3,1,1792]{2,1,0:T(1,128)S(1)}, f32[3,1,1792]{2,1,0:T(1,128)}, u32[]{:S(2)}) copy-start(f32[3,1,1792]{2,1,0:T(1,128)} %param.17) | copy-start | bytes 64516
  0.7 9.7 %copy-start.7 = (f32[1,2,256,1024]{3,2,1,0:T(8,128)S(1)}, f32[1,2,256,1024]{3,2,1,0:T(8,128)}, u32[]{:S(2)}) copy-start(f32[1,2,256,1024]{3,2,1,0:T(8,128)} %param.13) | copy-start | bytes 6291460
  7.3 4.2 copy-start.4
  170.9 2.8 copy-start.6
  171.9 2.2 copy-start.18
  174.1 35.5 %slice-start = ((s8[8388608]{0:T(1024)(128)(4,1)}), s8[4194304]{0:T(1024)(128)(4,1)S(1)}, s32[]{:S(2)}) async-start(s8[8388608]{0:T(1024)(128)(4,1)} %bitcast.111), calls=%async_computation | async-start | bytes 8388608
  184.4 25.3 %slice-start.1 = ((s8[8388608]{0:T(1024)(128)(4,1)}), s8[4194304]{0:T(1024)(128)(4,1)S(1)}, s32[]{:S(2)}) async-start(s8[8388608]{0:T(1024)(128)(4,1)} %bitcast.111), calls=%async_computation.1 | async-start | bytes 8388608
  213.4 70.0 %copy-start.9 = (f32[512,1024]{1,0:T(8,128)}, f32[512,1024]{1,0:T(8,128)S(1)}, u32[]{:S(2)}) copy-start(f32[512,1024]{1,0:T(8,128)S(1)} %get-tuple-element.105) | copy-start | bytes 6291460
  213.4 2.0 copy-start
  213.4 2.3 copy-start.1
  213.4 2.3 copy-start.2
  213.4 2.3 copy-start.3
  215.7 30.9 %copy-start.17 = (bf16[1,4,4,2,32,1024]{5,4,3,2,1,0:T(8,128)(2,1)S(1)}, bf16[1,4,4,2,32,1024]{5,4,3,2,1,0:T(8,128)(2,1)}, u32[]{:S(2)}) copy-start(bf16[1,4,4,2,32,1024]{5,4,3,2,1,0:T(8,128)(2,1)} %get-tuple-element.108) | copy-start | bytes 6291460
  246.5 5.6 copy-start.12
  246.5 5.6 copy-start.16
  257.5 12.6 %copy-start.13 = (bf16[1536,1024]{1,0:T(8,128)(2,1)S(1)}, bf16[1536,1024]{1,0:T(8,128)(2,1)}, u32[]{:S(2)}) copy-start(bf16[1536,1024]{1,0:T(8,128)(2,1)} %get-tuple-element.40) | copy-start | bytes 9437188
  259.0 11.7 %copy-start.11 = (bf16[512,1024]{1,0:T(8,128)(2,1)S(1)}, bf16[512,1024]{1,0:T(8,128)(2,1)}, u32[]{:S(2)}) copy-start(bf16[512,1024]{1,0:T(8,128)(2,1)} %fusion.17.a_ref) | copy-start | bytes 3145732
  259.0 61.7 %collective-permute-start = (bf16[512,1024]{1,0:T(8,128)(2,1)}, bf16[512,1024]{1,0:T(8,128)(2,1)}, u32[]{:S(2)}, u32[]{:S(2)}) collective-permute-start(bf16[512,1024]{1,0:T(8,128)(2,1)} %get-tuple-element.113), channel_id=1, source_target_pairs={{1,0},{2,1},{3,2},{5,4},{6,5},{7,6},{9,8},{10,9},{11,10},{13,12},{... | collective-permute-start | bytes 3145736 | tf_op jit(solution)/shard_map/ppermute | solution.py:873
  268.8 68.0 %collective-permute-start.1 = (bf16[512,1024]{1,0:T(8,128)(2,1)}, bf16[512,1024]{1,0:T(8,128)(2,1)}, u32[]{:S(2)}, u32[]{:S(2)}) collective-permute-start(bf16[512,1024]{1,0:T(8,128)(2,1)} %get-tuple-element.114), channel_id=1, source_target_pairs={{2,0},{3,1},{6,4},{7,5},{10,8},{11,9},{14,12},{15,13},{18,16},{19,... | collective-permute-start | bytes 3145736 | tf_op jit(solution)/shard_map/ppermute | solution.py:873
  270.7 2.7 copy-start.26
  283.3 2.7 copy-start.27
  293.3 12.6 %copy-start.19 = (bf16[512,1024]{1,0:T(8,128)(2,1)S(1)}, bf16[512,1024]{1,0:T(8,128)(2,1)}, u32[]{:S(2)}) copy-start(bf16[512,1024]{1,0:T(8,128)(2,1)} %param.10) | copy-start | bytes 3145732
  319.0 0.8 copy-start.23
  319.0 1.2 copy-start.24
  319.0 17.8 %copy-start.5 = (bf16[512,1024]{1,0:T(8,128)(2,1)S(1)}, bf16[512,1024]{1,0:T(8,128)(2,1)}, u32[]{:S(2)}) copy-start(bf16[512,1024]{1,0:T(8,128)(2,1)} %x_ref.1) | copy-start | bytes 3145732
  320.5 22.5 %copy-start.25 = (s32[16]{0:T(128)}, s32[16]{0:T(128)S(1)}, u32[]{:S(2)}) copy-start(s32[16]{0:T(128)S(1)} %select_reduce_fusion.1.unit_ref) | copy-start | bytes 196
  343.8 216.2 %copy-start.21 = (f32[3,6,1024]{2,1,0:T(8,128)S(1)}, f32[3,6,1024]{2,1,0:T(8,128)}, u32[]{:S(2)}) copy-start(f32[3,6,1024]{2,1,0:T(8,128)} %param.16) | copy-start | bytes 221188
  343.8 220.4 %copy-start.10 = (f32[512,1024]{1,0:T(8,128)S(1)}, f32[512,1024]{1,0:T(8,128)}, u32[]{:S(2)}) copy-start(f32[512,1024]{1,0:T(8,128)} %copy-done.9) | copy-start | bytes 6291460
  564.2 3.8 copy-start.8
  564.2 3.8 copy-start.14
  564.2 3.8 copy-start.15
  564.2 4.4 copy-start.20

commit v4 on v3

--- a/solution.py
+++ b/solution.py
@@ -21,6 +21,8 @@
 EPS_ADAM = 1e-08
 CLIP_TAU = 10.0
 MASKED = -1e30
+GELU_A = 0.7978845608
+GELU_B = 0.044715
 BF = jnp.bfloat16
 F32 = jnp.float32
 MESH = pl.DeviceIdType.MESH
@@ -273,20 +275,21 @@
 
 
 def loop_with(count, body, events):
-    per = -(-len(events) // count)
-
     def step(i, carry):
         body(i)
-        for n in range(count):
-            mine = events[n * per : (n + 1) * per]
-            if mine:
-                @pl.when(i == n)
-                def _(mine=mine):
-                    for event in mine:
-                        event()
+        for n, mine in events.items():
+            @pl.when(i == n)
+            def _(mine=mine):
+                for event in mine:
+                    event()
         return carry
 
     lax.fori_loop(0, count, step, 0)
+
+
+def spaced(count, events):
+    per = -(-len(events) // count)
+    return {n: events[n * per : (n + 1) * per] for n in range(count) if events[n * per : (n + 1) * per]}
 
 
 def attend_pair(i, q_ref, k_ref, v_ref, o_ref, lse_ref, peak_ref, bias_ref):
@@ -489,13 +492,13 @@
     tiles = width // tile
     n_late = len(late)
     cut = n_late // 5
-    loop_with(tiles, project(0, a_ref, q_ref, scale), late[:0])
-    loop_with(tiles, project(1, None, k_ref, None), late[:cut])
-    loop_with(tiles, project(2, None, v_ref, None), late[cut : 2 * cut])
+    loop_with(tiles, project(0, a_ref, q_ref, scale), {})
+    loop_with(tiles, project(1, None, k_ref, None), spaced(tiles, late[:cut]))
+    loop_with(tiles, project(2, None, v_ref, None), spaced(tiles, late[cut : 2 * cut]))
     loop_with(
         width // PAIR,
         lambda i: attend_pair(i, q_ref, k_ref, v_ref, o_ref, lse_ref, peak_ref, seen_ref),
-        late[2 * cut :],
+        spaced(width // PAIR, late[2 * cut :]),
     )
     w_out = att_ref[3].reshape(width, width)
     half = rows_here // 2
@@ -570,138 +573,439 @@
     )
 
 
-def unit_groups(n_units):
-    half = (n_units - 4) // 2
-    return ((0, 4), (4, 4 + half), (4 + half, n_units))
-
-
-def add_block(into, part, count):
-    def body(i, _):
-        a, b = into(i), part(i)
-        a[...] = a[...] + b[...]
-        return 0
+def add_blocks(into, part, count):
+    def body(i, carry):
+        a = into(i)
+        a[...] = a[...] + part(i)[...]
+        return carry
+
     lax.fori_loop(0, count, body, 0)
+
+
+class Reducer:
+    def __init__(self, groups, n_tensor, other, near, one, two, up_in, down_in, final, sems):
+        self.groups, self.n_tensor = groups, n_tensor
+        self.other, self.near, self.one, self.two = other, near, one, two
+        self.up_in, self.down_in, self.final = up_in, down_in, final
+        (
+            self.near_sem, self.core_send, self.core_recv, self.one_send, self.one_recv,
+            self.two_send, self.two_recv, self.z_send, self.z_recv,
+        ) = sems
+        self.d, self.t, self.core, self.x, self.y = place()
+        self.by_x, self.by_y = self.d + 2 - 4 * self.x, self.d + 4 - 8 * self.y
+        self.sibling = self.d + 1 - 2 * self.core
+        self.order = sorted(range(n_tensor), key=lambda a: -abs(2 * a - n_tensor + 1))
+        self.merges = [(g, at) for g in range(len(groups)) for at in self.order]
+        self.starts, total = [], 0
+        for refs in groups:
+            self.starts.append(total)
+            total += sum(r.shape[0] for r in refs)
+        self.ends = [*self.starts[1:], total]
+
+    @staticmethod
+    def scratch(n_units, n_group, n_groups, n_refs, n_tensor, block):
+        dma = pltpu.SemaphoreType.DMA
+        return [
+            pltpu.VMEM((n_units, n_tensor, 2, 2, *block), BF),
+            pltpu.VMEM((2, n_group, 2, 2, *block), BF),
+            pltpu.VMEM((n_units, n_tensor, 2, *block), BF),
+            pltpu.VMEM((n_units, n_tensor, *block), BF),
+            pltpu.VMEM((n_units, n_tensor, *block), BF),
+            pltpu.VMEM((n_units, n_tensor, *block), BF),
+            dma((2, n_refs)), dma((n_groups, n_refs)), dma((n_groups, n_refs)),
+            dma((n_groups, n_tensor)), dma((n_groups, n_tensor)),
+            dma((n_groups, n_tensor)), dma((n_groups, n_tensor)),
+            dma((n_groups, n_tensor)), dma((n_groups, n_tensor, 2)),
+        ]
+
+    def parts(self, g):
+        u = self.starts[g]
+        for n, ref in enumerate(self.groups[g]):
+            yield n, ref, u, ref.shape[0]
+            u += ref.shape[0]
+
+    def units(self, g):
+        return pl.ds(self.starts[g], self.ends[g] - self.starts[g])
+
+    def count(self, g):
+        return self.ends[g] - self.starts[g]
+
+    def near_copies(self, m):
+        g, at = self.merges[m]
+        for n, ref, u, many in self.parts(g):
+            yield pltpu.make_async_copy(
+                ref.at[:, at, :, :, self.core],
+                self.near.at[m % 2, pl.ds(u - self.starts[g], many)],
+                self.near_sem.at[m % 2, n],
+            )
+
+    def start(self):
+        for g in range(len(self.groups)):
+            for n, ref, u, many in self.parts(g):
+                send(
+                    ref.at[:, :, :, :, 1 - self.core], self.other.at[pl.ds(u, many)],
+                    self.core_send.at[g, n], self.core_recv.at[g, n], (self.sibling, self.t),
+                )
+        for m in range(2):
+            for copy in self.near_copies(m):
+                copy.start()
+
+    def by_rows(self, at):
+        return at * 2 < self.n_tensor
+
+    def first_hop(self, m):
+        g, at = self.merges[m]
+        if m % self.n_tensor == 0:
+            for n, ref, u, many in self.parts(g):
+                arrived(self.other.at[pl.ds(u, many)], self.core_recv.at[g, n])
+        for copy in self.near_copies(m):
+            copy.wait()
+        u0 = self.starts[g]
+        add_blocks(
+            lambda i: self.other.at[u0 + i // 4, at, (i // 2) % 2, i % 2],
+            lambda i: self.near.at[m % 2, i // 4, (i // 2) % 2, i % 2],
+            4 * self.count(g),
+        )
+        if m + 2 < len(self.merges):
+            for copy in self.near_copies(m + 2):
+                copy.start()
+        us = self.units(g)
+        rows = self.by_rows(at)
+        source = self.other.at[us, at, 1 - self.y] if rows else self.other.at[us, at, :, 1 - self.x]
+        to = self.by_y if rows else self.by_x
+        send(source, self.one.at[us, at], self.one_send.at[g, at], self.one_recv.at[g, at], (to, self.t))
+
+    def second_hop(self, m):
+        g, at = self.merges[m]
+        us, u0 = self.units(g), self.starts[g]
+        arrived(self.one.at[us, at], self.one_recv.at[g, at])
+        if self.by_rows(at):
+            into = lambda i: self.other.at[u0 + i // 2, at, self.y, i % 2]
+            source, to = self.other.at[us, at, self.y, 1 - self.x], self.by_x
+        else:
+            into = lambda i: self.other.at[u0 + i // 2, at, i % 2, self.x]
+            source, to = self.other.at[us, at, 1 - self.y, self.x], self.by_y
+        add_blocks(into, lambda i: self.one.at[u0 + i // 2, at, i % 2], 2 * self.count(g))
+        send(source, self.two.at[us, at], self.two_send.at[g, at], self.two_recv.at[g, at], (to, self.t))
+
+    def plane_sum(self, m):
+        g, at = self.merges[m]
+        us, u0, n = self.units(g), self.starts[g], self.count(g)
+        arrived(self.two.at[us, at], self.two_recv.at[g, at])
+        add_blocks(lambda i: self.other.at[u0 + i, at, self.y, self.x], lambda i: self.two.at[u0 + i, at], n)
+        if at > 0:
+            pl.when(self.t == 0)(functools.partial(self.line_go, g, at, True))
+        if at < self.n_tensor - 1:
+            pl.when(self.t == self.n_tensor - 1)(functools.partial(self.line_go, g, at, False))
+
+    def line_go(self, g, at, up):
+        us = self.units(g)
+        into, way, to = (self.up_in, 0, self.t + 1) if up else (self.down_in, 1, self.t - 1)
+        send(self.other.at[us, at, self.y, self.x], into.at[us, at], self.z_send.at[g, at], self.z_recv.at[g, at, way], (self.d, to))
+
+    def line_in(self, g, at, up):
+        us, u0, n, t = self.units(g), self.starts[g], self.count(g), self.t
+        buffer, way = (self.up_in, 0) if up else (self.down_in, 1)
+        arrived(buffer.at[us, at], self.z_recv.at[g, at, way])
+        add_blocks(lambda i: self.other.at[u0 + i, at, self.y, self.x], lambda i: buffer.at[u0 + i, at], n)
+        pl.when(t < at if up else t > at)(functools.partial(self.line_go, g, at, up))
+
+    def line(self, g, k):
+        n, t = self.n_tensor, self.t
+        high, low = n - 1 - k, k
+        near_top = t * 2 >= n
+        came_down = (t >= low) & (t < n - 1)
+        pl.when(came_down & near_top)(functools.partial(self.line_in, g, low, False))
+        pl.when((t <= high) & (t > 0))(functools.partial(self.line_in, g, high, True))
+        pl.when(came_down & (t * 2 < n))(functools.partial(self.line_in, g, low, False))
+
+    def keep(self, g):
+        us = self.units(g)
+        self.final[us] = self.other[us, self.t, self.y, self.x]
+
+    def events(self):
+        n, count = self.n_tensor, len(self.groups)
+        first, second, third = (
+            [[functools.partial(f, g * n + i) for i in range(n)] for g in range(count)]
+            for f in (self.first_hop, self.second_hop, self.plane_sum)
+        )
+        lines = [[functools.partial(self.line, g, k) for k in range(n - 1)] + [functools.partial(self.keep, g)] for g in range(count)]
+        return first, second, third, lines
+
+    def finish(self):
+        for g in range(len(self.groups)):
+            us = self.units(g)
+            for n, ref, u, many in self.parts(g):
+                arrived(self.other.at[pl.ds(u, many)], self.core_send.at[g, n])
+            for at in range(self.n_tensor):
+                arrived(self.one.at[us, at], self.one_send.at[g, at])
+                arrived(self.two.at[us, at], self.two_send.at[g, at])
+
+                @pl.when(self.t != at)
+                def _(us=us, g=g, at=at):
+                    arrived(self.up_in.at[us, at], self.z_send.at[g, at])
+
+
+REDUCER = 15
+
+
+def backward_kernel(
+    n_tensor, back, scale,
+    proj_ref, fc_ref, q_ref, k_ref, v_ref, o_ref, do_ref, lse_ref, first_ref, wide_ref, att_ref,
+    shard_ref, grad_ref, gq_ref, gk_ref, gv_ref, sums_ref, *scratch,
+):
+    reducer_scratch, (
+        seen_ref, q_in, k_in, v_in, o_in, do_in, dq_ref, dk_ref, dv_ref, big, away, away_in, stage, dk_acc, dv_acc,
+        pair_sem, load_sem, stage_sem, away_send, away_recv,
+    ) = scratch[:REDUCER], scratch[REDUCER:]
+    d, t, core, x, y = place()
+    greet(d, t, n_tensor)
+    n_fc = fc_ref.shape[0]
+    other, near, one, two, up_in, down_in, *sems = reducer_scratch
+    reducer = Reducer([[fc_ref], [proj_ref]], n_tensor, other, near, one, two, up_in, down_in, shard_ref, sems)
+    reducer.start()
+    rows_here, width = do_ref.shape
+    n_keys = k_ref.shape[0]
+    size, span = q_tiles(rows_here, n_keys)
+    sources = ((q_ref, q_in), (k_ref, k_in), (v_ref, v_in), (o_ref, o_in), (do_ref, do_in))
+
+    def pair_copies(i):
+        lanes = pl.ds(pl.multiple_of(i * PAIR, PAIR), PAIR)
+        return [
+            pltpu.make_async_copy(ref.at[:, lanes], buffer.at[i % 2], pair_sem.at[i % 2, n])
+            for n, (ref, buffer) in enumerate(sources)
+        ]
+
+    for copy in pair_copies(0):
+        copy.start()
+    weights = pltpu.make_async_copy(att_ref.at[pl.ds(0, 3 * width)], big, load_sem.at[0])
+    weights.start()
+    fill_bias(seen_ref, first_ref)
+    pairs = width // PAIR
+
+    def attend_back(i):
+        for copy in pair_copies(i):
+            copy.wait()
+
+        @pl.when(i + 1 < pairs)
+        def _():
+            for copy in pair_copies(i + 1):
+                copy.start()
+
+        slot = i % 2
+        lanes_here = pl.ds(pl.multiple_of(i * PAIR, PAIR), PAIR)
+        dk_acc[...] = jnp.zeros_like(dk_acc)
+        dv_acc[...] = jnp.zeros_like(dv_acc)
+        dq_sum = jnp.zeros((1, PAIR), F32)
+        for j in range(rows_here // size):
+            rows, keys = pl.ds(j * size, size), pl.ds(j * size, span)
+            q_here, do_here = q_in[slot, rows, :], do_in[slot, rows, :]
+            k_here, v_here = k_in[slot, keys, :], v_in[slot, keys, :]
+            k_t = k_here.T
+            meet = (do_here.astype(F32) * o_in[slot, rows, :].astype(F32)).T
+            outs = []
+            for h in range(2):
+                lanes = head_lanes(h)
+                delta = jnp.sum(meet[h * HD : (h + 1) * HD], axis=0, keepdims=True)
+                s = rows_by_rows(jnp.where(lanes, k_here, 0), q_here) + seen_ref[keys, rows]
+                p = jnp.exp(s - lse_ref[i, h : h + 1, rows])
+                dp = rows_by_rows(jnp.where(lanes, v_here, 0), do_here)
+                ds = (p * (dp - delta)).astype(BF)
+                dv_acc[keys, :] += plain_dot(p.astype(BF), jnp.where(lanes, do_here, 0))
+                dk_acc[keys, :] += plain_dot(ds, jnp.where(lanes, q_here, 0))
+                outs.append(plain_dot(k_t[h * HD : (h + 1) * HD], ds))
+            dq = (jnp.concatenate(outs, axis=0).T * scale).astype(BF)
+            dq_ref[rows, lanes_here] = dq
+            dq_sum += jnp.sum(dq.astype(F32), axis=0, keepdims=True)
+        dk, dv = dk_acc[...].astype(BF), dv_acc[...].astype(BF)
+        dk_ref[:, lanes_here] = dk
+        dv_ref[:, lanes_here] = dv
+        sums_ref[0:1, lanes_here] = dq_sum
+        sums_ref[1:2, lanes_here] = jnp.sum(dk.astype(F32), axis=0, keepdims=True)
+        sums_ref[2:3, lanes_here] = jnp.sum(dv.astype(F32), axis=0, keepdims=True)
+
+    tile = 256
+    tiles = width // tile
+
+    def input_grad(r):
+        rows = pl.ds((back - r) * rows_here, rows_here)
+
+        def body(i):
+            cols = pl.ds(pl.multiple_of(i * tile, tile), tile)
+            total = plain_dot(dk_ref[rows, :], big[width : 2 * width, cols]) + plain_dot(dv_ref[rows, :], big[2 * width :, cols])
+            if r == 0:
+                grad_ref[:, cols] = total + plain_dot(dq_ref[...], big[:width, cols])
+            else:
+                away[r - 1, :, cols] = total.astype(BF)
+
+        return body
+
+    def have_down(r):
+        return (t + 1 >= r) & (t + 1 < n_tensor)
+
+    def give(r):
+        if r < back:
+            @pl.when(have_down(r + 1) & (t >= r))
+            def _():
+                arrived(away_in.at[r], away_recv.at[r])
+                away[r - 1] = (away[r - 1].astype(F32) + away_in[r].astype(F32)).astype(BF)
+
+        @pl.when(t >= r)
+        def _():
+            send(away.at[r - 1], away_in.at[r - 1], away_send.at[r - 1], away_recv.at[r - 1], (d, t - 1))
+
+    def weight_grad(n, from_ref, into_ref, first_row, many):
+        def body(i):
+            cols = pl.ds(pl.multiple_of(i * tile, tile), tile)
+            slot = i % 2
+            out = pltpu.make_async_copy(stage.at[slot], into_ref.at[pl.ds(i * tile, tile)], stage_sem.at[slot])
+
+            @pl.when((i >= 2) | (n > 0))
+            def _():
+                out.wait()
+
+            total = lax.dot_general(
+                from_ref[:, cols], tokens_of(first_row, many), (((0,), (0,)), ((), ())), preferred_element_type=F32
+            )
+            stage[slot] = total.astype(BF)
+            out.start()
+
+        return body
+
+    def tokens_of(first_row, many):
+        return big[pl.ds(first_row, many), :]
+
+    first, second, third, lines = reducer.events()
+    loop_with(pairs, attend_back, {1: first[0], 3: first[1]})
+    weights.wait()
+    for r in range(back, -1, -1):
+        loop_with(tiles, input_grad(r), {})
+        if r == back:
+            give(r)
+    load = pltpu.make_async_copy(wide_ref, big.at[pl.ds(0, n_keys)], load_sem.at[1])
+    load.start()
+    for event in second[0]:
+        event()
+    load.wait()
+    own = n_keys - rows_here
+    loop_with(tiles, weight_grad(0, dq_ref, gq_ref, own, rows_here), {})
+    loop_with(tiles, weight_grad(1, dk_ref, gk_ref, 0, n_keys), {1: third[0]})
+    loop_with(tiles, weight_grad(2, dv_ref, gv_ref, 0, n_keys), {1: lines[0][:1]})
+    for r in range(back - 1, 0, -1):
+        give(r)
+    for event in lines[0][1:] + second[1] + third[1] + lines[1]:
+        event()
+    for slot in range(2):
+        arrived(stage.at[slot], stage_sem.at[slot])
+
+    @pl.when(have_down(1))
+    def _():
+        arrived(away_in.at[0], away_recv.at[0])
+        grad_ref[...] = grad_ref[...] + away_in[0].astype(F32)
+    for r in range(1, back + 1):
+        @pl.when(t >= r)
+        def _(r=r):
+            arrived(away.at[r - 1], away_send.at[r - 1])
+    reducer.finish()
+
+
+def backward_reduce(grad_proj, grad_fc, q, k, v, o, do, lse, first_seen, wide, w_att, n_tensor, back):
+    rows, width = q.shape
+    n_keys = k.shape[0]
+    n_ff = grad_fc.shape[0]
+    block = grad_fc.shape[-2:]
+    any_spec = pl.BlockSpec(memory_space=pl.ANY)
+    vmem = pl.BlockSpec(memory_space=pltpu.VMEM)
+    dma = pltpu.SemaphoreType.DMA
+    shape = jax.ShapeDtypeStruct
+    square = shape((width, width), BF)
+    pair = lambda n: pltpu.VMEM((2, n, PAIR), BF)
+    return pl.pallas_call(
+        functools.partial(backward_kernel, n_tensor, back, 1.0 / math.sqrt(HD)),
+        out_shape=[shape((2 * n_ff, *block), BF), shape((rows, width), F32), square, square, square, shape((3, width), F32)],
+        in_specs=[any_spec] * 7 + [vmem, vmem] + [any_spec] * 2,
+        out_specs=[vmem, vmem, any_spec, any_spec, any_spec, vmem],
+        scratch_shapes=[
+            *Reducer.scratch(2 * n_ff, n_ff, 2, 1, n_tensor, block),
+            pltpu.VMEM((n_keys, rows), F32),
+            pair(rows), pair(n_keys), pair(n_keys), pair(rows), pair(rows),
+            pltpu.VMEM((rows, width), BF), pltpu.VMEM((n_keys, width), BF), pltpu.VMEM((n_keys, width), BF),
+            pltpu.VMEM((3 * width, width), BF),
+            pltpu.VMEM((back, rows, width), BF), pltpu.VMEM((back, rows, width), BF),
+            pltpu.VMEM((2, 256, width), BF),
+            pltpu.VMEM((n_keys, PAIR), F32), pltpu.VMEM((n_keys, PAIR), F32),
+            dma((2, 5)), dma((2,)), dma((2,)), dma((back,)), dma((back,)),
+        ],
+        compiler_params=pltpu.CompilerParams(collective_id=1, has_side_effects=True, vmem_limit_bytes=60 << 20),
+        name="backward_reduce",
+    )(grad_proj, grad_fc, q, k, v, o, do, lse, first_seen, wide, w_att)
 
 
 def join(row, a, b):
     return jnp.where(row == MAX_ROW, jnp.maximum(a, b), a + b)
 
 
-def reduce_kernel(
-    groups, n_tensor,
-    unit_ref, g_ref, v_ref, out_ref, vsum_ref,
-    half, other, plane_one, plane_two, up_in, down_in, final, outgo, v_in, v_z,
-    load_sem, core_send, core_recv, one_send, one_recv, two_send, two_recv, z_send, z_recv,
-    swap_send, swap_recv, v_send, v_recv, local_sem,
+def finish_kernel(
+    n_tensor,
+    unit_ref, gq_ref, gk_ref, gv_ref, go_ref, shard_ref, grad_ref, hidden_ref, x_ref, shared_ref, v_ref,
+    out_ref, vsum_ref, input_ref, *scratch,
 ):
+    reducer_scratch, (final, outgo, v_in, v_z, swap_send, swap_recv, v_send, v_recv, local_sem) = (
+        scratch[:REDUCER], scratch[REDUCER:]
+    )
     d, t, core, x, y = place()
-    by_x, by_y = d + 2 - 4 * x, d + 4 - 8 * y
-    sibling = d + 1 - 2 * core
     greet(d, t, n_tensor)
-    n_groups = len(groups)
-    ends = lambda g: (groups[g][0], groups[g][1] - groups[g][0])
-    order = sorted(range(n_tensor), key=lambda a: -abs(2 * a - n_tensor + 1))
-
-    loads = {}
-    for g in range(n_groups):
-        u0, n = ends(g)
-        us = pl.ds(u0, n)
-        send(g_ref.at[us, :, :, :, 1 - core], other.at[us], core_send.at[g], core_recv.at[g], (sibling, t))
-        loads[g] = pltpu.make_async_copy(g_ref.at[us, :, :, :, core], half.at[us], load_sem.at[g])
-        loads[g].start()
-
-    row = lax.broadcasted_iota(jnp.int32, v_ref.shape, 0)
+    other, near, one, two, up_in, down_in, *sems = reducer_scratch
+    reducer = Reducer([[gq_ref, gk_ref], [gv_ref, go_ref]], n_tensor, other, near, one, two, up_in, down_in, final, sems)
+    reducer.start()
+    rows_here = x_ref.shape[0]
+    n_att = other.shape[0]
+    final[n_att:] = shard_ref[...]
+
     vsum_ref[...] = v_ref[...]
-    for i, to in enumerate((sibling, by_x, by_y)):
-        send(vsum_ref, v_in.at[i], v_send.at[i], v_recv.at[i], (to, t))
+    part = 128
+    gain = shared_ref[0:1, :]
+
+    def norm_back_rows(i, carry):
+        rows = pl.ds(pl.multiple_of(i * part, part), part)
+        _, hat, inverse = norm_rows(x_ref[rows, :].astype(F32), 1.0, 0.0)
+        grad = grad_ref[rows, :]
+        input_ref[rows, :] = hidden_ref[rows, :] + norm_back(grad, hat, inverse, gain)
+        vsum_ref[0:1, :] += jnp.sum(grad * hat, axis=0, keepdims=True)
+        vsum_ref[1:2, :] += jnp.sum(grad, axis=0, keepdims=True)
+        return carry
+
+    lax.fori_loop(0, rows_here // part, norm_back_rows, 0)
+    row = lax.broadcasted_iota(jnp.int32, vsum_ref.shape, 0)
+    hops = (reducer.sibling, reducer.by_x, reducer.by_y)
+
+    def vector_go(i):
+        send(vsum_ref, v_in.at[i], v_send.at[i], v_recv.at[i], (hops[i], t))
+
+    def vector_in(i):
         arrived(v_in.at[i], v_recv.at[i])
         arrived(v_in.at[i], v_send.at[i])
         vsum_ref[...] = join(row, vsum_ref[...], v_in[i])
-    for k in range(1, n_tensor):
-        to = (t + k) % n_tensor
-        send(vsum_ref, v_z.at[k - 1], v_send.at[2 + k], v_recv.at[2 + k], (d, to))
-
-    def merge(g, at):
-        u0, n = ends(g)
-        lead = half.shape[2] * half.shape[3]
-        def pick(ref):
-            return lambda i: ref.at[u0 + i // lead, at, (i % lead) // 2, i % 2]
-        add_block(pick(half), pick(other), n * lead)
-
-    def first_hop(g, at):
-        u0, n = ends(g)
-        us = pl.ds(u0, n)
-        by_rows = at * 2 < n_tensor
-        source = half.at[us, at, 1 - y] if by_rows else half.at[us, at, :, 1 - x]
-        send(source, plane_one.at[us, at], one_send.at[g, at], one_recv.at[g, at], (by_y if by_rows else by_x, t))
-
-    def second_hop(g, at):
-        u0, n = ends(g)
-        us = pl.ds(u0, n)
-        by_rows = at * 2 < n_tensor
-        arrived(plane_one.at[us, at], one_recv.at[g, at])
-        if by_rows:
-            into = lambda i: half.at[u0 + i // 2, at, y, i % 2]
+        if i + 1 < len(hops):
+            vector_go(i + 1)
         else:
-            into = lambda i: half.at[u0 + i // 2, at, i % 2, x]
-        add_block(into, lambda i: plane_one.at[u0 + i // 2, at, i % 2], 2 * n)
-        source = half.at[us, at, y, 1 - x] if by_rows else half.at[us, at, 1 - y, x]
-        send(source, plane_two.at[us, at], two_send.at[g, at], two_recv.at[g, at], (by_x if by_rows else by_y, t))
-
-    def line(g, at):
-        u0, n = ends(g)
-        us = pl.ds(u0, n)
-        arrived(plane_two.at[us, at], two_recv.at[g, at])
-        mine = lambda i: half.at[u0 + i, at, y, x]
-        add_block(mine, lambda i: plane_two.at[u0 + i, at], n)
-
-        def take(buffer, way):
-            arrived(buffer.at[us, at], z_recv.at[g, at, way])
-            add_block(mine, lambda i: buffer.at[u0 + i, at], n)
-
-        @pl.when((t <= at) & (t > 0))
-        def _():
-            take(up_in, 0)
-
-        @pl.when((t >= at) & (t < n_tensor - 1))
-        def _():
-            take(down_in, 1)
-
-        source = half.at[us, at, y, x]
-
-        @pl.when(t < at)
-        def _():
-            send(source, up_in.at[us, at], z_send.at[g, at], z_recv.at[g, at, 0], (d, t + 1))
-
-        @pl.when(t > at)
-        def _():
-            send(source, down_in.at[us, at], z_send.at[g, at], z_recv.at[g, at, 1], (d, t - 1))
-
-        @pl.when(t == at)
-        def _():
-            add_block(lambda i: final.at[u0 + i], lambda i: half.at[u0 + i, at, y, x], n)
-
-    final[...] = jnp.zeros_like(final)
-    for g in range(n_groups):
-        u0, n = ends(g)
-        loads[g].wait()
-        arrived(other.at[pl.ds(u0, n)], core_recv.at[g])
-        for at in order:
-            merge(g, at)
-            first_hop(g, at)
-        if g == 0:
             for k in range(1, n_tensor):
-                arrived(v_z.at[k - 1], v_recv.at[2 + k])
-                arrived(v_z.at[k - 1], v_send.at[2 + k])
-            for k in range(1, n_tensor):
-                vsum_ref[...] = join(row, vsum_ref[...], v_z[k - 1])
-        if g > 0:
-            for at in order:
-                line(g - 1, at)
-        for at in order:
-            second_hop(g, at)
-    for at in order:
-        line(n_groups - 1, at)
+                send(vsum_ref, v_z.at[k - 1], v_send.at[2 + k], v_recv.at[2 + k], (d, (t + k) % n_tensor))
+
+    def vector_end():
+        for k in range(1, n_tensor):
+            arrived(v_z.at[k - 1], v_recv.at[2 + k])
+            arrived(v_z.at[k - 1], v_send.at[2 + k])
+        for k in range(1, n_tensor):
+            vsum_ref[...] = join(row, vsum_ref[...], v_z[k - 1])
+
+    vector_go(0)
+    first, second, third, lines = reducer.events()
+    events = first[0] + first[1] + second[0] + third[0] + second[1] + lines[0] + third[1] + lines[1]
+    for n, event in enumerate((functools.partial(vector_in, 0), functools.partial(vector_in, 1), functools.partial(vector_in, 2), vector_end)):
+        events.insert(4 + 5 * n, event)
+    for event in events:
+        event()
 
     cap = out_ref.shape[0]
     for k in range(1, 9):
@@ -714,59 +1018,101 @@
     keep.start()
     for k in range(1, 8):
         arrived(out_ref.at[:, (d + 8 - k) % 8], swap_recv.at[k - 1])
-    for g in range(n_groups):
-        us = pl.ds(*ends(g))
-        arrived(other.at[us], core_send.at[g])
-        for at in range(n_tensor):
-            arrived(plane_one.at[us, at], one_send.at[g, at])
-            arrived(plane_two.at[us, at], two_send.at[g, at])
-
-            @pl.when(t != at)
-            def _():
-                arrived(up_in.at[us, at], z_send.at[g, at])
+    reducer.finish()
     for k in range(1, 8):
         arrived(outgo.at[0], swap_send.at[k - 1])
     keep.wait()
 
 
-def reduce_units(grads, vectors, unit_of_slot, n_tensor, cap, groups):
-    n_units, _, width = grads.shape
-    piece = grads.shape[1] // (8 * n_tensor)
-    grads = grads.reshape(n_units, n_tensor, 2, 2, 2, piece, width)
-    n_groups = len(groups)
+def finish_reduce(grads, shard, grad_first, grad_hidden, tokens, shared, vectors, unit_of_slot, n_tensor, cap):
+    block = shard.shape[1:]
+    n_units = len(grads) + shard.shape[0]
+    rows, width = tokens.shape
     any_spec = pl.BlockSpec(memory_space=pl.ANY)
     vmem = pl.BlockSpec(memory_space=pltpu.VMEM)
     dma = pltpu.SemaphoreType.DMA
-    block = (piece, width)
-    out, vsum = pl.pallas_call(
-        functools.partial(reduce_kernel, groups, n_tensor),
-        out_shape=[
-            jax.ShapeDtypeStruct((cap, 8, *block), BF),
-            jax.ShapeDtypeStruct(vectors.shape, F32),
-        ],
-        in_specs=[pl.BlockSpec(memory_space=pltpu.SMEM), any_spec, vmem],
-        out_specs=[vmem, vmem],
+    shape = jax.ShapeDtypeStruct
+    out, vsum, input_grad = pl.pallas_call(
+        functools.partial(finish_kernel, n_tensor),
+        out_shape=[shape((cap, 8, *block), BF), shape(vectors.shape, F32), shape((rows, width), F32)],
+        in_specs=[pl.BlockSpec(memory_space=pltpu.SMEM)] + [any_spec] * 4 + [vmem] * 6,
+        out_specs=[vmem, vmem, vmem],
         scratch_shapes=[
-            pltpu.VMEM((n_units, n_tensor, 2, 2, *block), BF),
-            pltpu.VMEM((n_units, n_tensor, 2, 2, *block), BF),
-            pltpu.VMEM((n_units, n_tensor, 2, *block), BF),
-            pltpu.VMEM((n_units, n_tensor, *block), BF),
-            pltpu.VMEM((n_units, n_tensor, *block), BF),
-            pltpu.VMEM((n_units, n_tensor, *block), BF),
+            *Reducer.scratch(len(grads), 2, 2, 2, n_tensor, block),
             pltpu.VMEM((n_units, *block), BF),
             pltpu.VMEM((8, cap, *block), BF),
             pltpu.VMEM((3, *vectors.shape), F32),
             pltpu.VMEM((n_tensor - 1, *vectors.shape), F32),
-            dma((n_groups,)), dma((n_groups,)), dma((n_groups,)),
-            dma((n_groups, n_tensor)), dma((n_groups, n_tensor)),
-            dma((n_groups, n_tensor)), dma((n_groups, n_tensor)),
-            dma((n_groups, n_tensor)), dma((n_groups, n_tensor, 2)),
             dma((7,)), dma((7,)), dma((2 + n_tensor,)), dma((2 + n_tensor,)), dma((1,)),
         ],
-        compiler_params=pltpu.CompilerParams(collective_id=1, has_side_effects=True, vmem_limit_bytes=56 << 20),
-        name="reduce_units",
-    )(unit_of_slot, grads, vectors)
-    return out.reshape(cap, -1, width), vsum
+        compiler_params=pltpu.CompilerParams(collective_id=2, has_side_effects=True, vmem_limit_bytes=48 << 20),
+        name="finish_reduce",
+    )(unit_of_slot, *grads, shard, grad_first, grad_hidden, tokens, shared, vectors)
+    return out.reshape(cap, -1, width), vsum, input_grad
+
+
+def feed_forward_kernel(
+    hidden_ref, dy_ref, shared_ref, bias_ref, fc_ref, proj_ref,
+    out_ref, grad_ref, low_ref, fc_grad_ref, proj_grad_ref, fc_bias_ref, sums_ref,
+    second_ref, acc_ref,
+):
+    step = pl.program_id(0)
+
+    @pl.when(step == 0)
+    def _():
+        normed, _, _ = norm_rows(hidden_ref[...], shared_ref[3:4, :], shared_ref[4:5, :])
+        second_ref[...] = normed.astype(BF)
+        out_ref[...] = hidden_ref[...] + shared_ref[5:6, :]
+        acc_ref[...] = jnp.zeros_like(acc_ref)
+
+    dy, second = dy_ref[...], second_ref[...]
+    pre = rows_by_rows(second, fc_ref[...]) + bias_ref[0]
+    cube = pre * pre
+    inner = jnp.tanh(GELU_A * (pre + GELU_B * (cube * pre)))
+    half = 0.5 * pre
+    activ = (half + half * inner).astype(BF)
+    slope = 0.5 + 0.5 * inner + half * (1.0 - inner * inner) * (GELU_A + (3.0 * GELU_A * GELU_B) * cube)
+    out_ref[...] += plain_dot(activ, proj_ref[...])
+    proj_grad_ref[...] = cols_by_cols(activ, dy).astype(BF)
+    grad_pre = (rows_by_rows(dy, proj_ref[...]) * slope).astype(BF)
+    fc_bias_ref[0] = jnp.sum(grad_pre.astype(F32), axis=0, keepdims=True)
+    fc_grad_ref[...] = cols_by_cols(grad_pre, second).astype(BF)
+    acc_ref[...] += plain_dot(grad_pre, fc_ref[...])
+
+    @pl.when(step == pl.num_programs(0) - 1)
+    def _():
+        _, hat, inverse = norm_rows(hidden_ref[...], 1.0, 0.0)
+        grad_second, grad_y = acc_ref[...], dy.astype(F32)
+        grad = grad_y + norm_back(grad_second, hat, inverse, shared_ref[3:4, :])
+        low = grad.astype(BF)
+        grad_ref[...] = grad
+        low_ref[...] = low
+        for n, rows in enumerate((low.astype(F32), grad_second * hat, grad_second, grad_y)):
+            sums_ref[n : n + 1, :] = jnp.sum(rows, axis=0, keepdims=True)
+
+
+def feed_forward(hidden, out_grad, shared, b_fc, w_fc, w_proj):
+    rows, width = hidden.shape
+    tile = 256
+    steps = w_fc.shape[0] // tile
+    whole = lambda *dims: pl.BlockSpec(dims, lambda i: (0,) * len(dims))
+    strip = pl.BlockSpec((tile, width), lambda i: (i, 0))
+    bias = pl.BlockSpec((1, 1, tile), lambda i: (i, 0, 0))
+    shape = jax.ShapeDtypeStruct
+    out = pl.pallas_call(
+        feed_forward_kernel,
+        grid=(steps,),
+        in_specs=[whole(rows, width), whole(rows, width), whole(*shared.shape), bias, strip, strip],
+        out_specs=[whole(rows, width)] * 3 + [strip, strip, bias, whole(4, width)],
+        out_shape=[
+            shape((rows, width), F32), shape((rows, width), F32), shape((rows, width), BF),
+            shape(w_fc.shape, BF), shape(w_proj.shape, BF), shape((steps, 1, tile), F32), shape((4, width), F32),
+        ],
+        scratch_shapes=[pltpu.VMEM((rows, width), BF), pltpu.VMEM((rows, width), F32)],
+        compiler_params=pltpu.CompilerParams(vmem_limit_bytes=48 << 20),
+        name="feed_forward",
+    )(hidden, out_grad, shared, b_fc.reshape(steps, 1, tile), w_fc, w_proj)
+    return (*out[:5], out[5].reshape(-1), out[6])
 
 
 def per_device(
@@ -842,76 +1188,61 @@
         hidden = inputs_f32 + (plain_dot(attended, w_out) + shared[2])
     swap = (lambda v: v.swapaxes(0, 1)) if own_kernels else (lambda v: v)
     b_fc = swap(all_bias[:, 3 * head_rows :].reshape(n_tensor, -1, unit_rows)).reshape(-1)
-    normed_two, hat_two, inverse_two = norm_rows(hidden, shared[3], shared[4])
-    second_low = normed_two.astype(BF)
-    pre_act = rows_by_rows(second_low, w_fc) + b_fc
-    activ, gelu_back = jax.vjp(gelu_tanh, pre_act)
-    activ_low = activ.astype(BF)
-    layer_out = hidden + (plain_dot(activ_low, w_proj) + shared[5])
-
-    grad_y = out_grad.astype(F32)
-    grad_proj_w = cols_by_cols(activ_low, out_grad)
-    grad_activ = rows_by_rows(out_grad, w_proj)
-    grad_pre_low = gelu_back(grad_activ)[0].astype(BF)
-    grad_fc_b = jnp.sum(grad_pre_low, axis=0, dtype=F32)
-    grad_fc_w = cols_by_cols(grad_pre_low, second_low)
-    grad_second = plain_dot(grad_pre_low, w_fc)
-    grad_hidden = grad_y + norm_back(grad_second, hat_two, inverse_two, shared[3])
-    grad_hidden_low = grad_hidden.astype(BF)
-    grad_out_w = cols_by_cols(attended, grad_hidden_low)
+    layer_out, grad_hidden, grad_hidden_low, grad_fc_w, grad_proj_w, grad_fc_b, shared_rows = feed_forward(
+        hidden, out_grad, shared, b_fc, w_fc, w_proj
+    )
+    grad_out_w = cols_by_cols(attended, grad_hidden_low).astype(BF)
     grad_attended = rows_by_rows(grad_hidden_low, w_out).astype(BF)
-    grad_q, grad_k, grad_v = attend_backward(
-        q_scaled, keys_in, values_in, attended, grad_attended, log_norms, first_seen
-    )
-    grad_q_w = cols_by_cols(grad_q, normed_low)
-    grad_k_w = cols_by_cols(grad_k, normed_all)
-    grad_v_w = cols_by_cols(grad_v, normed_all)
-    grad_wide = plain_dot(grad_k, w_k) + plain_dot(grad_v, w_v)
-    grad_first = grad_wide[reach:] + plain_dot(grad_q, w_q)
-    for r in range(1, min(back, n_tensor - 1) + 1):
-        away = grad_wide[reach - r * rows_here : reach - (r - 1) * rows_here].astype(BF)
-        grad_first += lax.ppermute(away, "tensor", [(i, i - r) for i in range(r, n_tensor)]).astype(F32)
-    input_grad = grad_hidden + norm_back(grad_first, hat_one, inverse_one, shared[0])
-
     head_here = jnp.max(peaks, axis=2).reshape(-1)
-    grad_qkv_b = [jnp.sum(g, axis=0, dtype=F32) for g in (grad_q, grad_k, grad_v)]
-    shared_part = jnp.stack(
-        [
-            jnp.sum(grad_first * hat_one, axis=0),
-            jnp.sum(grad_first, axis=0),
-            jnp.sum(grad_hidden_low, axis=0, dtype=F32),
-            jnp.sum(grad_second * hat_two, axis=0),
-            jnp.sum(grad_second, axis=0),
-            jnp.sum(grad_y, axis=0),
-        ]
-    )
-    by_tensor = lambda v: v.reshape(n_tensor, -1)
-    fc_shape = (-1, n_tensor, unit_rows) if own_kernels else (n_tensor, -1, unit_rows)
-    grad_fc_b = swap(grad_fc_b.reshape(fc_shape))
-    bias_part = jnp.concatenate([by_tensor(v) for v in (*grad_qkv_b, grad_fc_b)], axis=1)
     if own_kernels:
-        head_row = jnp.pad(head_here, (0, width - head_here.shape[0]))[None]
-        vectors = jnp.concatenate([shared_part, bias_part.reshape(-1, width), head_row], axis=0)
-        vectors = jnp.pad(vectors, ((0, 16 - vectors.shape[0]), (0, 0)))
-        grad_units = jnp.concatenate(
-            [g.astype(BF) for g in (grad_q_w, grad_k_w, grad_v_w, grad_out_w, grad_fc_w, grad_proj_w)], axis=0
-        ).reshape(n_units, -1, width)
-        my_grads, totals = reduce_units(
-            grad_units, vectors, unit_of_slot, n_tensor, slot_cap, unit_groups(n_units)[::-1]
+        in_blocks = lambda g: g.reshape(-1, n_tensor, 2, 2, 2, unit_rows // 8, width)
+        shard, grad_first, grad_q_w, grad_k_w, grad_v_w, sums = backward_reduce(
+            in_blocks(grad_proj_w), in_blocks(grad_fc_w), q_scaled, keys_in, values_in, attended, grad_attended,
+            log_norms, first_seen, normed_all, w_att.reshape(-1, width), n_tensor, back,
+        )
+        vectors = jnp.concatenate(
+            [
+                jnp.zeros((2, width), F32), shared_rows, sums, grad_fc_b.reshape(-1, width),
+                jnp.pad(head_here, (0, width - head_here.shape[0]))[None], jnp.zeros((2, width), F32),
+            ],
+            axis=0,
+        )
+        grads = [in_blocks(g) for g in (grad_q_w, grad_k_w, grad_v_w, grad_out_w)]
+        my_grads, totals, input_grad = finish_reduce(
+            grads, shard, grad_first, grad_hidden, tokens_in, shared, vectors, unit_of_slot, n_tensor, slot_cap
         )
         my_grads = my_grads.astype(F32)
-        shared_grad, bias_total = totals[:6], totals[6:MAX_ROW].reshape(n_tensor, -1)
+        shared_grad = totals[:6]
         head_all = totals[MAX_ROW, : head_here.shape[0]]
+        bias_total = totals[6:MAX_ROW].reshape(-1, n_tensor, unit_rows)
+        bias_grad = lax.dynamic_index_in_dim(bias_total, tensor_index, 1, keepdims=False).reshape(-1)
     else:
+        grad_q, grad_k, grad_v = attend_backward(
+            q_scaled, keys_in, values_in, attended, grad_attended, log_norms, first_seen
+        )
+        grad_q_w = cols_by_cols(grad_q, normed_low)
+        grad_k_w = cols_by_cols(grad_k, normed_all)
+        grad_v_w = cols_by_cols(grad_v, normed_all)
+        grad_wide = plain_dot(grad_k, w_k) + plain_dot(grad_v, w_v)
+        grad_first = grad_wide[reach:] + plain_dot(grad_q, w_q)
+        for r in range(1, min(back, n_tensor - 1) + 1):
+            away = grad_wide[reach - r * rows_here : reach - (r - 1) * rows_here].astype(BF)
+            grad_first += lax.ppermute(away, "tensor", [(i, i - r) for i in range(r, n_tensor)]).astype(F32)
+        input_grad = grad_hidden + norm_back(grad_first, hat_one, inverse_one, shared[0])
+        grad_qkv_b = [jnp.sum(g, axis=0, dtype=F32) for g in (grad_q, grad_k, grad_v)]
+        first_rows = jnp.stack([jnp.sum(grad_first * hat_one, axis=0), jnp.sum(grad_first, axis=0)])
+        shared_part = jnp.concatenate([first_rows, shared_rows], axis=0)
+        by_tensor = lambda v: v.reshape(n_tensor, -1)
+        bias_part = jnp.concatenate([by_tensor(v) for v in (*grad_qkv_b, grad_fc_b)], axis=1)
         head_all = lax.pmax(head_here, ("dp", "tensor"))
         shared_grad, bias_total = lax.psum((shared_part, bias_part), ("dp", "tensor"))
+        bias_grad = lax.dynamic_index_in_dim(bias_total, tensor_index, 0, keepdims=False)
         by_stack = lambda g: g.astype(BF).reshape(n_tensor, -1, width)
         grad_units = jnp.concatenate(
             [by_stack(g) for g in (grad_q_w, grad_k_w, grad_v_w, grad_out_w, grad_fc_w, grad_proj_w)], axis=1
         ).reshape(units.shape)
         my_grads = scatter_units(grad_units, unit_of_slot).astype(F32)
     head_peak = lax.dynamic_slice_in_dim(head_all, tensor_index * heads_here, heads_here)
-    bias_grad = lax.dynamic_index_in_dim(bias_total, tensor_index, 0, keepdims=False)
 
     my_units = lax.dynamic_slice_in_dim(unit_of_slot, data_index * slot_cap, slot_cap, 0)
     my_occupied = lax.dynamic_slice_in_dim(occupied, data_index * slot_cap, slot_cap, 0)[:, None, None]

time: 582 us -> 492 us (0.85); the launches traced: 574 us -> 492 us
  matrix products: 102 us -> 4.87 us
  Pallas kernels: 404 us -> 458 us
  waiting for transfers between devices: 16.1 us -> 0 us
  starting transfers between devices: 11.1 us -> 0 us
  other arithmetic: 26.2 us -> 18.8 us
    pallas_call x2 -> x3, Pallas kernels: 246 us -> 300 us  [the longest x1 161 us: backward_reduce(): pl.pallas_call(functools.partial(backward_kernel, n_tensor, back, 1.0 / m...]
    dot_general x5 -> x0, matrix products: 38.5 us -> none  [plain_dot(): return jnp.dot(left, right, preferred_element_type=F32)]
    dot_general x6 -> x1, matrix products: 35.6 us -> 2.62 us  [cols_by_cols(): lax.dot_general(left, right, (((0,), (0,)), ((), ())), preferred_element_...]
    dot_general x3 -> x1, matrix products: 28.1 us -> 2.26 us  [rows_by_rows(): lax.dot_general(left, right, (((1,), (1,)), ((), ())), preferred_element_...]
    ppermute x2 -> x0, waiting for transfers between devices: 16.1 us -> none  [per_device(): lax.ppermute(away, 'tensor', [(i, i - r) for i in range(r, n_tensor)])]
    ppermute x2 -> x0, starting transfers between devices: 11.1 us -> none  [per_device(): lax.ppermute(away, 'tensor', [(i, i - r) for i in range(r, n_tensor)])]
  transfers between devices with their start and end apart: 2 -> 0, of which waited for: 1 -> 0; matrix products, arithmetic and copies ran while one was open for 9% -> 0% of each run, Pallas kernels for 0% -> 0%
where the time goes in v4:
time: 492 us
  Pallas kernels  458 us (93%)
  other arithmetic  18.8 us (4%)
  local copies, waits for them, and re-layouts  9.27 us (2%)
    pallas_call x1, Pallas kernels, backward_reduce(): pl.pallas_call(functools.partial(backward_kernel, n_tensor, back, 1.0 / m...  161 us
    pallas_call x1, Pallas kernels, forward_spread(): pl.pallas_call(functools.partial(forward_kernel, n_tensor, back, 1.0 / ma...  158 us
    pallas_call x1, Pallas kernels, finish_reduce(): pl.pallas_call(functools.partial(finish_kernel, n_tensor), out_shape=[sha...  83.2 us
    pallas_call x1, Pallas kernels, feed_forward(): pl.pallas_call(feed_forward_kernel, grid=(steps,), in_specs=[whole(rows,...  55.9 us

profile of v4, /device:TPU:9, one launch (start us, length us, event | category | flops | bytes accessed | tf_op | source)
XLA Modules:
  0.0 491.7 jit_solution(9821661328236090813)
XLA Ops:
  0.7 0.9 select_reduce_fusion.3
  1.5 0.1 select_reduce_fusion.2
  1.6 0.6 subtract_add_fusion
  2.2 0.8 fusion.19
  3.1 1.6 convert_reduce_fusion
  4.7 1.6 fusion.2
  6.3 1.4 fusion.5.a_ref
  7.8 0.6 slice_bitcast_fusion.shared_ref
  8.4 0.2 convert_reduce_fusion.1
  8.6 0.5 multiply_add_fusion.slot_ref
  9.1 1.1 convert_element_type.48
  10.2 0.6 slice_reduce_fusion
  10.8 158.1 %forward_spread.1 = (bf16[4,4,4,2,32,1024]{5,4,3,2,1,0:T(8,128)(2,1)}, bf16[4,4,4,2,32,1024]{5,4,3,2,1,0:T(8,128)(2,1)}, bf16[4,4,4,2,32,1024]{5,4,3,2,1,0:T(8,1...) custom-call(s32[12]{0:T(128)} %multiply_add_fusion.slot_ref, ...), custom_call_target="tpu_custom_call" | custom-call | tf_op jit(solution)/shard_map/forward_spread/pallas_call | solution.py:545
  168.9 0.8 copy.29
  169.7 55.9 %feed_forward.1 = (f32[512,1024]{1,0:T(8,128)}, f32[512,1024]{1,0:T(8,128)S(1)}, bf16[512,1024]{1,0:T(8,128)(2,1)S(1)}, bf16[4096,1024]{1,0:T(8,128)(2,1)}, bf16...) custom-call(f32[512,1024]{1,0:T(8,128)} %get-tuple-element.41.hidden_ref, ...), custom_call_target="tpu_custom_call" | custom-call | tf_op jit(solution)/shard_map/feed_forward/pallas_call | solution.py:1102
  225.6 2.6 slice.50
  228.2 2.3 convolution_convert_fusion.1.do_ref
  230.5 160.7 %backward_reduce.1 = (bf16[8,32,1024]{2,1,0:T(8,128)(2,1)}, f32[512,1024]{1,0:T(8,128)}, bf16[1024,1024]{1,0:T(8,128)(2,1)}, bf16[1024,1024]{1,0:T(8,128)(2,1)},...) custom-call(bf16[4,4,2,2,2,32,1024]{6,5,4,3,2,1,0:T(8,128)(2,1)} %bitcast.72, ...), custom_call_target="tpu_custom_call" | custom-call | tf_op jit(solution)/shard_map/backward_reduce/pallas_call | solution.py:923
  391.3 0.1 reduce_max.19
  391.5 0.9 concatenate.3.v_ref
  392.5 2.6 convolution_convert_fusion
  395.1 0.1 select_reduce_fusion.1.unit_ref
  395.2 83.2 %finish_reduce.1 = (bf16[2,8,32,1024]{3,2,1,0:T(8,128)(2,1)S(1)}, f32[16,1024]{1,0:T(8,128)S(1)}, f32[512,1024]{1,0:T(8,128)S(1)}) custom-call(s32[16]{0:T(128)S(1)} %select_reduce_fusion.1.unit_ref, bf16[1,4,2,2,2,32,1024]{6,5,4,3,2,1,0:T(8,128)(2,1)} %bitcast.76, bf16[1,4,2,2,2,32,1024]{6,5,4,3,2,1,0:T(8,128)(2,1)} %bitcast.77, ...), custom_call_target="tpu_custom_call" | custom-call | tf_op jit(solution)/shard_map/finish_reduce/pallas_call | solution.py:1035
  478.4 0.7 bitcast_subtract_fusion
  479.1 0.6 broadcast_in_dim.103
  479.7 0.7 multiply_subtract_fusion
  480.4 0.7 copy.26
  481.1 0.6 divide_sqrt_fusion
  481.7 0.1 compare_select_fusion
  482.0 0.1 fusion.11
  482.2 8.2 %multiply_select_fusion = (f32[1,2,256,1024]{3,2,1,0:T(8,128)}, f32[1,2,256,1024]{3,2,1,0:T(8,128)}, f32[1,2,256,1024]{3,2,1,0:T(8,128)}, f32[1,2,256,1024]{3,2,1,0:T(8,128)}) fusion(f32[1,2,256,1024]{3,2,1,0:T(8,128)} %param.13, bf16[1,2,256,1024]{3,2,1,0:T(8,128)(2,1)S(1)} %bitcast.67, f32[1,2,256,1024]{3,2,1,0:T(8,128)} %param.14, ...), kind=kLoop, calls=%fused_computation.14 | loop fusion | flops 11010048 | bytes 15730690 | tf_op jit(solution)/shard_map/jit(_where)/select_n | solution.py:1260
  490.3 1.3 copy.31
  (46 shorter events, 0.6 us)
Async XLA Ops:
  0.6 5.7 %copy-start = (bf16[512,1024]{1,0:T(8,128)(2,1)S(1)}, bf16[512,1024]{1,0:T(8,128)(2,1)}, u32[]{:S(2)}) copy-start(bf16[512,1024]{1,0:T(8,128)(2,1)} %x_ref.3) | copy-start | bytes 3145732
  3.0 4.7 copy-start.8
  3.1 5.3 %copy-start.12 = (s32[12]{0:T(128)S(1)}, s32[12]{0:T(128)}, u32[]{:S(2)}) copy-start(s32[12]{0:T(128)} %param.12) | copy-start | bytes 148
  3.1 6.0 %copy-start.6 = (f32[1,2,256,1024]{3,2,1,0:T(8,128)S(1)}, f32[1,2,256,1024]{3,2,1,0:T(8,128)}, u32[]{:S(2)}) copy-start(f32[1,2,256,1024]{3,2,1,0:T(8,128)} %param.13) | copy-start | bytes 6291460
  7.8 2.5 copy-start.9
  10.2 159.5 %copy-start.3 = (bf16[512,1024]{1,0:T(8,128)(2,1)S(1)}, bf16[512,1024]{1,0:T(8,128)(2,1)}, u32[]{:S(2)}) copy-start(bf16[512,1024]{1,0:T(8,128)(2,1)} %dy_ref.1) | copy-start | bytes 3145732
  10.2 159.5 %copy-start.4 = (f32[6,1024]{1,0:T(8,128)S(1)}, f32[6,1024]{1,0:T(8,128)}, u32[]{:S(2)}) copy-start(f32[6,1024]{1,0:T(8,128)} %slice_bitcast_fusion.shared_ref) | copy-start | bytes 73732
  225.6 2.6 copy-start.2
  230.5 160.8 %copy-start.10 = (f32[8,2,512]{2,1,0:T(2,128)S(1)}, f32[8,2,512]{2,1,0:T(2,128)}, u32[]{:S(2)}) copy-start(f32[8,2,512]{2,1,0:T(2,128)} %get-tuple-element.65) | copy-start | bytes 98308
  230.5 161.9 %copy-start.7 = (bf16[512,1024]{1,0:T(8,128)(2,1)S(1)}, bf16[512,1024]{1,0:T(8,128)(2,1)}, u32[]{:S(2)}) copy-start(bf16[512,1024]{1,0:T(8,128)(2,1)} %get-tuple-element.51.o_ref) | copy-start | bytes 3145732
  392.4 2.7 copy-start.11
  392.4 2.8 copy-start.1
  392.4 2.7 copy-start.5

commit v5 on v4

--- a/solution.py
+++ b/solution.py
@@ -313,12 +313,38 @@
         o_ref[rows, lanes] = jnp.concatenate(outs, axis=0).T.astype(BF)
 
 
+def paired(n_units):
+    half = (n_units - 4) // 2
+    return [0, 1, 2, 3] + [4 + i + half * b for i in range(half) for b in range(2)]
+
+
+def gelu_parts(pre):
+    square = pre * pre
+    inner = jnp.tanh(GELU_A * (pre + GELU_B * (square * pre)))
+    half = 0.5 * pre
+    slope = 0.5 + 0.5 * inner + half * (1.0 - inner * inner) * (GELU_A + (3.0 * GELU_A * GELU_B) * square)
+    return half + half * inner, slope
+
+
+ORDER = (
+    "o2", "g0d", "o0", "z00d", "g0u", "z01d", "z02d", "z00u", "z01u", "f01d", "g2d", "z02u", "f01u", "t0", "g1d",
+    "f0o", "f02d", "f02u", "f00d", "f00u", "e01u", "e01d", "z10d", "e00d", "e0o", "e02u", "o1", "d2", "e02d",
+    "e00u", "g1u", "d0", "f1o", "d1", "d3", "Q", "Q", "Q", "g2u", "t1", "z20d", "Q", "z11d", "K", "K", "K", "K",
+    "z10u", "V", "V", "V", "z20u", "V", "A", "z11u", "z21d", "A", "A", "z21u", "z22d", "A", "f11d", "z12u",
+    "f10u", "A", "z12d", "f11u", "f10d", "A", "e1o", "A", "z22u", "A", "f20d", "f12u", "f20u", "e10u", "e11u",
+    "e11d", "f12d", "f2o", "O", "e10d", "F", "e12u", "f21u", "f22d", "F", "e12d", "e20d", "F", "f21d", "e2o",
+    "e22d", "e20u", "F", "f22u", "F", "F", "F", "F", "e21u", "e21d", "F", "e22u", "F", "F", "F", "F", "F",
+)
+
+
 def forward_kernel(
     n_tensor, back, scale,
-    slot_ref, master_ref, a_ref, x_ref, bias_in_ref, first_ref, shared_ref,
-    att_ref, fc_ref, proj_ref, wide_ref, biases_ref, q_ref, k_ref, v_ref, o_ref, lse_ref, peak_ref, hidden_ref,
-    pieces, own, seen_ref, bias_rows, swap_send, swap_recv, local_sem, a_send, a_recv, bias_send, bias_recv,
-    z_send, z_recv, xy_send, xy_recv, core_send, core_recv,
+    slot_ref, master_ref, a_ref, x_ref, dy_ref, bias_in_ref, first_ref, shared_ref,
+    att_ref, ff_ref, wide_ref, q_ref, k_ref, v_ref, o_ref, lse_ref, peak_ref,
+    out_ref, grad_ref, do_ref, ff_grad_ref, go_ref, fc_bias_ref, sums_ref,
+    pieces, own, seen_ref, bias_rows, biases_ref, fc_rows, hidden_ref, second_ref, acc_ref, tiles_in, stage,
+    swap_send, swap_recv, local_sem, a_send, a_recv, bias_send, bias_recv,
+    z_send, z_recv, xy_send, xy_recv, core_send, core_recv, tile_sem, stage_sem,
 ):
     d, t, core, x, y = place()
     column = y * 2 + x
@@ -326,10 +352,11 @@
     sibling = d + 1 - 2 * core
     first, last = t > 0, t < n_tensor - 1
     rows_here, width = a_ref.shape
-    weights = (att_ref, fc_ref, proj_ref)
-    starts = [0]
-    for w in weights:
-        starts.append(starts[-1] + w.shape[0])
+    n_half = ff_ref.shape[0] // 2
+    weights = (att_ref, ff_ref.at[pl.ds(0, n_half)], ff_ref.at[pl.ds(n_half, n_half)])
+    starts = (0, 4, 4 + n_half, 4 + 2 * n_half)
+    n_groups, steps = len(weights), n_tensor - 1
+    slots = 2 * n_tensor - 1
     greet(d, t, n_tensor)
 
     def tokens_up(r):
@@ -345,10 +372,10 @@
         if r + 1 < back:
             tokens_up(r + 1)
 
-    tokens_up(0)
     for k in range(1, 8):
         to = (d + k) % 8
         send(master_ref.at[:, to], pieces.at[d], swap_send.at[k - 1], swap_recv.at[k - 1], (to, t))
+    tokens_up(0)
     mine = pltpu.make_async_copy(master_ref.at[:, d], pieces.at[d], local_sem.at[0])
     mine.start()
     for k in range(1, n_tensor):
@@ -364,9 +391,9 @@
     for k in range(1, 8):
         arrived(pieces.at[(d + 8 - k) % 8], swap_recv.at[k - 1])
     cap = master_ref.shape[0]
-    for u in range(own.shape[0]):
+    for n, u in enumerate(paired(own.shape[0])):
         slot = slot_ref[u]
-        own[u] = pieces[slot // cap, slot % cap]
+        own[n] = pieces[slot // cap, slot % cap]
 
     def block(g, at, col, c):
         return weights[g].at[:, at, col, c]
@@ -398,73 +425,82 @@
 
     def done(g, k, at):
         arrived(weights[g].at[:, at, :, 1 - core], core_recv.at[g, k])
+
+    def given(g, k, at):
         arrived(weights[g].at[:, at, :, core], core_send.at[g, k])
 
-    def z_go(g, s, up, source, at):
+    def z_go(g, s, up, source):
         i = 0 if up else 1
 
         @pl.when(last if up else first)
         def _():
-            send(source, block(g, at, column, core), z_send.at[g, i, s], z_recv.at[g, i, s], (d, t + 1 if up else t - 1))
+            here = block(g, t if s == 0 else (t - s if up else t + s), column, core)
+            send(source, here, z_send.at[g, i, s], z_recv.at[g, i, s], (d, t + 1 if up else t - 1))
 
     def z_step(s, up):
         at = t - 1 - s if up else t + 1 + s
         return 1 + 2 * s + (0 if up else 1), at, (at >= 0) if up else (at < n_tensor)
 
-    def z_event(g, s):
-        for up in (True, False):
-            k, at, have = z_step(s, up)
-
-            @pl.when(have)
-            def _(k=k, at=at, up=up):
-                got = block(g, at, column, core)
-                arrived(got, z_recv.at[g, 0 if up else 1, s])
-                if s + 1 < n_tensor - 1:
-                    z_go(g, s + 1, up, got, at)
-                onward(g, k, at, got)
+    def z_event(g, s, up):
+        k, at, have = z_step(s, up)
+
+        @pl.when(have)
+        def _():
+            got = block(g, at, column, core)
+            arrived(got, z_recv.at[g, 0 if up else 1, s])
+            if s + 1 < steps:
+                z_go(g, s + 1, up, got)
+            onward(g, k, at, got)
+
+    def step(fn, g, s, up):
+        k, at, have = z_step(s, up)
+        pl.when(have)(functools.partial(fn, g, k, at))
 
     def each(fn, g, s):
         if s < 0:
             fn(g, 0, t)
         else:
             for up in (True, False):
-                k, at, have = z_step(s, up)
-                pl.when(have)(functools.partial(fn, g, k, at))
-
-    n_groups, steps = len(weights), n_tensor - 1
+                step(fn, g, s, up)
+
     local = []
+    mine_of = [own.at[starts[g] : starts[g + 1]] for g in range(n_groups)]
     for g in range(n_groups):
-        source = own.at[starts[g] : starts[g + 1]]
-        for up in (True, False):
-            z_go(g, 0, up, source, t)
-        copy = pltpu.make_async_copy(source, block(g, t, column, core), local_sem.at[1 + g])
+        copy = pltpu.make_async_copy(mine_of[g], block(g, t, column, core), local_sem.at[1 + g])
         copy.start()
         local.append(copy)
-        onward(g, 0, t, source)
-
-    def chain(g):
-        events = []
-        for s in range(steps + 2):
-            if s < steps:
-                events.append(functools.partial(z_event, g, s))
-            if s <= steps:
-                events.append(functools.partial(each, forward, g, s - 1))
-            if s >= 1:
-                if s == 1:
-                    events.append(local[g].wait)
-                events.append(functools.partial(each, settle, g, s - 2))
-        return events
-
-    events = chain(0)
-    for r in range(back):
-        events.insert(1 + 4 * r, functools.partial(tokens_in, r))
-    early = [functools.partial(z_event, g, 0) for g in range(1, n_groups)]
-    events[3:3] = early
-    for event in events:
+
+    def own_settled(g):
+        local[g].wait()
+        settle(g, 0, t)
+
+    by_code = {f"t{r}": functools.partial(tokens_in, r) for r in range(back)}
+    by_code |= {f"d{s + 1}": functools.partial(each, done, 0, s) for s in range(-1, steps)}
+    for g in range(n_groups):
+        by_code[f"o{g}"] = functools.partial(onward, g, 0, t, mine_of[g])
+        by_code[f"f{g}o"] = functools.partial(forward, g, 0, t)
+        by_code[f"e{g}o"] = functools.partial(own_settled, g)
+        for way, up in (("u", True), ("d", False)):
+            by_code[f"g{g}{way}"] = functools.partial(z_go, g, 0, up, mine_of[g])
+            for s in range(steps):
+                by_code[f"z{g}{s}{way}"] = functools.partial(z_event, g, s, up)
+                by_code[f"f{g}{s}{way}"] = functools.partial(step, forward, g, s, up)
+                by_code[f"e{g}{s}{way}"] = functools.partial(step, settle, g, s, up)
+    tile = 256
+    tiles = width // tile
+    early, during = [], {}
+    counts = {"Q": tiles, "K": tiles, "V": tiles, "A": width // PAIR, "O": 1, "F": 2 * slots}
+    now, seen = None, 0
+    for code in ORDER:
+        if code in counts:
+            now, seen = code, 0 if code != now else seen + 1
+            during.setdefault(code, {})
+        elif now is None:
+            early.append(by_code[code])
+        else:
+            during[now].setdefault(seen, []).append(by_code[code])
+    for event in early:
         event()
-    late = []
-    for g in range(1, n_groups):
-        late += chain(g)[1:]
     for k in range(1, n_tensor):
         arrived(biases_ref.at[(t + n_tensor - k) % n_tensor], bias_recv.at[k - 1])
         arrived(bias_in_ref, bias_send.at[k - 1])
@@ -474,42 +510,122 @@
             for i in range(per):
                 lanes = pl.ds((at * per + i) * 128, 128)
                 bias_rows[n : n + 1, lanes] = biases_ref[at, n * per + i : n * per + i + 1]
-    for s in range(-1, steps):
-        each(done, 0, s)
-
-    tile = 256
-
-    def project(n, source_ref, into_ref, factor):
+    strip = fc_rows.shape[-1]
+    for h in range(2):
+        for at in range(n_tensor):
+            for i in range(strip // 128):
+                row = 3 * per + h * (strip // 128) + i
+                fc_rows[h, at, 0:1, i * 128 : (i + 1) * 128] = biases_ref[at, row : row + 1]
+
+    def project(n, own_only, into_ref, factor):
         def body(i):
             cols = pl.ds(pl.multiple_of(i * tile, tile), tile)
             w = att_ref[n, pl.ds(i * tile // (width // n_tensor), 1)].reshape(tile, width)
             for r in range(into_ref.shape[0] // rows_here):
-                a = wide_ref[r] if source_ref is None else source_ref[...]
-                full = rows_by_rows(a, w) + bias_rows[n : n + 1, cols]
-                into_ref[r * rows_here : (r + 1) * rows_here, cols] = (full.astype(BF) * jnp.asarray(factor, BF)) if factor else full.astype(BF)
+                a = a_ref[...] if own_only else wide_ref[r]
+                full = (rows_by_rows(a, w) + bias_rows[n : n + 1, cols]).astype(BF)
+                into_ref[r * rows_here : (r + 1) * rows_here, cols] = full * jnp.asarray(factor, BF) if factor else full
         return body
 
-    tiles = width // tile
-    n_late = len(late)
-    cut = n_late // 5
-    loop_with(tiles, project(0, a_ref, q_ref, scale), {})
-    loop_with(tiles, project(1, None, k_ref, None), spaced(tiles, late[:cut]))
-    loop_with(tiles, project(2, None, v_ref, None), spaced(tiles, late[cut : 2 * cut]))
+    loop_with(tiles, project(0, True, q_ref, scale), during["Q"])
+    loop_with(tiles, project(1, False, k_ref, None), during["K"])
+    loop_with(tiles, project(2, False, v_ref, None), during["V"])
     loop_with(
         width // PAIR,
         lambda i: attend_pair(i, q_ref, k_ref, v_ref, o_ref, lse_ref, peak_ref, seen_ref),
-        spaced(width // PAIR, late[2 * cut :]),
+        during["A"],
     )
     w_out = att_ref[3].reshape(width, width)
     half = rows_here // 2
     for r in range(2):
         rows = pl.ds(r * half, half)
-        hidden_ref[rows, :] = x_ref[rows, :].astype(F32) + (plain_dot(o_ref[rows, :], w_out) + shared_ref[2:3, :])
+        hidden = x_ref[rows, :].astype(F32) + (plain_dot(o_ref[rows, :], w_out) + shared_ref[2:3, :])
+        hidden_ref[rows, :] = hidden
+        normed, _, _ = norm_rows(hidden, shared_ref[3:4, :], shared_ref[4:5, :])
+        second_ref[rows, :] = normed.astype(BF)
+        out_ref[rows, :] = hidden + shared_ref[5:6, :]
+    acc_ref[...] = jnp.zeros_like(acc_ref)
+
+    def tile_copies(h, at, b):
+        for i in range(n_half // 2):
+            yield pltpu.make_async_copy(
+                ff_ref.at[h * n_half + 2 * i + b, at], tiles_in.at[b, i], tile_sem.at[b, i]
+            )
+
+    def grad_copies(h, at):
+        for b in range(2):
+            for i in range(n_half // 2):
+                part = stage.at[b, i]
+                yield pltpu.make_async_copy(part, ff_grad_ref.at[h * n_half + 2 * i + b, at], stage_sem.at[b, i])
+
+    def feed(n):
+        h, k = n // slots, n % slots
+        at = t + (k + 1) // 2 * (1 - 2 * (k % 2))
+
+        @pl.when((at >= 0) & (at < n_tensor))
+        def _():
+            arrived(ff_ref.at[pl.ds(h * n_half, n_half), at, :, 1 - core], core_recv.at[1 + h, k])
+            for b in range(2):
+                for copy in tile_copies(h, at, b):
+                    copy.start()
+            for copy in tile_copies(h, at, 0):
+                copy.wait()
+            w_fc = tiles_in[0].reshape(strip, width)
+            second, dy = second_ref[...], dy_ref[...]
+            activ, slope = gelu_parts(rows_by_rows(second, w_fc) + fc_rows[h, at])
+            activ = activ.astype(BF)
+            for copy in tile_copies(h, at, 1):
+                copy.wait()
+            w_proj = tiles_in[1].reshape(strip, width)
+            grad_pre = (rows_by_rows(dy, w_proj) * slope).astype(BF)
+            out_ref[...] += plain_dot(activ, w_proj)
+            acc_ref[...] += plain_dot(grad_pre, w_fc)
+            fc_bias_ref[h, at] = jnp.sum(grad_pre.astype(F32), axis=0, keepdims=True)
+
+            @pl.when(n > 0)
+            def _():
+                for copy in grad_copies(h, at):
+                    copy.wait()
+
+            stage[0] = cols_by_cols(grad_pre, second).astype(BF).reshape(stage.shape[1:])
+            stage[1] = cols_by_cols(activ, dy).astype(BF).reshape(stage.shape[1:])
+            for copy in grad_copies(h, at):
+                copy.start()
+
+    for event in during["O"].get(0, []):
+        event()
+    loop_with(2 * slots, feed, during["F"])
+    for copy in grad_copies(0, 0):
+        copy.wait()
+
+    part = min(128, rows_here)
+    sums_ref[...] = jnp.zeros_like(sums_ref)
+
+    def norm_back_rows(i, carry):
+        rows = pl.ds(pl.multiple_of(i * part, part), part)
+        _, hat, inverse = norm_rows(hidden_ref[rows, :], 1.0, 0.0)
+        grad_second, grad_y = acc_ref[rows, :], dy_ref[rows, :].astype(F32)
+        grad = grad_y + norm_back(grad_second, hat, inverse, shared_ref[3:4, :])
+        low = grad.astype(BF)
+        grad_ref[rows, :] = grad
+        second_ref[rows, :] = low
+        for n, term in enumerate((low.astype(F32), grad_second * hat, grad_second, grad_y)):
+            sums_ref[n : n + 1, :] += jnp.sum(term, axis=0, keepdims=True)
+        return carry
+
+    lax.fori_loop(0, rows_here // part, norm_back_rows, 0)
+
+    def out_back(i):
+        cols = pl.ds(pl.multiple_of(i * tile, tile), tile)
+        w = att_ref[3, pl.ds(i * tile // (width // n_tensor), 1)].reshape(tile, width)
+        do_ref[:, cols] = rows_by_rows(second_ref[...], w).astype(BF)
+        go_ref[pl.ds(pl.multiple_of(i * tile, tile), tile), :] = cols_by_cols(o_ref[:, cols], second_ref[...]).astype(BF)
+
+    loop_with(tiles, out_back, {})
 
     for g in range(n_groups):
-        if g > 0:
-            for s in range(-1, steps):
-                each(done, g, s)
+        for s in range(-1, steps):
+            each(given, g, s)
         arrived(weights[g].at[:, :, pl.ds(0, 3), 0], xy_send.at[g])
         for up in (True, False):
             for s in range(steps):
@@ -528,13 +644,14 @@
         arrived(pieces.at[0], swap_send.at[k - 1])
 
 
-def forward_spread(master_low, normed_low, tokens, bias_row, first_seen, shared, slot_of_unit, n_tensor, back):
+def forward_spread(master_low, normed_low, tokens, out_grad, bias_row, first_seen, shared, slot_of_unit, n_tensor, back):
     cap, unit_rows, width = master_low.shape
     n_units = slot_of_unit.shape[0]
-    n_ff = (n_units - 4) // 2
+    n_ff = n_units - 4
     piece = unit_rows // 8
     rows = normed_low.shape[0]
     n_keys = (back + 1) * rows
+    strip = n_ff // 4 * unit_rows
     bias_row = bias_row.reshape(-1, 128)
     any_spec = pl.BlockSpec(memory_space=pl.ANY)
     vmem = pl.BlockSpec(memory_space=pltpu.VMEM)
@@ -542,35 +659,43 @@
     shape = jax.ShapeDtypeStruct
     units = lambda n: shape((n, n_tensor, 4, 2, piece, width), BF)
     stats = shape((width // PAIR, 2, rows), F32)
+    low, high = shape((rows, width), BF), shape((rows, width), F32)
+    keys = shape((n_keys, width), BF)
     outs = pl.pallas_call(
         functools.partial(forward_kernel, n_tensor, back, 1.0 / math.sqrt(HD)),
         out_shape=[
-            units(4), units(n_ff), units(n_ff),
-            shape((back + 1, rows, width), BF), shape((n_tensor, *bias_row.shape), F32),
-            shape((rows, width), BF), shape((n_keys, width), BF), shape((n_keys, width), BF), shape((rows, width), BF),
-            stats, stats, shape((rows, width), F32),
+            units(4), units(n_ff), shape((back + 1, rows, width), BF), low, keys, keys, low, stats, stats,
+            high, high, low, shape((n_ff, n_tensor, 4, 2, piece, width), BF), shape((width, width), BF),
+            shape((2, n_tensor, 1, strip), F32), shape((4, width), F32),
         ],
-        in_specs=[pl.BlockSpec(memory_space=pltpu.SMEM), any_spec, vmem, vmem, vmem, vmem, vmem],
-        out_specs=[vmem, any_spec, any_spec, vmem, vmem, vmem, vmem, vmem, vmem, vmem, vmem, vmem],
+        in_specs=[pl.BlockSpec(memory_space=pltpu.SMEM), any_spec] + [vmem] * 6,
+        out_specs=[vmem, any_spec] + [vmem] * 10 + [any_spec] + [vmem] * 3,
         scratch_shapes=[
             pltpu.VMEM((8, cap, piece, width), BF),
             pltpu.VMEM((n_units, piece, width), BF),
             pltpu.VMEM((n_keys, rows), F32),
             pltpu.VMEM((3, width), F32),
+            pltpu.VMEM((n_tensor, *bias_row.shape), F32),
+            pltpu.VMEM((2, n_tensor, 1, strip), F32),
+            pltpu.VMEM((rows, width), F32),
+            pltpu.VMEM((rows, width), BF),
+            pltpu.VMEM((rows, width), F32),
+            pltpu.VMEM((2, n_ff // 4, 4, 2, piece, width), BF),
+            pltpu.VMEM((2, n_ff // 4, 4, 2, piece, width), BF),
             dma((7,)), dma((7,)), dma((4,)), dma((back,)), dma((back,)),
             dma((n_tensor - 1,)), dma((n_tensor - 1,)),
             dma((3, 2, n_tensor - 1)), dma((3, 2, n_tensor - 1)),
             dma((3,)), dma((3, 2 * n_tensor - 1, 3)),
             dma((3, 2 * n_tensor - 1)), dma((3, 2 * n_tensor - 1)),
+            dma((2, n_ff // 4)), dma((2, n_ff // 4)),
         ],
-        compiler_params=pltpu.CompilerParams(collective_id=0, has_side_effects=True, vmem_limit_bytes=56 << 20),
+        compiler_params=pltpu.CompilerParams(collective_id=0, has_side_effects=True, vmem_limit_bytes=60 << 20),
         name="forward_spread",
-    )(slot_of_unit, master_low.reshape(cap, 8, piece, width), normed_low, tokens, bias_row, first_seen, shared)
-    att, fc, proj, wide, biases, q, k, v, o, lse, peaks, hidden = outs
-    return (
-        att.reshape(4, -1, width), fc.reshape(-1, width), proj.reshape(-1, width), wide.reshape(-1, width),
-        biases.reshape(n_tensor, -1), q, k, v, o, lse, peaks, hidden,
+    )(
+        slot_of_unit, master_low.reshape(cap, 8, piece, width), normed_low, tokens, out_grad, bias_row, first_seen, shared
     )
+    att, _, wide, *rest = outs
+    return att.reshape(-1, width), wide.reshape(-1, width), *rest
 
 
 def add_blocks(into, part, count):
@@ -751,7 +876,7 @@
 
 def backward_kernel(
     n_tensor, back, scale,
-    proj_ref, fc_ref, q_ref, k_ref, v_ref, o_ref, do_ref, lse_ref, first_ref, wide_ref, att_ref,
+    ff_grad_ref, q_ref, k_ref, v_ref, o_ref, do_ref, lse_ref, first_ref, wide_ref, att_ref,
     shard_ref, grad_ref, gq_ref, gk_ref, gv_ref, sums_ref, *scratch,
 ):
     reducer_scratch, (
@@ -760,9 +885,10 @@
     ) = scratch[:REDUCER], scratch[REDUCER:]
     d, t, core, x, y = place()
     greet(d, t, n_tensor)
-    n_fc = fc_ref.shape[0]
     other, near, one, two, up_in, down_in, *sems = reducer_scratch
-    reducer = Reducer([[fc_ref], [proj_ref]], n_tensor, other, near, one, two, up_in, down_in, shard_ref, sems)
+    half = ff_grad_ref.shape[0] // 2
+    groups = [[ff_grad_ref.at[pl.ds(0, half)]], [ff_grad_ref.at[pl.ds(half, half)]]]
+    reducer = Reducer(groups, n_tensor, other, near, one, two, up_in, down_in, shard_ref, sems)
     reducer.start()
     rows_here, width = do_ref.shape
     n_keys = k_ref.shape[0]
@@ -909,11 +1035,11 @@
     reducer.finish()
 
 
-def backward_reduce(grad_proj, grad_fc, q, k, v, o, do, lse, first_seen, wide, w_att, n_tensor, back):
+def backward_reduce(grad_ff, q, k, v, o, do, lse, first_seen, wide, w_att, n_tensor, back):
     rows, width = q.shape
     n_keys = k.shape[0]
-    n_ff = grad_fc.shape[0]
-    block = grad_fc.shape[-2:]
+    n_ff = grad_ff.shape[0]
+    block = grad_ff.shape[-2:]
     any_spec = pl.BlockSpec(memory_space=pl.ANY)
     vmem = pl.BlockSpec(memory_space=pltpu.VMEM)
     dma = pltpu.SemaphoreType.DMA
@@ -922,11 +1048,11 @@
     pair = lambda n: pltpu.VMEM((2, n, PAIR), BF)
     return pl.pallas_call(
         functools.partial(backward_kernel, n_tensor, back, 1.0 / math.sqrt(HD)),
-        out_shape=[shape((2 * n_ff, *block), BF), shape((rows, width), F32), square, square, square, shape((3, width), F32)],
-        in_specs=[any_spec] * 7 + [vmem, vmem] + [any_spec] * 2,
+        out_shape=[shape((n_ff, *block), BF), shape((rows, width), F32), square, square, square, shape((3, width), F32)],
+        in_specs=[any_spec] * 6 + [vmem, vmem] + [any_spec] * 2,
         out_specs=[vmem, vmem, any_spec, any_spec, any_spec, vmem],
         scratch_shapes=[
-            *Reducer.scratch(2 * n_ff, n_ff, 2, 1, n_tensor, block),
+            *Reducer.scratch(n_ff, n_ff // 2, 2, 1, n_tensor, block),
             pltpu.VMEM((n_keys, rows), F32),
             pair(rows), pair(n_keys), pair(n_keys), pair(rows), pair(rows),
             pltpu.VMEM((rows, width), BF), pltpu.VMEM((n_keys, width), BF), pltpu.VMEM((n_keys, width), BF),
@@ -938,7 +1064,7 @@
         ],
         compiler_params=pltpu.CompilerParams(collective_id=1, has_side_effects=True, vmem_limit_bytes=60 << 20),
         name="backward_reduce",
-    )(grad_proj, grad_fc, q, k, v, o, do, lse, first_seen, wide, w_att)
+    )(grad_ff, q, k, v, o, do, lse, first_seen, wide, w_att)
 
 
 def join(row, a, b):
@@ -1093,7 +1219,7 @@
 
 def feed_forward(hidden, out_grad, shared, b_fc, w_fc, w_proj):
     rows, width = hidden.shape
-    tile = 256
+    tile = 512
     steps = w_fc.shape[0] // tile
     whole = lambda *dims: pl.BlockSpec(dims, lambda i: (0,) * len(dims))
     strip = pl.BlockSpec((tile, width), lambda i: (i, 0))
@@ -1140,10 +1266,10 @@
     ff_rows = (n_units * unit_rows - 4 * head_rows) // 2
     slot_of_unit, unit_of_slot, occupied = slot_tables(owners, n_slots, slot_cap)
 
-    own_kernels = n_data == 8 and head_rows == unit_rows and unit_rows % 128 == 0 and n_tensor > 1
 
     back = -(-(DOC_MOST - 1) // rows_here)
     reach = back * rows_here
+    own_kernels = n_data == 8 and n_tensor == 4 and back == 2 and head_rows == unit_rows and unit_rows % 128 == 0
     sizes = lengths[0]
     upto = jnp.arange(sizes.shape[0])[:, None] >= jnp.arange(sizes.shape[0])[None, :]
     bounds = jnp.sum(jnp.where(upto, sizes[None, :], 0), axis=1)
@@ -1157,13 +1283,12 @@
     normed_low = normed_one.astype(BF)
     if own_kernels:
         (
-            w_att, w_fc, w_proj, normed_all, all_bias,
-            q_scaled, keys_in, values_in, attended, log_norms, peaks, hidden,
+            w_att, normed_all, q_scaled, keys_in, values_in, attended, log_norms, peaks,
+            layer_out, grad_hidden, grad_attended, grad_ff_w, grad_out_w, grad_fc_b, shared_rows,
         ) = forward_spread(
-            matrix_master[0].astype(BF), normed_low, tokens_in, bias_params[0, 0], first_seen, shared,
+            matrix_master[0].astype(BF), normed_low, tokens_in, out_grad, bias_params[0, 0], first_seen, shared,
             slot_of_unit, n_tensor, back,
         )
-        w_q, w_k, w_v, w_out = (w_att[i] for i in range(4))
     else:
         units = gather_units(matrix_master[0], slot_of_unit)
         stacks = units.reshape(n_tensor, n_units * unit_rows, width)
@@ -1178,28 +1303,27 @@
         ]
         blank = [jnp.zeros_like(normed_low)] * (back - len(before))
         normed_all = jnp.concatenate([*blank, *before, normed_low], axis=0)
-    if not own_kernels:
         bias = lambda first, count: all_bias[:, first : first + count].reshape(-1)
         b_q, b_k, b_v = (bias(i * head_rows, head_rows) for i in range(3))
+        b_fc = bias(3 * head_rows, ff_rows)
         q_scaled = (rows_by_rows(normed_low, w_q) + b_q).astype(BF) * jnp.asarray(1.0 / math.sqrt(HD), BF)
         keys_in = (rows_by_rows(normed_all, w_k) + b_k).astype(BF)
         values_in = (rows_by_rows(normed_all, w_v) + b_v).astype(BF)
         attended, log_norms, peaks = attend_forward(q_scaled, keys_in, values_in, first_seen)
         hidden = inputs_f32 + (plain_dot(attended, w_out) + shared[2])
-    swap = (lambda v: v.swapaxes(0, 1)) if own_kernels else (lambda v: v)
-    b_fc = swap(all_bias[:, 3 * head_rows :].reshape(n_tensor, -1, unit_rows)).reshape(-1)
-    layer_out, grad_hidden, grad_hidden_low, grad_fc_w, grad_proj_w, grad_fc_b, shared_rows = feed_forward(
-        hidden, out_grad, shared, b_fc, w_fc, w_proj
-    )
-    grad_out_w = cols_by_cols(attended, grad_hidden_low).astype(BF)
-    grad_attended = rows_by_rows(grad_hidden_low, w_out).astype(BF)
+        layer_out, grad_hidden, grad_hidden_low, grad_fc_w, grad_proj_w, grad_fc_b, shared_rows = feed_forward(
+            hidden, out_grad, shared, b_fc, w_fc, w_proj
+        )
+        grad_out_w = cols_by_cols(attended, grad_hidden_low).astype(BF)
+        grad_attended = rows_by_rows(grad_hidden_low, w_out).astype(BF)
     head_here = jnp.max(peaks, axis=2).reshape(-1)
     if own_kernels:
         in_blocks = lambda g: g.reshape(-1, n_tensor, 2, 2, 2, unit_rows // 8, width)
         shard, grad_first, grad_q_w, grad_k_w, grad_v_w, sums = backward_reduce(
-            in_blocks(grad_proj_w), in_blocks(grad_fc_w), q_scaled, keys_in, values_in, attended, grad_attended,
-            log_norms, first_seen, normed_all, w_att.reshape(-1, width), n_tensor, back,
+            in_blocks(grad_ff_w), q_scaled, keys_in, values_in, attended, grad_attended,
+            log_norms, first_seen, normed_all, w_att, n_tensor, back,
         )
+        grad_fc_b = grad_fc_b.reshape(2, n_tensor, -1, unit_rows).swapaxes(1, 2)
         vectors = jnp.concatenate(
             [
                 jnp.zeros((2, width), F32), shared_rows, sums, grad_fc_b.reshape(-1, width),
@@ -1208,8 +1332,11 @@
             axis=0,
         )
         grads = [in_blocks(g) for g in (grad_q_w, grad_k_w, grad_v_w, grad_out_w)]
+        half = (n_units - 4) // 2
+        later = unit_of_slot - 4
+        spot_of_slot = jnp.where(later < 0, unit_of_slot, 4 + jnp.where(later < half, 2 * later, 2 * (later - half) + 1))
         my_grads, totals, input_grad = finish_reduce(
-            grads, shard, grad_first, grad_hidden, tokens_in, shared, vectors, unit_of_slot, n_tensor, slot_cap
+            grads, shard, grad_first, grad_hidden, tokens_in, shared, vectors, spot_of_slot, n_tensor, slot_cap
         )
         my_grads = my_grads.astype(F32)
         shared_grad = totals[:6]

time: 492 us -> 429 us (0.87)
  Pallas kernels: 458 us -> 398 us
    pallas_call x1 -> x0, Pallas kernels: 55.9 us -> none  [feed_forward(): pl.pallas_call(feed_forward_kernel, grid=(steps,), in_specs=[whole(rows,...]
    pallas_call x1, Pallas kernels: 161 us -> 134 us  [backward_reduce(): pl.pallas_call(functools.partial(backward_kernel, n_tensor, back, 1.0 / m...]
    pallas_call x1, Pallas kernels: 158 us -> 182 us  [forward_spread(): pl.pallas_call(functools.partial(forward_kernel, n_tensor, back, 1.0 / ma...]
where the time goes in v5:
time: 429 us; the launch traced here: 428 us
  Pallas kernels  398 us (93%)
  other arithmetic  19.3 us (4%)
  local copies, waits for them, and re-layouts  9.17 us (2%)
    pallas_call x1, Pallas kernels, forward_spread(): pl.pallas_call(functools.partial(forward_kernel, n_tensor, back, 1.0 / ma...  182 us
    pallas_call x1, Pallas kernels, backward_reduce(): pl.pallas_call(functools.partial(backward_kernel, n_tensor, back, 1.0 / m...  134 us
    pallas_call x1, Pallas kernels, finish_reduce(): pl.pallas_call(functools.partial(finish_kernel, n_tensor), out_shape=[sha...  82.7 us
    select_n x1, other arithmetic, per_device(): master_new = jnp.where(my_occupied, master_new * factor[..., None], 0.0)  8.64 us

profile of v5, /device:TPU:9, one launch (start us, length us, event | category | flops | bytes accessed | tf_op | source)
XLA Modules:
  0.0 427.8 jit_solution(12410485507438486690)
XLA Ops:
  0.7 0.9 select_reduce_fusion.3
  1.5 0.1 select_reduce_fusion.2
  1.6 0.6 subtract_add_fusion
  2.2 0.8 fusion.20
  3.1 1.6 convert_reduce_fusion
  4.7 1.6 fusion.2
  6.3 1.4 fusion.5.a_ref
  7.8 0.2 convert_reduce_fusion.1
  7.9 0.5 multiply_add_fusion.slot_ref
  8.5 0.6 slice_bitcast_fusion.shared_ref
  9.1 1.1 convert_element_type.42
  10.2 0.6 slice_reduce_fusion
  10.8 181.5 %forward_spread.1 = (bf16[4,4,4,2,32,1024]{5,4,3,2,1,0:T(8,128)(2,1)}, bf16[8,4,4,2,32,1024]{5,4,3,2,1,0:T(8,128)(2,1)}, bf16[3,512,1024]{2,1,0:T(8,128)(2,1)}, ...) custom-call(s32[12]{0:T(128)} %multiply_add_fusion.slot_ref, ...), custom_call_target="tpu_custom_call" | custom-call | tf_op jit(solution)/shard_map/forward_spread/pallas_call | solution.py:664
  192.4 134.2 %backward_reduce.1 = (bf16[8,32,1024]{2,1,0:T(8,128)(2,1)}, f32[512,1024]{1,0:T(8,128)}, bf16[1024,1024]{1,0:T(8,128)(2,1)}, bf16[1024,1024]{1,0:T(8,128)(2,1)},...) custom-call(bf16[8,4,2,2,2,32,1024]{6,5,4,3,2,1,0:T(8,128)(2,1)} %bitcast.59, bf16[512,1024]{1,0:T(8,128)(2,1)} %get-tuple-element.39.q_ref, ...), custom_call_target="tpu_custom_call" | custom-call | tf_op jit(solution)/shard_map/backward_reduce/pallas_call | solution.py:1049
  326.7 0.1 reduce_max.19
  326.8 0.1 reshape.345
  326.9 0.9 concatenate.3.v_ref
  327.9 0.1 select_reduce_fusion.1
  328.0 1.0 copy-done.3
  329.0 82.7 %finish_reduce.1 = (bf16[2,8,32,1024]{3,2,1,0:T(8,128)(2,1)S(1)}, f32[16,1024]{1,0:T(8,128)S(1)}, f32[512,1024]{1,0:T(8,128)S(1)}) custom-call(s32[16]{0:T(128)S(1)} %compare_select_fusion.3.unit_ref, bf16[1,4,2,2,2,32,1024]{6,5,4,3,2,1,0:T(8,128)(2,1)} %bitcast.64, bf16[1,4,2,2,2,32,1024]{6,5,4,3,2,1,0:T(8,128)(2,1)} %bitcast.65, ...), custom_call_target="tpu_custom_call" | custom-call | tf_op jit(solution)/shard_map/finish_reduce/pallas_call | solution.py:1161
  411.8 1.0 copy-done.2
  412.8 0.7 bitcast_subtract_fusion
  413.5 0.6 broadcast_in_dim.103
  414.1 0.7 multiply_subtract_fusion
  414.8 0.7 copy.27
  415.4 0.6 divide_sqrt_fusion
  416.1 0.1 compare_select_fusion
  416.2 0.1 select_reduce_fusion
  416.3 0.1 fusion.11
  416.5 8.6 %multiply_select_fusion = (f32[1,2,256,1024]{3,2,1,0:T(8,128)}, f32[1,2,256,1024]{3,2,1,0:T(8,128)}, f32[1,2,256,1024]{3,2,1,0:T(8,128)}, f32[1,2,256,1024]{3,2,1,0:T(8,128)}) fusion(f32[1,2,256,1024]{3,2,1,0:T(8,128)} %param.13, bf16[1,2,256,1024]{3,2,1,0:T(8,128)(2,1)} %bitcast.58, f32[1,2,256,1024]{3,2,1,0:T(8,128)} %param.14, ...), kind=kLoop, calls=%fused_computation.14 | loop fusion | flops 11010048 | bytes 15730690 | tf_op jit(solution)/shard_map/jit(_where)/select_n | solution.py:1387
  425.2 1.3 copy.31
  426.5 1.3 copy.32
  (43 shorter events, 0.5 us)
Async XLA Ops:
  0.6 5.7 %copy-start = (bf16[512,1024]{1,0:T(8,128)(2,1)S(1)}, bf16[512,1024]{1,0:T(8,128)(2,1)}, u32[]{:S(2)}) copy-start(bf16[512,1024]{1,0:T(8,128)(2,1)} %x_ref.3) | copy-start | bytes 3145732
  3.0 4.7 %copy-start.13 = (s32[12]{0:T(128)S(1)}, s32[12]{0:T(128)}, u32[]{:S(2)}) copy-start(s32[12]{0:T(128)} %param.12) | copy-start | bytes 148
  3.1 5.4 %copy-start.7 = (f32[3,6,1024]{2,1,0:T(8,128)S(1)}, f32[3,6,1024]{2,1,0:T(8,128)}, u32[]{:S(2)}) copy-start(f32[3,6,1024]{2,1,0:T(8,128)} %param.16) | copy-start | bytes 221188
  3.1 6.0 %copy-start.5 = (f32[1,2,256,1024]{3,2,1,0:T(8,128)S(1)}, f32[1,2,256,1024]{3,2,1,0:T(8,128)}, u32[]{:S(2)}) copy-start(f32[1,2,256,1024]{3,2,1,0:T(8,128)} %param.13) | copy-start | bytes 6291460
  7.8 2.5 copy-start.8
  192.4 134.3 %copy-start.11 = (f32[2,4,1,512]{3,2,1,0:T(1,128)S(1)}, f32[2,4,1,512]{3,2,1,0:T(1,128)}, u32[]{:S(2)}) copy-start(f32[2,4,1,512]{3,2,1,0:T(1,128)} %get-tuple-element.56) | copy-start | bytes 49156
  192.4 134.4 %copy-start.9 = (f32[8,2,512]{2,1,0:T(2,128)S(1)}, f32[8,2,512]{2,1,0:T(2,128)}, u32[]{:S(2)}) copy-start(f32[8,2,512]{2,1,0:T(2,128)} %get-tuple-element.57) | copy-start | bytes 98308
  192.4 134.6 %copy-start.10 = (f32[4,1024]{1,0:T(4,128)S(1)}, f32[4,1024]{1,0:T(4,128)}, u32[]{:S(2)}) copy-start(f32[4,1024]{1,0:T(4,128)} %get-tuple-element.54) | copy-start | bytes 49156
  192.4 135.5 %copy-start.12 = (s32[12]{0:T(128)S(1)}, s32[12]{0:T(128)}, u32[]{:S(2)}) copy-start(s32[12]{0:T(128)} %multiply_add_fusion.slot_ref) | copy-start | bytes 148
  192.4 135.6 %copy-start.1 = (bf16[512,1024]{1,0:T(8,128)(2,1)S(1)}, bf16[512,1024]{1,0:T(8,128)(2,1)}, u32[]{:S(2)}) copy-start(bf16[512,1024]{1,0:T(8,128)(2,1)} %x_ref.3) | copy-start | bytes 3145732
  192.4 135.6 %copy-start.4 = (f32[6,1024]{1,0:T(8,128)S(1)}, f32[6,1024]{1,0:T(8,128)}, u32[]{:S(2)}) copy-start(f32[6,1024]{1,0:T(8,128)} %slice_bitcast_fusion.shared_ref) | copy-start | bytes 73732
  328.0 1.0 copy-start.3
  411.8 1.0 copy-start.2
  416.5 8.6 %copy-start.6 = (f32[512,1024]{1,0:T(8,128)S(1)}, f32[512,1024]{1,0:T(8,128)}, u32[]{:S(2)}) copy-start(f32[512,1024]{1,0:T(8,128)} %get-tuple-element.128) | copy-start | bytes 6291460

commit v6 on v5

--- a/solution.py
+++ b/solution.py
@@ -27,6 +27,8 @@
 F32 = jnp.float32
 MESH = pl.DeviceIdType.MESH
 MAX_ROW = 13
+BACK_GROUPS = 4
+LAST_GROUPS = 2
 
 
 def plain_dot(left, right):
@@ -287,9 +289,17 @@
     lax.fori_loop(0, count, step, 0)
 
 
-def spaced(count, events):
-    per = -(-len(events) // count)
-    return {n: events[n * per : (n + 1) * per] for n in range(count) if events[n * per : (n + 1) * per]}
+def by_step(order, by_code, kinds):
+    early, during = [], {kind: {} for kind in range(1, kinds + 1)}
+    now, count = None, 0
+    for code in order:
+        if code < 0:
+            now, count = -code, 0 if -code != now else count + 1
+        elif now is None:
+            early.append(by_code[code])
+        else:
+            during[now].setdefault(count, []).append(by_code[code])
+    return early, during
 
 
 def attend_pair(i, q_ref, k_ref, v_ref, o_ref, lse_ref, peak_ref, bias_ref):
@@ -327,13 +337,11 @@
 
 
 ORDER = (
-    "o2", "g0d", "o0", "z00d", "g0u", "z01d", "z02d", "z00u", "z01u", "f01d", "g2d", "z02u", "f01u", "t0", "g1d",
-    "f0o", "f02d", "f02u", "f00d", "f00u", "e01u", "e01d", "z10d", "e00d", "e0o", "e02u", "o1", "d2", "e02d",
-    "e00u", "g1u", "d0", "f1o", "d1", "d3", "Q", "Q", "Q", "g2u", "t1", "z20d", "Q", "z11d", "K", "K", "K", "K",
-    "z10u", "V", "V", "V", "z20u", "V", "A", "z11u", "z21d", "A", "A", "z21u", "z22d", "A", "f11d", "z12u",
-    "f10u", "A", "z12d", "f11u", "f10d", "A", "e1o", "A", "z22u", "A", "f20d", "f12u", "f20u", "e10u", "e11u",
-    "e11d", "f12d", "f2o", "O", "e10d", "F", "e12u", "f21u", "f22d", "F", "e12d", "e20d", "F", "f21d", "e2o",
-    "e22d", "e20u", "F", "f22u", "F", "F", "F", "F", "e21u", "e21d", "F", "e22u", "F", "F", "F", "F", "F",
+    220, 100, 200, 600, 0, 601, 602, 500, 501, 801, 120, 502, 701, 1900, 110, 300, 802, 702, 800, 700, 901,
+    1001, 610, 1000, 400, 902, 210, 1952, 1002, 900, 10, 1950, 310, 1951, 1953, -1, -1, -1, 20, 1901, 620, -1,
+    611, -2, -2, -2, -2, 510, -3, -3, -3, 520, -3, -4, 511, 621, -4, -4, 521, 622, -4, 811, 512, 710, -4, 612,
+    711, 810, -4, 410, -4, 522, -4, 820, 712, 720, 910, 911, 1011, 812, 320, -5, 1010, -6, 912, 721, 822, -6,
+    1012, 1020, -6, 821, 420, 1022, 920, -6, 722, -6, -6, -6, -6, 921, 1021, -6, 922, -6, -6, -6, -6, -6,
 )
 
 
@@ -474,31 +482,21 @@
         local[g].wait()
         settle(g, 0, t)
 
-    by_code = {f"t{r}": functools.partial(tokens_in, r) for r in range(back)}
-    by_code |= {f"d{s + 1}": functools.partial(each, done, 0, s) for s in range(-1, steps)}
+    by_code = {1900 + r: functools.partial(tokens_in, r) for r in range(back)}
+    by_code |= {1951 + s: functools.partial(each, done, 0, s) for s in range(-1, steps)}
     for g in range(n_groups):
-        by_code[f"o{g}"] = functools.partial(onward, g, 0, t, mine_of[g])
-        by_code[f"f{g}o"] = functools.partial(forward, g, 0, t)
-        by_code[f"e{g}o"] = functools.partial(own_settled, g)
-        for way, up in (("u", True), ("d", False)):
-            by_code[f"g{g}{way}"] = functools.partial(z_go, g, 0, up, mine_of[g])
+        by_code[200 + 10 * g] = functools.partial(onward, g, 0, t, mine_of[g])
+        by_code[300 + 10 * g] = functools.partial(forward, g, 0, t)
+        by_code[400 + 10 * g] = functools.partial(own_settled, g)
+        for way, up in ((0, True), (100, False)):
+            by_code[way + 10 * g] = functools.partial(z_go, g, 0, up, mine_of[g])
             for s in range(steps):
-                by_code[f"z{g}{s}{way}"] = functools.partial(z_event, g, s, up)
-                by_code[f"f{g}{s}{way}"] = functools.partial(step, forward, g, s, up)
-                by_code[f"e{g}{s}{way}"] = functools.partial(step, settle, g, s, up)
+                by_code[500 + way + 10 * g + s] = functools.partial(z_event, g, s, up)
+                by_code[700 + way + 10 * g + s] = functools.partial(step, forward, g, s, up)
+                by_code[900 + way + 10 * g + s] = functools.partial(step, settle, g, s, up)
     tile = 256
     tiles = width // tile
-    early, during = [], {}
-    counts = {"Q": tiles, "K": tiles, "V": tiles, "A": width // PAIR, "O": 1, "F": 2 * slots}
-    now, seen = None, 0
-    for code in ORDER:
-        if code in counts:
-            now, seen = code, 0 if code != now else seen + 1
-            during.setdefault(code, {})
-        elif now is None:
-            early.append(by_code[code])
-        else:
-            during[now].setdefault(seen, []).append(by_code[code])
+    early, during = by_step(ORDER, by_code, 6)
     for event in early:
         event()
     for k in range(1, n_tensor):
@@ -527,13 +525,13 @@
                 into_ref[r * rows_here : (r + 1) * rows_here, cols] = full * jnp.asarray(factor, BF) if factor else full
         return body
 
-    loop_with(tiles, project(0, True, q_ref, scale), during["Q"])
-    loop_with(tiles, project(1, False, k_ref, None), during["K"])
-    loop_with(tiles, project(2, False, v_ref, None), during["V"])
+    loop_with(tiles, project(0, True, q_ref, scale), during[1])
+    loop_with(tiles, project(1, False, k_ref, None), during[2])
+    loop_with(tiles, project(2, False, v_ref, None), during[3])
     loop_with(
         width // PAIR,
         lambda i: attend_pair(i, q_ref, k_ref, v_ref, o_ref, lse_ref, peak_ref, seen_ref),
-        during["A"],
+        during[4],
     )
     w_out = att_ref[3].reshape(width, width)
     half = rows_here // 2
@@ -592,9 +590,9 @@
             for copy in grad_copies(h, at):
                 copy.start()
 
-    for event in during["O"].get(0, []):
+    for event in during[5].get(0, []):
         event()
-    loop_with(2 * slots, feed, during["F"])
+    loop_with(2 * slots, feed, during[6])
     for copy in grad_copies(0, 0):
         copy.wait()
 
@@ -698,6 +696,11 @@
     return att.reshape(-1, width), wide.reshape(-1, width), *rest
 
 
+def split_units(ref, count):
+    many = ref.shape[0] // count
+    return [ref.at[pl.ds(i * many, many)] for i in range(count)]
+
+
 def add_blocks(into, part, count):
     def body(i, carry):
         a = into(i)
@@ -705,6 +708,23 @@
         return carry
 
     lax.fori_loop(0, count, body, 0)
+
+
+BACK_ORDER = (
+    0, -1, -1, 103, 10, 100, -1, 102, 101, -1, 113, -1, 110, -1, 201, 203, 20, 202, -1, 112, 301, 213, -1, 302,
+    303, 200, -2, 111, -2, -2, -2, 313, 900, 123, 120, -2, 300, 212, -2, 122, 121, -2, 600, 210, 502, -2, -2,
+    30, -2, -2, 211, -2, 223, 133, 130, 503, 310, -3, 312, 602, 700, -3, 702, -3, 512, 311, -3, 403, 220, -4,
+    -4, 221, -4, -4, 222, -5, 230, 610, -5, 401, 411, 323, 513, 402, 132, 501, 131, 601, 320, -5, 330, 321, -5,
+    523, 231, 620, 233, 901, 322, 423, 331, 611, 232, 612, 701, 621, 522, 511, 333, 421, 412, 720, 521, 711,
+    332, 722, 533, 710, 721, 532, 630, 631, 413, 712, 422, 730, 433, 531, 432, 732, 632, 731, 431, 622,
+)
+
+
+LAST_ORDER = (
+    0, 103, 100, 900, 10, 102, 101, 203, 113, 110, 202, 200, 303, 201, 213, 300, 112, 301, 111, 313, 210, 302,
+    901, 903, 910, 702, 503, 600, 212, 310, 911, 513, 211, 610, 312, 912, 501, 502, 700, 311, 403, 712, 601,
+    612, 913, 512, 413, 710, 602, 701, 511, 611, 914, 402, 411, 711, 401, 412,
+)
 
 
 class Reducer:
@@ -719,7 +739,7 @@
         self.d, self.t, self.core, self.x, self.y = place()
         self.by_x, self.by_y = self.d + 2 - 4 * self.x, self.d + 4 - 8 * self.y
         self.sibling = self.d + 1 - 2 * self.core
-        self.order = sorted(range(n_tensor), key=lambda a: -abs(2 * a - n_tensor + 1))
+        self.order = sorted(range(n_tensor), key=lambda a: (-abs(2 * a - n_tensor + 1), -a))
         self.merges = [(g, at) for g in range(len(groups)) for at in self.order]
         self.starts, total = [], 0
         for refs in groups:
@@ -764,13 +784,14 @@
                 self.near_sem.at[m % 2, n],
             )
 
+    def core_go(self, g):
+        for n, ref, u, many in self.parts(g):
+            send(
+                ref.at[:, :, :, :, 1 - self.core], self.other.at[pl.ds(u, many)],
+                self.core_send.at[g, n], self.core_recv.at[g, n], (self.sibling, self.t),
+            )
+
     def start(self):
-        for g in range(len(self.groups)):
-            for n, ref, u, many in self.parts(g):
-                send(
-                    ref.at[:, :, :, :, 1 - self.core], self.other.at[pl.ds(u, many)],
-                    self.core_send.at[g, n], self.core_recv.at[g, n], (self.sibling, self.t),
-                )
         for m in range(2):
             for copy in self.near_copies(m):
                 copy.start()
@@ -835,27 +856,29 @@
         add_blocks(lambda i: self.other.at[u0 + i, at, self.y, self.x], lambda i: buffer.at[u0 + i, at], n)
         pl.when(t < at if up else t > at)(functools.partial(self.line_go, g, at, up))
 
-    def line(self, g, k):
-        n, t = self.n_tensor, self.t
-        high, low = n - 1 - k, k
-        near_top = t * 2 >= n
-        came_down = (t >= low) & (t < n - 1)
-        pl.when(came_down & near_top)(functools.partial(self.line_in, g, low, False))
-        pl.when((t <= high) & (t > 0))(functools.partial(self.line_in, g, high, True))
-        pl.when(came_down & (t * 2 < n))(functools.partial(self.line_in, g, low, False))
-
-    def keep(self, g):
-        us = self.units(g)
-        self.final[us] = self.other[us, self.t, self.y, self.x]
-
-    def events(self):
-        n, count = self.n_tensor, len(self.groups)
-        first, second, third = (
-            [[functools.partial(f, g * n + i) for i in range(n)] for g in range(count)]
-            for f in (self.first_hop, self.second_hop, self.plane_sum)
-        )
-        lines = [[functools.partial(self.line, g, k) for k in range(n - 1)] + [functools.partial(self.keep, g)] for g in range(count)]
-        return first, second, third, lines
+    def line(self, g, at, up, near):
+        t, top = self.t, self.n_tensor - 1
+        have = ((t <= at) & (t > 0)) if up else ((t >= at) & (t < top))
+        half = t * 2 > top
+        pl.when(have & (half if near else ~half))(functools.partial(self.line_in, g, at, up))
+
+    def keep(self):
+        for g in range(len(self.groups)):
+            us = self.units(g)
+            self.final[us] = self.other[us, self.t, self.y, self.x]
+
+    def codes(self):
+        out = {}
+        for g in range(len(self.groups)):
+            out[10 * g] = functools.partial(self.core_go, g)
+            for i, at in enumerate(self.order):
+                m, here = g * self.n_tensor + i, 10 * g + at
+                out[100 + here] = functools.partial(self.first_hop, m)
+                out[200 + here] = functools.partial(self.second_hop, m)
+                out[300 + here] = functools.partial(self.plane_sum, m)
+                for kind in range(4):
+                    out[400 + 100 * kind + here] = functools.partial(self.line, g, at, kind < 2, kind % 2 == 0)
+        return out
 
     def finish(self):
         for g in range(len(self.groups)):
@@ -877,19 +900,35 @@
 def backward_kernel(
     n_tensor, back, scale,
     ff_grad_ref, q_ref, k_ref, v_ref, o_ref, do_ref, lse_ref, first_ref, wide_ref, att_ref,
-    shard_ref, grad_ref, gq_ref, gk_ref, gv_ref, sums_ref, *scratch,
+    shard_ref, grad_ref, away, gq_ref, gk_ref, gv_ref, sums_ref, *scratch,
 ):
     reducer_scratch, (
-        seen_ref, q_in, k_in, v_in, o_in, do_in, dq_ref, dk_ref, dv_ref, big, away, away_in, stage, dk_acc, dv_acc,
+        seen_ref, q_in, k_in, v_in, o_in, do_in, dq_ref, dk_ref, dv_ref, big, stage, dk_acc, dv_acc, away_in,
         pair_sem, load_sem, stage_sem, away_send, away_recv,
     ) = scratch[:REDUCER], scratch[REDUCER:]
     d, t, core, x, y = place()
     greet(d, t, n_tensor)
     other, near, one, two, up_in, down_in, *sems = reducer_scratch
-    half = ff_grad_ref.shape[0] // 2
-    groups = [[ff_grad_ref.at[pl.ds(0, half)]], [ff_grad_ref.at[pl.ds(half, half)]]]
+    groups = [[part] for part in split_units(ff_grad_ref, BACK_GROUPS)]
     reducer = Reducer(groups, n_tensor, other, near, one, two, up_in, down_in, shard_ref, sems)
     reducer.start()
+    by_code = reducer.codes()
+
+    def give():
+        @pl.when(t >= 2)
+        def _():
+            send(away.at[1], away_in, away_send, away_recv, (d, t - 1))
+
+    def add_given():
+        @pl.when((t >= 1) & (t + 1 < n_tensor))
+        def _():
+            arrived(away_in, away_recv)
+            away[0] = (away[0].astype(F32) + away_in[...].astype(F32)).astype(BF)
+
+    by_code |= {900: give, 901: add_given}
+    early, during = by_step(BACK_ORDER, by_code, 5)
+    for event in early:
+        event()
     rows_here, width = do_ref.shape
     n_keys = k_ref.shape[0]
     size, span = q_tiles(rows_here, n_keys)
@@ -966,20 +1005,6 @@
 
         return body
 
-    def have_down(r):
-        return (t + 1 >= r) & (t + 1 < n_tensor)
-
-    def give(r):
-        if r < back:
-            @pl.when(have_down(r + 1) & (t >= r))
-            def _():
-                arrived(away_in.at[r], away_recv.at[r])
-                away[r - 1] = (away[r - 1].astype(F32) + away_in[r].astype(F32)).astype(BF)
-
-        @pl.when(t >= r)
-        def _():
-            send(away.at[r - 1], away_in.at[r - 1], away_send.at[r - 1], away_recv.at[r - 1], (d, t - 1))
-
     def weight_grad(n, from_ref, into_ref, first_row, many):
         def body(i):
             cols = pl.ds(pl.multiple_of(i * tile, tile), tile)
@@ -1001,37 +1026,24 @@
     def tokens_of(first_row, many):
         return big[pl.ds(first_row, many), :]
 
-    first, second, third, lines = reducer.events()
-    loop_with(pairs, attend_back, {1: first[0], 3: first[1]})
+    loop_with(pairs, attend_back, during[1])
     weights.wait()
-    for r in range(back, -1, -1):
-        loop_with(tiles, input_grad(r), {})
-        if r == back:
-            give(r)
+    for n, r in enumerate(range(back, -1, -1)):
+        loop_with(tiles, input_grad(r), {i - n * tiles: e for i, e in during[2].items() if i // tiles == n})
     load = pltpu.make_async_copy(wide_ref, big.at[pl.ds(0, n_keys)], load_sem.at[1])
     load.start()
-    for event in second[0]:
-        event()
     load.wait()
     own = n_keys - rows_here
-    loop_with(tiles, weight_grad(0, dq_ref, gq_ref, own, rows_here), {})
-    loop_with(tiles, weight_grad(1, dk_ref, gk_ref, 0, n_keys), {1: third[0]})
-    loop_with(tiles, weight_grad(2, dv_ref, gv_ref, 0, n_keys), {1: lines[0][:1]})
-    for r in range(back - 1, 0, -1):
-        give(r)
-    for event in lines[0][1:] + second[1] + third[1] + lines[1]:
-        event()
+    loop_with(tiles, weight_grad(0, dq_ref, gq_ref, own, rows_here), during[3])
+    loop_with(tiles, weight_grad(1, dk_ref, gk_ref, 0, n_keys), during[4])
+    loop_with(tiles, weight_grad(2, dv_ref, gv_ref, 0, n_keys), during[5])
+    reducer.keep()
     for slot in range(2):
         arrived(stage.at[slot], stage_sem.at[slot])
 
-    @pl.when(have_down(1))
+    @pl.when(t >= 2)
     def _():
-        arrived(away_in.at[0], away_recv.at[0])
-        grad_ref[...] = grad_ref[...] + away_in[0].astype(F32)
-    for r in range(1, back + 1):
-        @pl.when(t >= r)
-        def _(r=r):
-            arrived(away.at[r - 1], away_send.at[r - 1])
+        arrived(away.at[1], away_send)
     reducer.finish()
 
 
@@ -1048,19 +1060,19 @@
     pair = lambda n: pltpu.VMEM((2, n, PAIR), BF)
     return pl.pallas_call(
         functools.partial(backward_kernel, n_tensor, back, 1.0 / math.sqrt(HD)),
-        out_shape=[shape((n_ff, *block), BF), shape((rows, width), F32), square, square, square, shape((3, width), F32)],
+        out_shape=[shape((n_ff, *block), BF), shape((rows, width), F32), shape((back, rows, width), BF), square, square, square, shape((3, width), F32)],
         in_specs=[any_spec] * 6 + [vmem, vmem] + [any_spec] * 2,
-        out_specs=[vmem, vmem, any_spec, any_spec, any_spec, vmem],
+        out_specs=[vmem, vmem, vmem, any_spec, any_spec, any_spec, vmem],
         scratch_shapes=[
-            *Reducer.scratch(n_ff, n_ff // 2, 2, 1, n_tensor, block),
+            *Reducer.scratch(n_ff, n_ff // BACK_GROUPS, BACK_GROUPS, 1, n_tensor, block),
             pltpu.VMEM((n_keys, rows), F32),
             pair(rows), pair(n_keys), pair(n_keys), pair(rows), pair(rows),
             pltpu.VMEM((rows, width), BF), pltpu.VMEM((n_keys, width), BF), pltpu.VMEM((n_keys, width), BF),
             pltpu.VMEM((3 * width, width), BF),
-            pltpu.VMEM((back, rows, width), BF), pltpu.VMEM((back, rows, width), BF),
             pltpu.VMEM((2, 256, width), BF),
             pltpu.VMEM((n_keys, PAIR), F32), pltpu.VMEM((n_keys, PAIR), F32),
-            dma((2, 5)), dma((2,)), dma((2,)), dma((back,)), dma((back,)),
+            pltpu.VMEM((rows, width), BF),
+            dma((2, 5)), dma((2,)), dma((2,)), dma, dma,
         ],
         compiler_params=pltpu.CompilerParams(collective_id=1, has_side_effects=True, vmem_limit_bytes=60 << 20),
         name="backward_reduce",
@@ -1073,21 +1085,41 @@
 
 def finish_kernel(
     n_tensor,
-    unit_ref, gq_ref, gk_ref, gv_ref, go_ref, shard_ref, grad_ref, hidden_ref, x_ref, shared_ref, v_ref,
+    unit_ref, gq_ref, gk_ref, gv_ref, go_ref, shard_ref, grad_ref, away_ref, hidden_ref, x_ref, shared_ref, v_ref,
     out_ref, vsum_ref, input_ref, *scratch,
 ):
-    reducer_scratch, (final, outgo, v_in, v_z, swap_send, swap_recv, v_send, v_recv, local_sem) = (
+    reducer_scratch, (
+        final, outgo, v_in, v_z, away_in, swap_send, swap_recv, v_send, v_recv, local_sem, away_send, away_recv,
+    ) = (
         scratch[:REDUCER], scratch[REDUCER:]
     )
     d, t, core, x, y = place()
     greet(d, t, n_tensor)
     other, near, one, two, up_in, down_in, *sems = reducer_scratch
-    reducer = Reducer([[gq_ref, gk_ref], [gv_ref, go_ref]], n_tensor, other, near, one, two, up_in, down_in, final, sems)
+    parts = [gq_ref, gk_ref, gv_ref, go_ref]
+    groups = [parts[i : i + 4 // LAST_GROUPS] for i in range(0, 4, 4 // LAST_GROUPS)]
+    reducer = Reducer(groups, n_tensor, other, near, one, two, up_in, down_in, final, sems)
     reducer.start()
     rows_here = x_ref.shape[0]
     n_att = other.shape[0]
     final[n_att:] = shard_ref[...]
 
+    from_above, to_below = t + 1 < n_tensor, t >= 1
+
+    @pl.when(~from_above)
+    def _():
+        away_in[...] = jnp.zeros_like(away_in)
+
+    def give():
+        @pl.when(to_below)
+        def _():
+            send(away_ref.at[0], away_in, away_send, away_recv, (d, t - 1))
+
+    def got():
+        @pl.when(from_above)
+        def _():
+            arrived(away_in, away_recv)
+
     vsum_ref[...] = v_ref[...]
     part = 128
     gain = shared_ref[0:1, :]
@@ -1095,25 +1127,22 @@
     def norm_back_rows(i, carry):
         rows = pl.ds(pl.multiple_of(i * part, part), part)
         _, hat, inverse = norm_rows(x_ref[rows, :].astype(F32), 1.0, 0.0)
-        grad = grad_ref[rows, :]
+        grad = grad_ref[rows, :] + away_in[rows, :].astype(F32)
         input_ref[rows, :] = hidden_ref[rows, :] + norm_back(grad, hat, inverse, gain)
         vsum_ref[0:1, :] += jnp.sum(grad * hat, axis=0, keepdims=True)
         vsum_ref[1:2, :] += jnp.sum(grad, axis=0, keepdims=True)
         return carry
 
-    lax.fori_loop(0, rows_here // part, norm_back_rows, 0)
     row = lax.broadcasted_iota(jnp.int32, vsum_ref.shape, 0)
     hops = (reducer.sibling, reducer.by_x, reducer.by_y)
 
-    def vector_go(i):
-        send(vsum_ref, v_in.at[i], v_send.at[i], v_recv.at[i], (hops[i], t))
-
-    def vector_in(i):
-        arrived(v_in.at[i], v_recv.at[i])
-        arrived(v_in.at[i], v_send.at[i])
-        vsum_ref[...] = join(row, vsum_ref[...], v_in[i])
-        if i + 1 < len(hops):
-            vector_go(i + 1)
+    def vector_step(i):
+        if i > 0:
+            arrived(v_in.at[i - 1], v_recv.at[i - 1])
+            arrived(v_in.at[i - 1], v_send.at[i - 1])
+            vsum_ref[...] = join(row, vsum_ref[...], v_in[i - 1])
+        if i < len(hops):
+            send(vsum_ref, v_in.at[i], v_send.at[i], v_recv.at[i], (hops[i], t))
         else:
             for k in range(1, n_tensor):
                 send(vsum_ref, v_z.at[k - 1], v_send.at[2 + k], v_recv.at[2 + k], (d, (t + k) % n_tensor))
@@ -1125,13 +1154,13 @@
         for k in range(1, n_tensor):
             vsum_ref[...] = join(row, vsum_ref[...], v_z[k - 1])
 
-    vector_go(0)
-    first, second, third, lines = reducer.events()
-    events = first[0] + first[1] + second[0] + third[0] + second[1] + lines[0] + third[1] + lines[1]
-    for n, event in enumerate((functools.partial(vector_in, 0), functools.partial(vector_in, 1), functools.partial(vector_in, 2), vector_end)):
-        events.insert(4 + 5 * n, event)
-    for event in events:
-        event()
+    by_code = reducer.codes()
+    by_code |= {910 + i: functools.partial(vector_step, i) for i in range(len(hops) + 1)}
+    by_code |= {900: give, 901: got, 914: vector_end}
+    by_code[903] = lambda: lax.fori_loop(0, rows_here // part, norm_back_rows, 0)
+    for code in LAST_ORDER:
+        by_code[code]()
+    reducer.keep()
 
     cap = out_ref.shape[0]
     for k in range(1, 9):
@@ -1147,10 +1176,14 @@
     reducer.finish()
     for k in range(1, 8):
         arrived(outgo.at[0], swap_send.at[k - 1])
+
+    @pl.when(to_below)
+    def _():
+        arrived(away_in, away_send)
     keep.wait()
 
 
-def finish_reduce(grads, shard, grad_first, grad_hidden, tokens, shared, vectors, unit_of_slot, n_tensor, cap):
+def finish_reduce(grads, shard, grad_first, away, grad_hidden, tokens, shared, vectors, unit_of_slot, n_tensor, cap):
     block = shard.shape[1:]
     n_units = len(grads) + shard.shape[0]
     rows, width = tokens.shape
@@ -1161,19 +1194,21 @@
     out, vsum, input_grad = pl.pallas_call(
         functools.partial(finish_kernel, n_tensor),
         out_shape=[shape((cap, 8, *block), BF), shape(vectors.shape, F32), shape((rows, width), F32)],
-        in_specs=[pl.BlockSpec(memory_space=pltpu.SMEM)] + [any_spec] * 4 + [vmem] * 6,
+        in_specs=[pl.BlockSpec(memory_space=pltpu.SMEM)] + [any_spec] * 4 + [vmem, vmem, any_spec] + [vmem] * 4,
         out_specs=[vmem, vmem, vmem],
         scratch_shapes=[
-            *Reducer.scratch(len(grads), 2, 2, 2, n_tensor, block),
+            *Reducer.scratch(len(grads), 4 // LAST_GROUPS, LAST_GROUPS, 4 // LAST_GROUPS, n_tensor, block),
             pltpu.VMEM((n_units, *block), BF),
             pltpu.VMEM((8, cap, *block), BF),
             pltpu.VMEM((3, *vectors.shape), F32),
             pltpu.VMEM((n_tensor - 1, *vectors.shape), F32),
+            pltpu.VMEM(away.shape[1:], BF),
             dma((7,)), dma((7,)), dma((2 + n_tensor,)), dma((2 + n_tensor,)), dma((1,)),
+            dma, dma,
         ],
         compiler_params=pltpu.CompilerParams(collective_id=2, has_side_effects=True, vmem_limit_bytes=48 << 20),
         name="finish_reduce",
-    )(unit_of_slot, *grads, shard, grad_first, grad_hidden, tokens, shared, vectors)
+    )(unit_of_slot, *grads, shard, grad_first, away, grad_hidden, tokens, shared, vectors)
     return out.reshape(cap, -1, width), vsum, input_grad
 
 
@@ -1319,7 +1354,7 @@
     head_here = jnp.max(peaks, axis=2).reshape(-1)
     if own_kernels:
         in_blocks = lambda g: g.reshape(-1, n_tensor, 2, 2, 2, unit_rows // 8, width)
-        shard, grad_first, grad_q_w, grad_k_w, grad_v_w, sums = backward_reduce(
+        shard, grad_first, away, grad_q_w, grad_k_w, grad_v_w, sums = backward_reduce(
             in_blocks(grad_ff_w), q_scaled, keys_in, values_in, attended, grad_attended,
             log_norms, first_seen, normed_all, w_att, n_tensor, back,
         )
@@ -1336,7 +1371,7 @@
         later = unit_of_slot - 4
         spot_of_slot = jnp.where(later < 0, unit_of_slot, 4 + jnp.where(later < half, 2 * later, 2 * (later - half) + 1))
         my_grads, totals, input_grad = finish_reduce(
-            grads, shard, grad_first, grad_hidden, tokens_in, shared, vectors, spot_of_slot, n_tensor, slot_cap
+            grads, shard, grad_first, away, grad_hidden, tokens_in, shared, vectors, spot_of_slot, n_tensor, slot_cap
         )
         my_grads = my_grads.astype(F32)
         shared_grad = totals[:6]

time: 429 us -> 411 us (0.958)
  Pallas kernels: 398 us -> 380 us
    pallas_call x1, Pallas kernels: 134 us -> 121 us  [backward_reduce(): pl.pallas_call(functools.partial(backward_kernel, n_tensor, back, 1.0 / m...]
    pallas_call x1, Pallas kernels: 82.7 us -> 77.8 us  [finish_reduce(): pl.pallas_call(functools.partial(finish_kernel, n_tensor), out_shape=[sha...]
where the time goes in v6:
time: 411 us; the launch traced here: 410 us
  Pallas kernels  380 us (92%)
  other arithmetic  19.3 us (5%)
  local copies, waits for them, and re-layouts  9.43 us (2%)
    pallas_call x1, Pallas kernels, forward_spread(): pl.pallas_call(functools.partial(forward_kernel, n_tensor, back, 1.0 / ma...  182 us
    pallas_call x1, Pallas kernels, backward_reduce(): pl.pallas_call(functools.partial(backward_kernel, n_tensor, back, 1.0 / m...  121 us
    pallas_call x1, Pallas kernels, finish_reduce(): pl.pallas_call(functools.partial(finish_kernel, n_tensor), out_shape=[sha...  77.8 us
    select_n x1, other arithmetic, per_device(): master_new = jnp.where(my_occupied, master_new * factor[..., None], 0.0)  8.64 us

profile of v6, /device:TPU:9, one launch (start us, length us, event | category | flops | bytes accessed | tf_op | source)
XLA Modules:
  0.0 409.8 jit_solution(15855003379395984967)
XLA Ops:
  0.7 0.9 select_reduce_fusion.3
  1.5 0.1 select_reduce_fusion.2
  1.6 0.6 subtract_add_fusion
  2.2 0.8 fusion.20
  3.1 1.6 convert_reduce_fusion
  4.7 1.6 fusion.2
  6.3 1.4 fusion.5.a_ref
  7.8 0.2 convert_reduce_fusion.1
  7.9 0.5 multiply_add_fusion.slot_ref
  8.5 0.6 slice_bitcast_fusion.shared_ref
  9.1 1.1 convert_element_type.42
  10.2 0.6 slice_reduce_fusion
  10.8 181.5 %forward_spread.1 = (bf16[4,4,4,2,32,1024]{5,4,3,2,1,0:T(8,128)(2,1)}, bf16[8,4,4,2,32,1024]{5,4,3,2,1,0:T(8,128)(2,1)}, bf16[3,512,1024]{2,1,0:T(8,128)(2,1)}, ...) custom-call(s32[12]{0:T(128)} %multiply_add_fusion.slot_ref, ...), custom_call_target="tpu_custom_call" | custom-call | tf_op jit(solution)/shard_map/forward_spread/pallas_call | solution.py:662
  192.4 120.9 %backward_reduce.1 = (bf16[8,32,1024]{2,1,0:T(8,128)(2,1)}, f32[512,1024]{1,0:T(8,128)}, bf16[2,512,1024]{2,1,0:T(8,128)(2,1)}, bf16[1024,1024]{1,0:T(8,128)(2,1...) custom-call(bf16[8,4,2,2,2,32,1024]{6,5,4,3,2,1,0:T(8,128)(2,1)} %bitcast.59, ...), custom_call_target="tpu_custom_call" | custom-call | tf_op jit(solution)/shard_map/backward_reduce/pallas_call | solution.py:1061
  313.4 0.1 reduce_max.19
  313.5 0.1 reshape.345
  313.6 1.2 concatenate.3.v_ref
  314.8 0.1 select_reduce_fusion.1
  315.0 1.0 copy-done.3
  316.0 77.8 %finish_reduce.1 = (bf16[2,8,32,1024]{3,2,1,0:T(8,128)(2,1)S(1)}, f32[16,1024]{1,0:T(8,128)S(1)}, f32[512,1024]{1,0:T(8,128)S(1)}) custom-call(s32[16]{0:T(128)S(1)} %compare_select_fusion.3.unit_ref, bf16[1,4,2,2,2,32,1024]{6,5,4,3,2,1,0:T(8,128)(2,1)} %bitcast.64, bf16[1,4,2,2,2,32,1024]{6,5,4,3,2,1,0:T(8,128)(2,1)} %bitcast.65, ...), custom_call_target="tpu_custom_call" | custom-call | tf_op jit(solution)/shard_map/finish_reduce/pallas_call | solution.py:1194
  393.8 1.0 copy-done.2
  394.8 0.7 bitcast_subtract_fusion
  395.5 0.6 broadcast_in_dim.103
  396.1 0.7 multiply_subtract_fusion
  396.8 0.7 copy.27
  397.4 0.6 divide_sqrt_fusion
  398.1 0.1 compare_select_fusion
  398.2 0.1 select_reduce_fusion
  398.3 0.1 fusion.11
  398.5 8.6 %multiply_select_fusion = (f32[1,2,256,1024]{3,2,1,0:T(8,128)}, f32[1,2,256,1024]{3,2,1,0:T(8,128)}, f32[1,2,256,1024]{3,2,1,0:T(8,128)}, f32[1,2,256,1024]{3,2,1,0:T(8,128)}) fusion(f32[1,2,256,1024]{3,2,1,0:T(8,128)} %param.13, bf16[1,2,256,1024]{3,2,1,0:T(8,128)(2,1)} %bitcast.58, f32[1,2,256,1024]{3,2,1,0:T(8,128)} %param.14, ...), kind=kLoop, calls=%fused_computation.14 | loop fusion | flops 11010048 | bytes 15730690 | tf_op jit(solution)/shard_map/jit(_where)/select_n | solution.py:1422
  407.2 1.3 copy.31
  408.5 1.3 copy.32
  (43 shorter events, 0.5 us)
Async XLA Ops:
  0.6 5.7 %copy-start = (bf16[512,1024]{1,0:T(8,128)(2,1)S(1)}, bf16[512,1024]{1,0:T(8,128)(2,1)}, u32[]{:S(2)}) copy-start(bf16[512,1024]{1,0:T(8,128)(2,1)} %x_ref.3) | copy-start | bytes 3145732
  3.0 4.7 %copy-start.13 = (s32[12]{0:T(128)S(1)}, s32[12]{0:T(128)}, u32[]{:S(2)}) copy-start(s32[12]{0:T(128)} %param.12) | copy-start | bytes 148
  3.1 5.4 %copy-start.7 = (f32[3,6,1024]{2,1,0:T(8,128)S(1)}, f32[3,6,1024]{2,1,0:T(8,128)}, u32[]{:S(2)}) copy-start(f32[3,6,1024]{2,1,0:T(8,128)} %param.16) | copy-start | bytes 221188
  3.1 6.0 %copy-start.5 = (f32[1,2,256,1024]{3,2,1,0:T(8,128)S(1)}, f32[1,2,256,1024]{3,2,1,0:T(8,128)}, u32[]{:S(2)}) copy-start(f32[1,2,256,1024]{3,2,1,0:T(8,128)} %param.13) | copy-start | bytes 6291460
  7.8 2.5 copy-start.8
  192.4 121.0 %copy-start.11 = (f32[2,4,1,512]{3,2,1,0:T(1,128)S(1)}, f32[2,4,1,512]{3,2,1,0:T(1,128)}, u32[]{:S(2)}) copy-start(f32[2,4,1,512]{3,2,1,0:T(1,128)} %get-tuple-element.58) | copy-start | bytes 49156
  192.4 121.1 %copy-start.9 = (f32[8,2,512]{2,1,0:T(2,128)S(1)}, f32[8,2,512]{2,1,0:T(2,128)}, u32[]{:S(2)}) copy-start(f32[8,2,512]{2,1,0:T(2,128)} %get-tuple-element.59) | copy-start | bytes 98308
  192.4 121.3 %copy-start.10 = (f32[4,1024]{1,0:T(4,128)S(1)}, f32[4,1024]{1,0:T(4,128)}, u32[]{:S(2)}) copy-start(f32[4,1024]{1,0:T(4,128)} %get-tuple-element.56) | copy-start | bytes 49156
  192.4 122.4 %copy-start.12 = (s32[12]{0:T(128)S(1)}, s32[12]{0:T(128)}, u32[]{:S(2)}) copy-start(s32[12]{0:T(128)} %multiply_add_fusion.slot_ref) | copy-start | bytes 148
  192.4 122.6 %copy-start.1 = (bf16[512,1024]{1,0:T(8,128)(2,1)S(1)}, bf16[512,1024]{1,0:T(8,128)(2,1)}, u32[]{:S(2)}) copy-start(bf16[512,1024]{1,0:T(8,128)(2,1)} %x_ref.3) | copy-start | bytes 3145732
  192.4 122.5 %copy-start.4 = (f32[6,1024]{1,0:T(8,128)S(1)}, f32[6,1024]{1,0:T(8,128)}, u32[]{:S(2)}) copy-start(f32[6,1024]{1,0:T(8,128)} %slice_bitcast_fusion.shared_ref) | copy-start | bytes 73732
  315.0 1.0 copy-start.3
  393.8 1.0 copy-start.2
  398.5 8.6 %copy-start.6 = (f32[512,1024]{1,0:T(8,128)S(1)}, f32[512,1024]{1,0:T(8,128)}, u32[]{:S(2)}) copy-start(f32[512,1024]{1,0:T(8,128)} %get-tuple-element.130) | copy-start | bytes 6291460

commit v7 on v6

--- a/solution.py
+++ b/solution.py
@@ -306,13 +306,19 @@
     n_keys, n_query = bias_ref.shape
     size, span = q_tiles(n_query, n_keys)
     lanes = pl.ds(pl.multiple_of(i * PAIR, PAIR), PAIR)
-    for j in range(n_query // size):
-        rows, keys = pl.ds(j * size, size), pl.ds(j * size, span)
+    tiles = [(pl.ds(j * size, size), pl.ds(j * size, span)) for j in range(n_query // size)]
+    scores = [
+        [
+            rows_by_rows(jnp.where(head_lanes(h), k_ref[keys, lanes], 0), q_ref[rows, lanes]) + bias_ref[keys, rows]
+            for h in range(2)
+        ]
+        for rows, keys in tiles
+    ]
+    for j, (rows, keys) in enumerate(tiles):
         v_t = v_ref[keys, lanes].T
         outs = []
         for h in range(2):
-            k_h = jnp.where(head_lanes(h), k_ref[keys, lanes], 0)
-            s = rows_by_rows(k_h, q_ref[rows, lanes]) + bias_ref[keys, rows]
+            s = scores[j][h]
             top = jnp.max(s, axis=0, keepdims=True)
             p = jnp.exp(s - top)
             total = jnp.sum(p, axis=0, keepdims=True)
@@ -347,7 +353,7 @@
 
 def forward_kernel(
     n_tensor, back, scale,
-    slot_ref, master_ref, a_ref, x_ref, dy_ref, bias_in_ref, first_ref, shared_ref,
+    slot_ref, master_ref, x_ref, dy_ref, bias_in_ref, first_ref, shared_ref,
     att_ref, ff_ref, wide_ref, q_ref, k_ref, v_ref, o_ref, lse_ref, peak_ref,
     out_ref, grad_ref, do_ref, ff_grad_ref, go_ref, fc_bias_ref, sums_ref,
     pieces, own, seen_ref, bias_rows, biases_ref, fc_rows, hidden_ref, second_ref, acc_ref, tiles_in, stage,
@@ -359,7 +365,7 @@
     by_x, by_y = d + 2 - 4 * x, d + 4 - 8 * y
     sibling = d + 1 - 2 * core
     first, last = t > 0, t < n_tensor - 1
-    rows_here, width = a_ref.shape
+    rows_here, width = x_ref.shape
     n_half = ff_ref.shape[0] // 2
     weights = (att_ref, ff_ref.at[pl.ds(0, n_half)], ff_ref.at[pl.ds(n_half, n_half)])
     starts = (0, 4, 4 + n_half, 4 + 2 * n_half)
@@ -370,8 +376,7 @@
     def tokens_up(r):
         @pl.when(last & (t >= r))
         def _():
-            source = a_ref if r == 0 else wide_ref.at[back - r]
-            send(source, wide_ref.at[back - r - 1], a_send.at[r], a_recv.at[r], (d, t + 1))
+            send(wide_ref.at[back - r], wide_ref.at[back - r - 1], a_send.at[r], a_recv.at[r], (d, t + 1))
 
     def tokens_in(r):
         @pl.when(t > r)
@@ -383,13 +388,17 @@
     for k in range(1, 8):
         to = (d + k) % 8
         send(master_ref.at[:, to], pieces.at[d], swap_send.at[k - 1], swap_recv.at[k - 1], (to, t))
+    part = min(128, rows_here)
+    for i in range(0, rows_here, part):
+        rows = pl.ds(i, part)
+        normed, _, _ = norm_rows(x_ref[rows, :].astype(F32), shared_ref[0:1, :], shared_ref[1:2, :])
+        wide_ref[back, rows, :] = normed.astype(BF)
     tokens_up(0)
     mine = pltpu.make_async_copy(master_ref.at[:, d], pieces.at[d], local_sem.at[0])
     mine.start()
     for k in range(1, n_tensor):
         send(bias_in_ref, biases_ref.at[t], bias_send.at[k - 1], bias_recv.at[k - 1], (d, (t + k) % n_tensor))
     biases_ref[t] = bias_in_ref[...]
-    wide_ref[back] = a_ref[...]
     for r in range(back):
         @pl.when(t < back - r)
         def _(r=r):
@@ -520,7 +529,7 @@
             cols = pl.ds(pl.multiple_of(i * tile, tile), tile)
             w = att_ref[n, pl.ds(i * tile // (width // n_tensor), 1)].reshape(tile, width)
             for r in range(into_ref.shape[0] // rows_here):
-                a = a_ref[...] if own_only else wide_ref[r]
+                a = wide_ref[back if own_only else r]
                 full = (rows_by_rows(a, w) + bias_rows[n : n + 1, cols]).astype(BF)
                 into_ref[r * rows_here : (r + 1) * rows_here, cols] = full * jnp.asarray(factor, BF) if factor else full
         return body
@@ -570,12 +579,14 @@
                 copy.wait()
             w_fc = tiles_in[0].reshape(strip, width)
             second, dy = second_ref[...], dy_ref[...]
-            activ, slope = gelu_parts(rows_by_rows(second, w_fc) + fc_rows[h, at])
-            activ = activ.astype(BF)
+            pre = rows_by_rows(second, w_fc) + fc_rows[h, at]
             for copy in tile_copies(h, at, 1):
                 copy.wait()
             w_proj = tiles_in[1].reshape(strip, width)
-            grad_pre = (rows_by_rows(dy, w_proj) * slope).astype(BF)
+            grad_activ = rows_by_rows(dy, w_proj)
+            activ, slope = gelu_parts(pre)
+            activ = activ.astype(BF)
+            grad_pre = (grad_activ * slope).astype(BF)
             out_ref[...] += plain_dot(activ, w_proj)
             acc_ref[...] += plain_dot(grad_pre, w_fc)
             fc_bias_ref[h, at] = jnp.sum(grad_pre.astype(F32), axis=0, keepdims=True)
@@ -596,7 +607,6 @@
     for copy in grad_copies(0, 0):
         copy.wait()
 
-    part = min(128, rows_here)
     sums_ref[...] = jnp.zeros_like(sums_ref)
 
     def norm_back_rows(i, carry):
@@ -637,17 +647,17 @@
     for r in range(back):
         @pl.when(last & (t >= r))
         def _(r=r):
-            arrived(a_ref, a_send.at[r])
+            arrived(wide_ref.at[back], a_send.at[r])
     for k in range(1, 8):
         arrived(pieces.at[0], swap_send.at[k - 1])
 
 
-def forward_spread(master_low, normed_low, tokens, out_grad, bias_row, first_seen, shared, slot_of_unit, n_tensor, back):
+def forward_spread(master_low, tokens, out_grad, bias_row, first_seen, shared, slot_of_unit, n_tensor, back):
     cap, unit_rows, width = master_low.shape
     n_units = slot_of_unit.shape[0]
     n_ff = n_units - 4
     piece = unit_rows // 8
-    rows = normed_low.shape[0]
+    rows = tokens.shape[0]
     n_keys = (back + 1) * rows
     strip = n_ff // 4 * unit_rows
     bias_row = bias_row.reshape(-1, 128)
@@ -666,7 +676,7 @@
             high, high, low, shape((n_ff, n_tensor, 4, 2, piece, width), BF), shape((width, width), BF),
             shape((2, n_tensor, 1, strip), F32), shape((4, width), F32),
         ],
-        in_specs=[pl.BlockSpec(memory_space=pltpu.SMEM), any_spec] + [vmem] * 6,
+        in_specs=[pl.BlockSpec(memory_space=pltpu.SMEM), any_spec] + [vmem] * 5,
         out_specs=[vmem, any_spec] + [vmem] * 10 + [any_spec] + [vmem] * 3,
         scratch_shapes=[
             pltpu.VMEM((8, cap, piece, width), BF),
@@ -690,7 +700,7 @@
         compiler_params=pltpu.CompilerParams(collective_id=0, has_side_effects=True, vmem_limit_bytes=60 << 20),
         name="forward_spread",
     )(
-        slot_of_unit, master_low.reshape(cap, 8, piece, width), normed_low, tokens, out_grad, bias_row, first_seen, shared
+        slot_of_unit, master_low.reshape(cap, 8, piece, width), tokens, out_grad, bias_row, first_seen, shared
     )
     att, _, wide, *rest = outs
     return att.reshape(-1, width), wide.reshape(-1, width), *rest
@@ -1321,7 +1331,7 @@
             w_att, normed_all, q_scaled, keys_in, values_in, attended, log_norms, peaks,
             layer_out, grad_hidden, grad_attended, grad_ff_w, grad_out_w, grad_fc_b, shared_rows,
         ) = forward_spread(
-            matrix_master[0].astype(BF), normed_low, tokens_in, out_grad, bias_params[0, 0], first_seen, shared,
+            matrix_master[0].astype(BF), tokens_in, out_grad, bias_params[0, 0], first_seen, shared,
             slot_of_unit, n_tensor, back,
         )
     else:

time: 411 us -> 408 us (level)
  no operation moved by 1% of the time
where the time goes in v7:
time: 408 us; the launch traced here: 407 us
  Pallas kernels  380 us (93%)
  other arithmetic  17.5 us (4%)
  local copies, waits for them, and re-layouts  9.06 us (2%)
    pallas_call x1, Pallas kernels, forward_spread(): pl.pallas_call(functools.partial(forward_kernel, n_tensor, back, 1.0 / ma...  181 us
    pallas_call x1, Pallas kernels, backward_reduce(): pl.pallas_call(functools.partial(backward_kernel, n_tensor, back, 1.0 / m...  122 us
    pallas_call x1, Pallas kernels, finish_reduce(): pl.pallas_call(functools.partial(finish_kernel, n_tensor), out_shape=[sha...  77.8 us
    select_n x1, other arithmetic, per_device(): master_new = jnp.where(my_occupied, master_new * factor[..., None], 0.0)  8.64 us

profile of v7, /device:TPU:9, one launch (start us, length us, event | category | flops | bytes accessed | tf_op | source)
XLA Modules:
  0.0 407.4 jit_solution(17503466474417098655)
XLA Ops:
  0.7 0.8 select_reduce_fusion.3
  1.4 0.1 select_reduce_fusion.2
  1.5 0.6 subtract_add_fusion
  2.1 0.9 convert_reduce_fusion
  3.0 1.2 multiply_add_fusion.slot_ref
  4.2 1.4 slice_bitcast_fusion.shared_ref
  5.6 2.7 convert_element_type.36
  8.3 0.6 slice_reduce_fusion
  8.9 180.6 %forward_spread.1 = (bf16[4,4,4,2,32,1024]{5,4,3,2,1,0:T(8,128)(2,1)}, bf16[8,4,4,2,32,1024]{5,4,3,2,1,0:T(8,128)(2,1)}, bf16[3,512,1024]{2,1,0:T(8,128)(2,1)}, ...) custom-call(s32[12]{0:T(128)} %multiply_add_fusion.slot_ref, ...), custom_call_target="tpu_custom_call" | custom-call | tf_op jit(solution)/shard_map/forward_spread/pallas_call | solution.py:672
  189.6 0.0 copy-start.10
  189.6 121.5 %backward_reduce.1 = (bf16[8,32,1024]{2,1,0:T(8,128)(2,1)}, f32[512,1024]{1,0:T(8,128)}, bf16[2,512,1024]{2,1,0:T(8,128)(2,1)}, bf16[1024,1024]{1,0:T(8,128)(2,1...) custom-call(bf16[8,4,2,2,2,32,1024]{6,5,4,3,2,1,0:T(8,128)(2,1)} %bitcast.57, ...), custom_call_target="tpu_custom_call" | custom-call | tf_op jit(solution)/shard_map/backward_reduce/pallas_call | solution.py:1071
  311.2 0.1 reduce_max.19
  311.3 0.1 reshape.329
  311.4 0.9 concatenate.3.v_ref
  312.3 0.1 select_reduce_fusion.1
  312.5 1.0 copy-done.2
  313.5 77.8 %finish_reduce.1 = (bf16[2,8,32,1024]{3,2,1,0:T(8,128)(2,1)S(1)}, f32[16,1024]{1,0:T(8,128)S(1)}, f32[512,1024]{1,0:T(8,128)S(1)}) custom-call(s32[16]{0:T(128)S(1)} %compare_select_fusion.3.unit_ref, bf16[1,4,2,2,2,32,1024]{6,5,4,3,2,1,0:T(8,128)(2,1)} %bitcast.62, bf16[1,4,2,2,2,32,1024]{6,5,4,3,2,1,0:T(8,128)(2,1)} %bitcast.63, ...), custom_call_target="tpu_custom_call" | custom-call | tf_op jit(solution)/shard_map/finish_reduce/pallas_call | solution.py:1204
  391.4 1.0 copy-done.1
  392.4 0.7 bitcast_subtract_fusion
  393.1 0.6 broadcast_in_dim.101
  393.7 0.7 multiply_subtract_fusion
  394.3 0.7 copy.27
  395.0 0.6 divide_sqrt_fusion
  395.6 0.1 dynamic-slice_multiply_fusion
  395.7 0.1 compare_select_fusion
  395.8 0.1 select_reduce_fusion
  395.8 0.1 compare_select_fusion.1
  395.9 0.1 fusion.5
  396.0 0.1 dynamic_slice.17
  396.1 8.6 %multiply_select_fusion = (f32[1,2,256,1024]{3,2,1,0:T(8,128)}, f32[1,2,256,1024]{3,2,1,0:T(8,128)}, f32[1,2,256,1024]{3,2,1,0:T(8,128)}, f32[1,2,256,1024]{3,2,1,0:T(8,128)}) fusion(f32[1,2,256,1024]{3,2,1,0:T(8,128)} %param.13, bf16[1,2,256,1024]{3,2,1,0:T(8,128)(2,1)} %bitcast.56, f32[1,2,256,1024]{3,2,1,0:T(8,128)} %param.14, ...), kind=kLoop, calls=%fused_computation.6 | loop fusion | flops 11010048 | bytes 15730690 | tf_op jit(solution)/shard_map/jit(_where)/select_n | solution.py:1432
  404.7 1.3 copy.31
  406.1 1.3 copy.32
  (31 shorter events, 0.2 us)
Async XLA Ops:
  0.6 7.7 %copy-start.6 = (f32[3,1,1792]{2,1,0:T(1,128)S(1)}, f32[3,1,1792]{2,1,0:T(1,128)}, u32[]{:S(2)}) copy-start(f32[3,1,1792]{2,1,0:T(1,128)} %param.17) | copy-start | bytes 64516
  189.6 121.6 %copy-start.9 = (f32[2,4,1,512]{3,2,1,0:T(1,128)S(1)}, f32[2,4,1,512]{3,2,1,0:T(1,128)}, u32[]{:S(2)}) copy-start(f32[2,4,1,512]{3,2,1,0:T(1,128)} %get-tuple-element.58) | copy-start | bytes 49156
  189.6 121.6 %copy-start.7 = (f32[8,2,512]{2,1,0:T(2,128)S(1)}, f32[8,2,512]{2,1,0:T(2,128)}, u32[]{:S(2)}) copy-start(f32[8,2,512]{2,1,0:T(2,128)} %get-tuple-element.59) | copy-start | bytes 98308
  189.6 121.8 %copy-start.8 = (f32[4,1024]{1,0:T(4,128)S(1)}, f32[4,1024]{1,0:T(4,128)}, u32[]{:S(2)}) copy-start(f32[4,1024]{1,0:T(4,128)} %get-tuple-element.56) | copy-start | bytes 49156
  189.6 122.7 %copy-start.10 = (s32[12]{0:T(128)S(1)}, s32[12]{0:T(128)}, u32[]{:S(2)}) copy-start(s32[12]{0:T(128)} %multiply_add_fusion.slot_ref) | copy-start | bytes 148
  189.6 122.9 %copy-start = (bf16[512,1024]{1,0:T(8,128)(2,1)S(1)}, bf16[512,1024]{1,0:T(8,128)(2,1)}, u32[]{:S(2)}) copy-start(bf16[512,1024]{1,0:T(8,128)(2,1)} %x_ref.3) | copy-start | bytes 3145732
  189.6 122.9 %copy-start.3 = (f32[6,1024]{1,0:T(8,128)S(1)}, f32[6,1024]{1,0:T(8,128)}, u32[]{:S(2)}) copy-start(f32[6,1024]{1,0:T(8,128)} %slice_bitcast_fusion.shared_ref) | copy-start | bytes 73732
  312.5 1.0 copy-start.2
  313.5 80.1 %copy-start.5 = (f32[3,6,1024]{2,1,0:T(8,128)S(1)}, f32[3,6,1024]{2,1,0:T(8,128)}, u32[]{:S(2)}) copy-start(f32[3,6,1024]{2,1,0:T(8,128)} %param.16) | copy-start | bytes 221188
  391.4 1.0 copy-start.1
  396.1 8.6 %copy-start.4 = (f32[512,1024]{1,0:T(8,128)S(1)}, f32[512,1024]{1,0:T(8,128)}, u32[]{:S(2)}) copy-start(f32[512,1024]{1,0:T(8,128)} %get-tuple-element.128) | copy-start | bytes 6291460

commit v8 on v7

--- a/solution.py
+++ b/solution.py
@@ -215,6 +215,33 @@
     fix_two = 1.0 - BETA_TWO**steps_done
     direction = first_new / fix_one / (jnp.sqrt(second_new / fix_two) + EPS_ADAM)
     return (first_new, second_new, param - LEARN_RATE * (direction + decay * param))
+
+
+def owner_kernel(grad_in, master_ref, first_ref, second_ref, factor_ref, keep_ref, grad_ref, m1_ref, m2_ref, new_ref):
+    grad = grad_in[...].astype(F32)
+    first, second, new = adam_step(master_ref[...], grad, first_ref[...], second_ref[...], float(STEP), WEIGHT_DECAY)
+    keep = keep_ref[...] > 0.5
+    for ref, value in ((grad_ref, grad), (m1_ref, first), (m2_ref, second), (new_ref, new * factor_ref[...])):
+        ref[...] = jnp.where(keep, value, 0.0)
+
+
+def owner_step(grads, master, first, second, factor, keep):
+    shape = master.shape
+    rows, width = shape[0] * shape[1], shape[2]
+    part = min(64, rows)
+    wide = pl.BlockSpec((part, width), lambda i: (i, 0))
+    thin = pl.BlockSpec((part, 1), lambda i: (i, 0))
+    flat = lambda v: v.reshape(rows, -1)
+    outs = pl.pallas_call(
+        owner_kernel,
+        grid=(rows // part,),
+        in_specs=[wide] * 4 + [thin] * 2,
+        out_specs=[wide] * 4,
+        out_shape=[jax.ShapeDtypeStruct((rows, width), F32)] * 4,
+        compiler_params=pltpu.CompilerParams(vmem_limit_bytes=60 << 20),
+        name="owner_step",
+    )(*(flat(v) for v in (grads, master, first, second, factor, keep)))
+    return [v.reshape(shape) for v in outs]
 
 
 def take_kernel(picks_ref, from_ref, to_ref):
@@ -1383,7 +1410,6 @@
         my_grads, totals, input_grad = finish_reduce(
             grads, shard, grad_first, away, grad_hidden, tokens_in, shared, vectors, spot_of_slot, n_tensor, slot_cap
         )
-        my_grads = my_grads.astype(F32)
         shared_grad = totals[:6]
         head_all = totals[MAX_ROW, : head_here.shape[0]]
         bias_total = totals[6:MAX_ROW].reshape(-1, n_tensor, unit_rows)
@@ -1413,25 +1439,22 @@
         grad_units = jnp.concatenate(
             [by_stack(g) for g in (grad_q_w, grad_k_w, grad_v_w, grad_out_w, grad_fc_w, grad_proj_w)], axis=1
         ).reshape(units.shape)
-        my_grads = scatter_units(grad_units, unit_of_slot).astype(F32)
+        my_grads = scatter_units(grad_units, unit_of_slot)
     head_peak = lax.dynamic_slice_in_dim(head_all, tensor_index * heads_here, heads_here)
 
     my_units = lax.dynamic_slice_in_dim(unit_of_slot, data_index * slot_cap, slot_cap, 0)
     my_occupied = lax.dynamic_slice_in_dim(occupied, data_index * slot_cap, slot_cap, 0)[:, None, None]
     steps_done = float(STEP)
-    first_new, second_new, master_new = adam_step(
-        matrix_master[0], my_grads, matrix_m1[0], matrix_m2[0], steps_done, WEIGHT_DECAY
-    )
     root_gamma = jnp.sqrt(CLIP_TAU / jnp.maximum(head_peak, CLIP_TAU))
     row_index = my_units[:, None] * unit_rows + jnp.arange(unit_rows, dtype=jnp.int32)[None, :]
     local_head = jnp.where(row_index < head_rows, row_index // HD, (row_index - head_rows) // HD)
     head_match = local_head[..., None] == jnp.arange(heads_here, dtype=jnp.int32)[None, None, :]
     picked_root = jnp.sum(jnp.where(head_match, root_gamma, 0.0), axis=-1)
     factor = jnp.where(row_index < 2 * head_rows, picked_root, 1.0)
-    my_grads = jnp.where(my_occupied, my_grads, 0.0)
-    master_new = jnp.where(my_occupied, master_new * factor[..., None], 0.0)
-    first_new = jnp.where(my_occupied, first_new, 0.0)
-    second_new = jnp.where(my_occupied, second_new, 0.0)
+    kept = jnp.broadcast_to(my_occupied.astype(F32), (slot_cap, unit_rows, 1))
+    my_grads, first_new, second_new, master_new = owner_step(
+        my_grads, matrix_master[0], matrix_m1[0], matrix_m2[0], factor[..., None], kept
+    )
     shared_first, shared_second, shared_new = adam_step(
         shared, shared_grad, shared_params[1], shared_params[2], steps_done, 0.0
     )

time: 408 us -> 413 us (1.012)
  Pallas kernels: 380 us -> 389 us
  other arithmetic: 17.5 us -> 8.95 us
    pallas_call x0 -> x1, Pallas kernels: none -> 9.35 us  [owner_step(): pl.pallas_call(owner_kernel, grid=(rows // part,), in_specs=[wide] * 4 +...]
    select_n x2 -> x0, other arithmetic: 8.71 us -> none  [the longest x1 8.64 us: per_device(): master_new = jnp.where(my_occupied, master_new * factor[..., None], 0.0)]
    unnamed x26 -> x29, local copies, waits for them, and re-layouts: 5.35 us -> 8.98 us
where the time goes in v8:
time: 413 us; the launch traced here: 412 us
  Pallas kernels  389 us (94%)
  local copies, waits for them, and re-layouts  12.6 us (3%)
  other arithmetic  8.95 us (2%)
    pallas_call x1, Pallas kernels, forward_spread(): pl.pallas_call(functools.partial(forward_kernel, n_tensor, back, 1.0 / ma...  181 us
    pallas_call x1, Pallas kernels, backward_reduce(): pl.pallas_call(functools.partial(backward_kernel, n_tensor, back, 1.0 / m...  122 us
    pallas_call x1, Pallas kernels, finish_reduce(): pl.pallas_call(functools.partial(finish_kernel, n_tensor), out_shape=[sha...  77.8 us
    pallas_call x1, Pallas kernels, owner_step(): pl.pallas_call(owner_kernel, grid=(rows // part,), in_specs=[wide] * 4 +...  9.35 us
    unnamed x29, local copies, waits for them, and re-layouts  8.98 us

profile of v8, /device:TPU:9, one launch (start us, length us, event | category | flops | bytes accessed | tf_op | source)
XLA Modules:
  0.0 411.7 jit_solution(1695770342595517987)
XLA Ops:
  0.7 0.8 select_reduce_fusion.3
  1.4 0.1 select_reduce_fusion.2
  1.5 0.6 subtract_add_fusion
  2.1 0.9 convert_reduce_fusion
  3.0 1.2 multiply_add_fusion.slot_ref
  4.2 1.4 slice_bitcast_fusion.shared_ref
  5.6 2.7 convert_element_type.18
  8.3 0.6 slice_reduce_fusion
  8.9 180.6 %forward_spread.1 = (bf16[4,4,4,2,32,1024]{5,4,3,2,1,0:T(8,128)(2,1)}, bf16[8,4,4,2,32,1024]{5,4,3,2,1,0:T(8,128)(2,1)}, bf16[3,512,1024]{2,1,0:T(8,128)(2,1)}, ...) custom-call(s32[12]{0:T(128)} %multiply_add_fusion.slot_ref, ...), custom_call_target="tpu_custom_call" | custom-call | tf_op jit(solution)/shard_map/forward_spread/pallas_call | solution.py:699
  189.6 121.5 %backward_reduce.1 = (bf16[8,32,1024]{2,1,0:T(8,128)(2,1)}, f32[512,1024]{1,0:T(8,128)}, bf16[2,512,1024]{2,1,0:T(8,128)(2,1)}, bf16[1024,1024]{1,0:T(8,128)(2,1...) custom-call(bf16[8,4,2,2,2,32,1024]{6,5,4,3,2,1,0:T(8,128)(2,1)} %bitcast.73, ...), custom_call_target="tpu_custom_call" | custom-call | tf_op jit(solution)/shard_map/backward_reduce/pallas_call | solution.py:1098
  311.2 0.1 reduce_max.19
  311.3 0.1 reshape.319
  311.4 0.9 concatenate.3.v_ref
  312.3 0.1 select_reduce_fusion.1
  312.5 1.0 copy-done.2
  313.5 77.8 %finish_reduce.1 = (bf16[2,8,32,1024]{3,2,1,0:T(8,128)(2,1)S(1)}, f32[16,1024]{1,0:T(8,128)S(1)}, f32[512,1024]{1,0:T(8,128)S(1)}) custom-call(s32[16]{0:T(128)S(1)} %compare_select_fusion.3.unit_ref, bf16[1,4,2,2,2,32,1024]{6,5,4,3,2,1,0:T(8,128)(2,1)} %bitcast.79, bf16[1,4,2,2,2,32,1024]{6,5,4,3,2,1,0:T(8,128)(2,1)} %bitcast.80, ...), custom_call_target="tpu_custom_call" | custom-call | tf_op jit(solution)/shard_map/finish_reduce/pallas_call | solution.py:1231
  391.4 1.0 copy-done.1
  392.4 0.7 bitcast_subtract_fusion
  393.1 0.6 broadcast_in_dim.79
  393.7 0.7 multiply_subtract_fusion
  394.3 0.7 copy.31
  395.0 0.6 divide_sqrt_fusion
  395.7 0.1 compare_select_fusion
  395.8 0.1 select_reduce_fusion
  395.8 0.1 fusion.7
  395.9 0.9 copy.34
  396.8 0.1 fusion.1
  396.9 0.1 dynamic-slice_convert_fusion
  397.1 0.9 copy.36
  397.9 9.4 %owner_step.1 = (f32[512,1024]{1,0:T(8,128)}, f32[512,1024]{1,0:T(8,128)}, f32[512,1024]{1,0:T(8,128)}, f32[512,1024]{1,0:T(8,128)}) custom-call(bf16[512,1024]{1,0:T(8,128)(2,1)} %bitcast.72, f32[512,1024]{1,0:T(8,128)} %bitcast.74, f32[512,1024]{1,0:T(8,128)} %bitcast.82, f32[512,1024]{1,0:T(8,128)} %bitcast.83, f32[512,1]{1,0:T(8,128)} %bitcast.84, ...), custom_call_target="tpu_custom_call" | custom-call | tf_op jit(solution)/shard_map/owner_step/pallas_call | solution.py:235
  407.3 3.2 copy.39
  410.4 1.3 copy.40
  (34 shorter events, 0.4 us)
Async XLA Ops:
  0.6 7.7 %copy-start.5 = (f32[3,1,1792]{2,1,0:T(1,128)S(1)}, f32[3,1,1792]{2,1,0:T(1,128)}, u32[]{:S(2)}) copy-start(f32[3,1,1792]{2,1,0:T(1,128)} %param.17) | copy-start | bytes 64516
  189.6 121.6 %copy-start.8 = (f32[2,4,1,512]{3,2,1,0:T(1,128)S(1)}, f32[2,4,1,512]{3,2,1,0:T(1,128)}, u32[]{:S(2)}) copy-start(f32[2,4,1,512]{3,2,1,0:T(1,128)} %get-tuple-element.62) | copy-start | bytes 49156
  189.6 121.6 %copy-start.6 = (f32[8,2,512]{2,1,0:T(2,128)S(1)}, f32[8,2,512]{2,1,0:T(2,128)}, u32[]{:S(2)}) copy-start(f32[8,2,512]{2,1,0:T(2,128)} %get-tuple-element.63) | copy-start | bytes 98308
  189.6 121.8 %copy-start.7 = (f32[4,1024]{1,0:T(4,128)S(1)}, f32[4,1024]{1,0:T(4,128)}, u32[]{:S(2)}) copy-start(f32[4,1024]{1,0:T(4,128)} %get-tuple-element.60) | copy-start | bytes 49156
  189.6 122.7 %copy-start.9 = (s32[12]{0:T(128)S(1)}, s32[12]{0:T(128)}, u32[]{:S(2)}) copy-start(s32[12]{0:T(128)} %multiply_add_fusion.slot_ref) | copy-start | bytes 148
  189.6 122.9 %copy-start = (bf16[512,1024]{1,0:T(8,128)(2,1)S(1)}, bf16[512,1024]{1,0:T(8,128)(2,1)}, u32[]{:S(2)}) copy-start(bf16[512,1024]{1,0:T(8,128)(2,1)} %x_ref.3) | copy-start | bytes 3145732
  189.6 122.9 %copy-start.3 = (f32[6,1024]{1,0:T(8,128)S(1)}, f32[6,1024]{1,0:T(8,128)}, u32[]{:S(2)}) copy-start(f32[6,1024]{1,0:T(8,128)} %slice_bitcast_fusion.shared_ref) | copy-start | bytes 73732
  312.5 1.0 copy-start.2
  313.5 80.1 %copy-start.4 = (f32[3,6,1024]{2,1,0:T(8,128)S(1)}, f32[3,6,1024]{2,1,0:T(8,128)}, u32[]{:S(2)}) copy-start(f32[3,6,1024]{2,1,0:T(8,128)} %param.16) | copy-start | bytes 221188
  391.4 1.0 copy-start.1
